TPU v7x, 32 devices: a whole 2x2x4 slice. The times are simulated.
32 devices in a mesh: dp: 8 (over z, x), blk: 4 (over y, core).
Axes of the slice: x: 2, y: 2, z: 4, core: 2. Of those that a mesh axis runs over, the one named last changes fastest.
Arguments:
- inputs: bfloat16 [16, 1024, 512], P('dp', 'blk'), may hold values from -16 to 16
- w_query: bfloat16 [512, 512], replicated, may hold values from -0.03125 to 0.03125
- w_key: bfloat16 [512, 512], replicated, may hold values from -0.25 to 0.25
- w_value: bfloat16 [512, 512], replicated, may hold values from -0.25 to 0.25
- w_out: bfloat16 [512, 512], replicated, may hold values from -4 to 4
- w_in: bfloat16 [512, 2048], replicated, may hold values from -0.25 to 0.25
- w_back: bfloat16 [2048, 512], replicated, may hold values from -0.125 to 0.125
- norm1_gain: float32 [512], replicated, may hold values from 0.1 to 1.9
- norm2_gain: float32 [512], replicated, may hold values from 0.1 to 1.9
- final_gain: float32 [512], replicated, may hold values from 0.1 to 1.9
- bias_table: float32 [32, 8], replicated, may hold values from -4 to 4
- bucket_table: int32 [2047], replicated, may hold values from 0 to 31
- prefix_len: int32 [16], P('dp'), may hold values from 5 to 40
- pad_len: int32 [16], P('dp'), may hold values from 0 to 255
- pooled_grad: float32 [16, 512], P('dp'), may hold values from -8 to 8
Outputs:
- pooled: float32 [16, 512], P('dp')
- input_grad: bfloat16 [16, 1024, 512], P('dp', 'blk')
- query_grad: float32 [512, 512], replicated
- key_grad: float32 [512, 512], replicated
- value_grad: float32 [512, 512], replicated
- out_grad: float32 [512, 512], replicated
- in_grad: float32 [512, 2048], replicated
- back_grad: float32 [2048, 512], replicated
- norm1_grad: float32 [512], replicated
- norm2_grad: float32 [512], replicated
- final_grad: float32 [512], replicated
- bias_grad: float32 [32, 8], replicated
Inputs may be any that keep to these rules, and one draw needn't show every extreme that they name: `bucket_table`: entry r is the bucket of the offset r - 1023, key position minus query position.
All inputs are finite; a program needn't handle non-finite values.
Results may differ from a plain program's by a relative error of at most 0.03.
Values may be sent and summed in bfloat16 or wider, within the bound.
No kernel may reach another device: no remote copies, remote signals or barrier semaphores. Data moves between devices by JAX's collectives and lax.ppermute only.
A program may use at most 192 MiB of HBM per device.

v0:
```python
import jax, jax.numpy as jnp
from jax import lax
from jax.experimental import pallas as pl
from jax.experimental.pallas import tpu as pltpu
from jax.sharding import PartitionSpec as P

F32, BF16 = jnp.float32, jnp.bfloat16
NEG = -1000000000.0
NT = (((1,), (1,)), ((), ()))
TN = (((0,), (0,)), ((), ()))
NN = (((1,), (0,)), ((), ()))

def dot(a, b, dims=NN):
    return lax.dot_general(a, b, dims, preferred_element_type=F32)

def skew(row, width, dtype=F32):
    return pltpu.roll(jnp.broadcast_to(row, (128, width)), width - 127, 1, stride=1, stride_axis=0)

def fwd_kernel(info, ql, qr, kl, kr, vl, vr, table, out, expo, inv, bias, scores):
    limit = info[0]
    lane = lax.broadcasted_iota(jnp.int32, (1, 128), 1)
    kref = [(kl, 0), (kl, 256), (kr, 0), (kr, 256)]
    vref = [(vl, 0), (vl, 256), (vr, 0), (vr, 256)]
    starts = [info[1 + b] for b in range(4)]
    parts = [[], []]
    for head in range(2):
        mine = (lane < 64) if head == 0 else (lane >= 64)
        spare = lane == (64 if head == 0 else 0)
        bias[...] = skew(table[head : head + 1, :], bias.shape[1])
        keys, vals = [], []
        for b in range(4):
            ref, at = kref[b]
            place = starts[b] + lax.broadcasted_iota(jnp.int32, (256, 1), 0)
            gate = jnp.where(place < limit, 0.0, NEG)
            edge = jnp.where(spare, gate, 0.0)
            keys.append(jnp.where(mine, ref[at : at + 256, :].astype(F32), edge).astype(BF16))
            ref, at = vref[b]
            vals.append(jnp.where(mine, ref[at : at + 256, :].astype(F32), jnp.where(spare, 1.0, 0.0)).astype(BF16))
        for chunk in range(2):
            q = (ql, qr)[chunk][...].astype(F32)
            q = jnp.where(mine, q, jnp.where(spare, 1.0, 0.0)).astype(BF16)
            begin = starts[2 * chunk]
            peak = None
            for b in range(4):
                s = dot(q, keys[b], NT)
                at = starts[b] - begin + 896
                lo = bias[:, pl.ds(pl.multiple_of(at, 128), 256)]
                hi = bias[:, pl.ds(pl.multiple_of(at - 128, 128), 256)]
                s = s + jnp.concatenate([lo, hi], axis=0)
                scores[:, b * 256 : (b + 1) * 256] = s
                top = jnp.maximum(s[:, :128], s[:, 128:])
                peak = top if peak is None else jnp.maximum(peak, top)
            peak = jnp.max(peak, axis=1, keepdims=True)
            acc = None
            for b in range(4):
                e = jnp.exp(scores[:, b * 256 : (b + 1) * 256] - peak).astype(BF16)
                expo[head, chunk * 256 : (chunk + 1) * 256, b * 256 : (b + 1) * 256] = e
                part = dot(e, vals[b])
                acc = part if acc is None else acc + part
            total = acc[:, 64:65] if head == 0 else acc[:, 0:1]
            parts[chunk].append((acc, 1.0 / total))
    for chunk in range(2):
        (a0, i0), (a1, i1) = parts[chunk]
        scale = jnp.where(lane < 64, i0, i1)
        rows = slice(chunk * 256, (chunk + 1) * 256)
        out[rows, :] = (jnp.where(lane < 64, a0, a1) * scale).astype(BF16)
        inv[rows, :] = scale

def attention(info, ql, qr, kl, kr, vl, vr, table):
    d = ql.shape[1]
    pairs = d // 128
    col = lambda rows: pl.BlockSpec((rows, 128), lambda g: (0, g))
    return pl.pallas_call(
        fwd_kernel,
        grid=(pairs,),
        in_specs=[pl.BlockSpec(memory_space=pltpu.SMEM), col(256), col(256), col(512), col(512), col(512), col(512),
                  pl.BlockSpec((None, 2, 2048), lambda g: (g, 0, 0))],
        out_specs=[col(512), pl.BlockSpec((2, 512, 1024), lambda g: (g, 0, 0)), col(512)],
        out_shape=[jax.ShapeDtypeStruct((512, d), BF16), jax.ShapeDtypeStruct((2 * pairs, 512, 1024), BF16),
                   jax.ShapeDtypeStruct((512, d), F32)],
        scratch_shapes=[pltpu.VMEM((128, 2048), F32), pltpu.VMEM((256, 1024), F32)],
        name="attn_fwd",
    )(info, ql, qr, kl, kr, vl, vr, table)

def bwd_kernel(info, ql, qr, kl, kr, vl, vr, gout, out, inv, expo, dq, dk, dv, diag, acc, tmp):
    lane = lax.broadcasted_iota(jnp.int32, (1, 128), 1)
    kref = [(kl, 0), (kl, 256), (kr, 0), (kr, 256)]
    vref = [(vl, 0), (vl, 256), (vr, 0), (vr, 256)]
    starts = [info[1 + b] for b in range(4)]
    scaled = gout[...].astype(F32) * inv[...]
    prod = scaled * out[...].astype(F32)
    gkeys = [None] * 4
    gvals = [None] * 4
    dqs = [None, None]
    for head in range(2):
        mine = (lane < 64) if head == 0 else (lane >= 64)
        base = 64 if head == 0 else 0
        delta = jnp.sum(jnp.where(mine, prod, 0.0), axis=1, keepdims=True)
        high = delta.astype(BF16).astype(F32)
        gaug = jnp.where(mine, scaled, jnp.where(lane == base, high, jnp.where(lane == base + 1, delta - high, 0.0))).astype(BF16)
        gplain = jnp.where(mine, scaled, 0.0).astype(BF16)
        minus = jnp.where((lane == base) | (lane == base + 1), -1.0, 0.0)
        acc[...] = jnp.zeros_like(acc)
        vals, keys = [], []
        for b in range(4):
            ref, at = vref[b]
            vals.append(jnp.where(mine, ref[at : at + 256, :].astype(F32), minus).astype(BF16))
            ref, at = kref[b]
            keys.append(jnp.where(mine, ref[at : at + 256, :].astype(F32), 0.0).astype(BF16))
        for chunk in range(2):
            rows = slice(chunk * 256, (chunk + 1) * 256)
            q = jnp.where(mine, (ql, qr)[chunk][...].astype(F32), 0.0).astype(BF16)
            begin = starts[2 * chunk]
            for b in range(4):
                e = expo[head, rows, b * 256 : (b + 1) * 256]
                ds = dot(gaug[rows], vals[b], NT) * e.astype(F32)
                at = starts[b] - begin + 896
                lo = pl.ds(pl.multiple_of(at, 128), 256)
                hi = pl.ds(pl.multiple_of(at - 128, 128), 256)
                acc[:, lo] += ds[:128]
                acc[:, hi] += ds[128:]
                ds = ds.astype(BF16)
                part = dot(ds, keys[b])
                dqs[chunk] = part if dqs[chunk] is None else dqs[chunk] + part
                part = dot(q, ds, TN)
                gkeys[b] = part if gkeys[b] is None else gkeys[b] + part
                part = dot(gplain[rows], e, TN)
                gvals[b] = part if gvals[b] is None else gvals[b] + part
        rest = acc[...]
        n = 64
        while n >= 8:
            rest = rest[:n] + pltpu.roll(rest[n:], 2048 - n, 1)
            n //= 2
        line = rest[7:8]
        for r in range(6, -1, -1):
            line = rest[r : r + 1] + pltpu.roll(line, 2047, 1)
        diag[head : head + 1, :] = pltpu.roll(line, 127, 1)
    for chunk in range(2):
        dq[chunk * 256 : (chunk + 1) * 256, :] = dqs[chunk].astype(BF16)
    for b in range(4):
        dk[b * 256 : (b + 1) * 256, :] = gkeys[b].T.astype(BF16)
        dv[b * 256 : (b + 1) * 256, :] = gvals[b].T.astype(BF16)

def attention_grads(info, ql, qr, kl, kr, vl, vr, gout, out, inv, expo):
    d = ql.shape[1]
    pairs = d // 128
    col = lambda rows: pl.BlockSpec((rows, 128), lambda g: (0, g))
    return pl.pallas_call(
        bwd_kernel,
        grid=(pairs,),
        in_specs=[pl.BlockSpec(memory_space=pltpu.SMEM), col(256), col(256), col(512), col(512), col(512), col(512),
                  col(512), col(512), col(512), pl.BlockSpec((2, 512, 1024), lambda g: (g, 0, 0))],
        out_specs=[col(512), col(1024), col(1024), pl.BlockSpec((None, 2, 2048), lambda g: (g, 0, 0))],
        out_shape=[jax.ShapeDtypeStruct((512, d), BF16), jax.ShapeDtypeStruct((1024, d), BF16),
                   jax.ShapeDtypeStruct((1024, d), BF16), jax.ShapeDtypeStruct((pairs, 2, 2048), F32)],
        scratch_shapes=[pltpu.VMEM((128, 2048), F32), pltpu.VMEM((8, 128), F32)],
        name="attn_bwd",
    )(info, ql, qr, kl, kr, vl, vr, gout, out, inv, expo)

BUCKETS = 32
EPS = 1e-06

def rms_scale(values):
    return lax.rsqrt(jnp.mean(values * values, axis=-1, keepdims=True) + EPS)

def norm_back(grad_out, values, scale, gain):
    weighted = grad_out * gain
    inner = jnp.mean(weighted * values, axis=-1, keepdims=True)
    grad_in = scale * weighted - scale * scale * scale * values * inner
    return grad_in, jnp.sum(grad_out * values * scale, axis=0)

def exchange(value, axis, bit):
    size = lax.axis_size(axis)
    return lax.ppermute(value, axis, [(i, i ^ bit) for i in range(size)])

def side(axis, bit):
    return (lax.axis_index(axis) // bit) % 2

def reduce_halves(value, steps):
    for axis, bit in steps:
        half = value.shape[0] // 2
        mine = side(axis, bit)
        keep = lax.dynamic_slice_in_dim(value, mine * half, half, 0)
        send = lax.dynamic_slice_in_dim(value, (1 - mine) * half, half, 0)
        value = (keep.astype(F32) + exchange(send, axis, bit).astype(F32)).astype(BF16)
    return value

def gather_halves(value, steps):
    for axis, bit in reversed(steps):
        other = exchange(value, axis, bit)
        mine = side(axis, bit)
        value = jnp.where(mine == 0, jnp.concatenate([value, other]), jnp.concatenate([other, value]))
    return value

def plans():
    bits = [("dp", 1 << b) for b in range(lax.axis_size("dp").bit_length() - 1)]
    near, rest = bits[0], bits[1:]
    y = ("blk", 2)
    return [[y, near] + rest, [near] + rest + [y], rest + [y, near]]

def reduce_all(value, cuts):
    core = [("blk", 1)]
    value = reduce_halves(value, core)
    at, pieces = 0, []
    for rows, steps in zip(cuts, plans()):
        if rows:
            piece = lax.slice_in_dim(value, at, at + rows, axis=0)
            pieces.append(gather_halves(reduce_halves(piece, steps), steps))
        at += rows
    return gather_halves(jnp.concatenate(pieces), core)

def reduce_small(value):
    for axis in ("blk", "dp"):
        for b in range(lax.axis_size(axis).bit_length() - 1):
            value = value + exchange(value, axis, 1 << b)
    return value

def mm(a, b, dims=NN):
    return lax.dot_general(a, b, dims, preferred_element_type=F32)

def local(inputs, w_query, w_key, w_value, w_out, w_in, w_back, norm1_gain, norm2_gain, final_gain, bias_table, bucket_table, prefix_len, pad_len, pooled_grad):
    rows, width = inputs.shape[1:]
    place = lax.axis_index("blk")
    length = rows * lax.axis_size("blk")
    doc, core = place // 2, place % 2
    block = [doc * 2 + core, doc * 2 + 1 - core, (1 - doc) * 2 + core, (1 - doc) * 2 + 1 - core]
    near = lax.dynamic_index_in_dim(inputs, doc, 0, keepdims=False)
    far = exchange(lax.dynamic_index_in_dim(inputs, 1 - doc, 0, keepdims=False), "blk", 2)
    near_other = exchange(near, "blk", 1)
    far_other = exchange(far, "blk", 1)
    limit = length - lax.dynamic_index_in_dim(pad_len, doc, 0, keepdims=False)
    prefix = lax.dynamic_index_in_dim(prefix_len, doc, 0, keepdims=False)
    count = (limit - prefix).astype(F32)
    cotangent = lax.dynamic_index_in_dim(pooled_grad, doc, 0, keepdims=True)
    info = jnp.stack([limit] + [b * rows for b in block]).astype(jnp.int32)
    picker = (jnp.arange(BUCKETS, dtype=jnp.int32)[:, None] == bucket_table[None, :]).astype(F32)
    picker = jnp.pad(picker, ((0, 0), (0, 1)))
    table = lax.dot_general(bias_table, picker, TN, precision=lax.Precision.HIGHEST)
    table = table.reshape(-1, 2, picker.shape[1])

    def front(raw, own):
        tokens = raw.astype(F32)
        scale = rms_scale(tokens)
        hidden = (tokens * scale * norm1_gain).astype(BF16)
        return hidden, mm(hidden[:own], w_query).astype(BF16), mm(hidden, w_key).astype(BF16), mm(hidden, w_value).astype(BF16)

    hid_l, q_l, k_l, v_l = front(jnp.concatenate([near, near_other]), rows)
    hid_r, q_r, k_r, v_r = front(jnp.concatenate([far, far_other]), rows)
    attended, expo, inverse = attention(info, q_l, q_r, k_l, k_r, v_l, v_r, table)

    raw = jnp.concatenate([near, far])
    tokens = raw.astype(F32)
    mixed = tokens + mm(attended, w_out)
    scale_two = rms_scale(mixed)
    inner = (mixed * scale_two * norm2_gain).astype(BF16)
    lifted = mm(inner, w_in)
    active = jnp.maximum(lifted, 0.0).astype(BF16)
    result = mixed + mm(active, w_back)
    scale_end = rms_scale(result)
    spots = jnp.concatenate([block[0] * rows + jnp.arange(rows), block[2] * rows + jnp.arange(rows)])
    live = ((spots >= prefix) & (spots < limit)).astype(F32)[:, None]
    pool_part = jnp.sum(result * scale_end * final_gain * live, axis=0, keepdims=True)
    pool_mine = (pool_part + exchange(pool_part, "blk", 1)) / count
    pool_other = exchange(pool_mine, "blk", 2)
    pooled = jnp.where(doc == 0, jnp.concatenate([pool_mine, pool_other]), jnp.concatenate([pool_other, pool_mine]))

    grad_final = live * (cotangent / count)
    grad_result, grad_end = norm_back(grad_final, result, scale_end, final_gain)
    grad_branch = grad_result.astype(BF16)
    grad_back_w = mm(active, grad_branch, TN)
    grad_lifted = jnp.where(active > 0, mm(grad_branch, w_back, NT).astype(BF16), jnp.zeros_like(active))
    grad_in_t = mm(grad_lifted, inner, TN)
    big = reduce_all(jnp.concatenate([grad_back_w.astype(BF16), grad_in_t.astype(BF16)]), (768, 768, 512))
    grad_inner = mm(grad_lifted, w_in, NT)
    grad_through, grad_two = norm_back(grad_inner, mixed, scale_two, norm2_gain)
    grad_mixed = grad_result + grad_through
    grad_att_out = grad_mixed.astype(BF16)
    grad_out_w = mm(attended, grad_att_out, TN)
    grad_attended = mm(grad_att_out, w_out, NT).astype(BF16)
    dq, dk, dv, offsets = attention_grads(info, q_l, q_r, k_l, k_r, v_l, v_r, grad_attended, attended, inverse, expo)
    grad_bias = lax.dot_general(picker, offsets.reshape(-1, picker.shape[1]), NT, precision=lax.Precision.HIGHEST)
    own = jnp.concatenate([hid_l[:rows], hid_r[:rows]])
    everyone = jnp.concatenate([hid_l, hid_r])
    grad_q_w = mm(own, dq, TN)
    grad_k_w = mm(everyone, dk, TN)
    grad_v_w = mm(everyone, dv, TN)
    rest = reduce_all(jnp.concatenate([g.astype(BF16) for g in (grad_out_w, grad_q_w, grad_k_w, grad_v_w)]), (384, 384, 256))
    through_kv = mm(dk, w_key, NT) + mm(dv, w_value, NT)
    through_kv = through_kv.reshape(2, 2, rows, width)
    sent = exchange(through_kv[:, 1].reshape(2 * rows, width).astype(BF16), "blk", 1).astype(F32)
    grad_hidden = mm(dq, w_query, NT) + through_kv[:, 0].reshape(2 * rows, width) + sent
    grad_norm, grad_one = norm_back(grad_hidden, tokens, rms_scale(tokens), norm1_gain)
    input_grad = (grad_mixed + grad_norm).astype(BF16)
    away = exchange(input_grad[rows:], "blk", 2)
    home = input_grad[:rows]
    input_grad = jnp.where(doc == 0, jnp.stack([home, away]), jnp.stack([away, home]))
    small = jnp.concatenate([jnp.stack([grad_one, grad_two, grad_end]), jnp.pad(grad_bias.reshape(1, -1), ((0, 0), (0, width - grad_bias.size)))])
    small = reduce_small(small)
    split = w_in.shape[1]
    grads = [rest[i * width : (i + 1) * width].astype(F32) for i in range(4)]
    return (
        pooled,
        input_grad,
        grads[1],
        grads[2],
        grads[3],
        grads[0],
        big[split:].astype(F32).T,
        big[:split].astype(F32),
        small[0],
        small[1],
        small[2],
        small[3, : grad_bias.size].reshape(grad_bias.shape),
    )

def solution(mesh):
    data = P("dp", "blk", None)
    placed = (data,) + (P(),) * 11 + (P("dp"), P("dp"), P("dp", None))
    return jax.shard_map(local, mesh=mesh, in_specs=placed, out_specs=(P("dp", None), data) + (P(),) * 10, check_vma=False)
```

profile of v0, /device:TPU:0, one launch (start us, length us, event | category | flops | bytes accessed | tf_op | source)
XLA Modules:
  0.0 307.9 jit_solution(2148301846417021415)
XLA Ops:
  2.1 3.0 collective-permute-start
  5.6 5.8 %collective-permute-done = bf16[256,512]{0,1:T(8,128)(2,1)S(1)} collective-permute-done((bf16[256,512]{0,1:T(8,128)(2,1)S(1)}, bf16[256,512]{0,1:T(8,128)(2,1)S(1)}, u32[]{:S(2)}, u32[]{:S(2)}) %collective-permute-start) | collective-permute-done | bytes 262176 | tf_op jit(solution)/shard_map/ppermute | solution.py:174
  27.0 13.1 %attn_fwd.1 = (bf16[512,512]{1,0:T(8,128)(2,1)}, bf16[8,512,1024]{2,1,0:T(8,128)(2,1)}, f32[512,512]{1,0:T(8,128)}) custom-call(s32[5]{0:T(128)} %stack.43.info, bf16[256,512]{1,0:T(8,128)(2,1)} %convolution_convert_fusion.13.ql, bf16[256,512]{1,0:T(8,128)(2,1)} %convolution_convert_fusion.12.qr, bf16[512,512]{1,0:T(8,128)(2,1)} %convolution_convert_fusion.9.kl, ...), custom_call_target="tpu_custom_call" | custom-call | tf_op jit(solution)/shard_map/attn_fwd/pallas_call | solution.py:73
  45.9 2.9 convolution_convert_fusion.1
  58.6 20.1 %attn_bwd.1 = (bf16[512,512]{1,0:T(8,128)(2,1)}, bf16[1024,512]{1,0:T(8,128)(2,1)}, bf16[1024,512]{1,0:T(8,128)(2,1)}, f32[4,2,2048]{2,1,0:T(2,128)}) custom-call(s32[5]{0:T(128)} %stack.43.info, bf16[256,512]{1,0:T(8,128)(2,1)} %convolution_convert_fusion.13.ql, bf16[256,512]{1,0:T(8,128)(2,1)} %convolution_convert_fusion.12.qr, ...), custom_call_target="tpu_custom_call" | custom-call | tf_op jit(solution)/shard_map/attn_bwd/pallas_call | solution.py:148
  85.0 2.9 convolution_convert_fusion.10
  99.4 4.3 %fusion = bf16[2048,512]{1,0:T(8,128)(2,1)S(1)} fusion(s32[]{:T(128)S(6)} %select_n.599, bf16[2048,512]{1,0:T(8,128)(2,1)S(1)} %copy-done.2, bf16[2048,512]{1,0:T(8,128)(2,1)} %convolution_convert_fusion), kind=kLoop, calls=%fused_computation.13 | loop fusion | flops 4194304 | bytes 6291460 | tf_op jit(solution)/shard_map/concatenate | solution.py:273
  119.7 2.9 collective-permute-start.25
  125.9 3.1 collective-permute-done.26
  133.5 3.1 %collective-permute-done.28 = bf16[16,512]{1,0:T(8,128)(2,1)S(1)} collective-permute-done((bf16[16,512]{1,0:T(8,128)(2,1)S(1)}, bf16[16,512]{1,0:T(8,128)(2,1)S(1)}, u32[]{:S(2)}, u32[]{:S(2)}) %collective-permute-start.28) | collective-permute-done | bytes 16416 | tf_op jit(solution)/shard_map/ppermute | solution.py:174
  140.6 3.0 collective-permute-start.30
  146.0 2.9 collective-permute-done.18
  170.7 3.9 %add_convert_fusion = bf16[2048,512]{1,0:T(8,128)(2,1)S(1)} fusion(bf16[2048,512]{1,0:T(8,128)(2,1)S(1)} %collective-permute-done.33, s32[]{:T(128)S(6)} %select_n.598, bf16[2048,512]{1,0:T(8,128)(2,1)S(1)} %copy-done.2, bf16[2048,512]{1,0:T(8,128)(2,1)S(1)} %copy-done.3), kind=kLoop, calls=%fused_computation.6 | loop fusion | flops 7340032 | bytes 8388612 | tf_op jit(solution)/shard_map/convert_element_type | solution.py:185
  176.2 4.9 %collective-permute-done.50 = bf16[256,512]{1,0:T(8,128)(2,1)S(1)} collective-permute-done((bf16[256,512]{1,0:T(8,128)(2,1)S(1)}, bf16[256,512]{1,0:T(8,128)(2,1)S(1)}, u32[]{:S(2)}, u32[]{:S(2)}) %collective-permute-start.50) | collective-permute-done | bytes 262176 | tf_op jit(solution)/shard_map/ppermute | solution.py:174
  183.5 5.2 %collective-permute-done.51 = bf16[128,512]{1,0:T(8,128)(2,1)S(1)} collective-permute-done((bf16[128,512]{1,0:T(8,128)(2,1)S(1)}, bf16[128,512]{1,0:T(8,128)(2,1)S(1)}, u32[]{:S(2)}, u32[]{:S(2)}) %collective-permute-start.51) | collective-permute-done | bytes 131104 | tf_op jit(solution)/shard_map/ppermute | solution.py:174
  192.0 5.4 %collective-permute-done.52 = bf16[64,512]{1,0:T(8,128)(2,1)S(1)} collective-permute-done((bf16[64,512]{1,0:T(8,128)(2,1)S(1)}, bf16[64,512]{1,0:T(8,128)(2,1)S(1)}, u32[]{:S(2)}, u32[]{:S(2)}) %collective-permute-start.52) | collective-permute-done | bytes 65568 | tf_op jit(solution)/shard_map/ppermute | solution.py:174
  202.8 2.9 collective-permute-done.54
  206.7 4.0 %collective-permute-done.55 = bf16[64,512]{1,0:T(8,128)(2,1)S(1)} collective-permute-done((bf16[64,512]{1,0:T(8,128)(2,1)S(1)}, bf16[64,512]{1,0:T(8,128)(2,1)S(1)}, u32[]{:S(2)}, u32[]{:S(2)}) %collective-permute-start.55) | collective-permute-done | bytes 65568 | tf_op jit(solution)/shard_map/ppermute | solution.py:174
  218.4 5.0 %collective-permute-done.44 = bf16[96,512]{1,0:T(8,128)(2,1)S(1)} collective-permute-done((bf16[96,512]{1,0:T(8,128)(2,1)S(1)}, bf16[96,512]{1,0:T(8,128)(2,1)S(1)}, u32[]{:S(2)}, u32[]{:S(2)}) %collective-permute-start.44) | collective-permute-done | bytes 98336 | tf_op jit(solution)/shard_map/ppermute | solution.py:174
  223.4 5.6 %collective-permute-done.36 = bf16[96,512]{1,0:T(8,128)(2,1)S(1)} collective-permute-done((bf16[96,512]{1,0:T(8,128)(2,1)S(1)}, bf16[96,512]{1,0:T(8,128)(2,1)S(1)}, u32[]{:S(2)}, u32[]{:S(2)}) %collective-permute-start.36) | collective-permute-done | bytes 98336 | tf_op jit(solution)/shard_map/ppermute | solution.py:174
  229.7 3.4 %collective-permute-done.45 = bf16[48,512]{1,0:T(8,128)(2,1)S(1)} collective-permute-done((bf16[48,512]{1,0:T(8,128)(2,1)S(1)}, bf16[48,512]{1,0:T(8,128)(2,1)S(1)}, u32[]{:S(2)}, u32[]{:S(2)}) %collective-permute-start.45) | collective-permute-done | bytes 49184 | tf_op jit(solution)/shard_map/ppermute | solution.py:174
  233.1 5.0 %collective-permute-done.37 = bf16[48,512]{1,0:T(8,128)(2,1)S(1)} collective-permute-done((bf16[48,512]{1,0:T(8,128)(2,1)S(1)}, bf16[48,512]{1,0:T(8,128)(2,1)S(1)}, u32[]{:S(2)}, u32[]{:S(2)}) %collective-permute-start.37) | collective-permute-done | bytes 49184 | tf_op jit(solution)/shard_map/ppermute | solution.py:174
  238.7 4.0 %collective-permute-done.46 = bf16[48,512]{1,0:T(8,128)(2,1)S(1)} collective-permute-done((bf16[48,512]{1,0:T(8,128)(2,1)S(1)}, bf16[48,512]{1,0:T(8,128)(2,1)S(1)}, u32[]{:S(2)}, u32[]{:S(2)}) %collective-permute-start.46) | collective-permute-done | bytes 49184 | tf_op jit(solution)/shard_map/ppermute | solution.py:174
  242.8 5.0 %collective-permute-done.38 = bf16[48,512]{1,0:T(8,128)(2,1)S(1)} collective-permute-done((bf16[48,512]{1,0:T(8,128)(2,1)S(1)}, bf16[48,512]{1,0:T(8,128)(2,1)S(1)}, u32[]{:S(2)}, u32[]{:S(2)}) %collective-permute-start.38) | collective-permute-done | bytes 49184 | tf_op jit(solution)/shard_map/ppermute | solution.py:174
  247.8 5.5 %collective-permute-done.47 = bf16[96,512]{1,0:T(8,128)(2,1)S(1)} collective-permute-done((bf16[96,512]{1,0:T(8,128)(2,1)S(1)}, bf16[96,512]{1,0:T(8,128)(2,1)S(1)}, u32[]{:S(2)}, u32[]{:S(2)}) %collective-permute-start.47) | collective-permute-done | bytes 98336 | tf_op jit(solution)/shard_map/ppermute | solution.py:174
  253.3 4.6 %collective-permute-done.39 = bf16[96,512]{1,0:T(8,128)(2,1)S(1)} collective-permute-done((bf16[96,512]{1,0:T(8,128)(2,1)S(1)}, bf16[96,512]{1,0:T(8,128)(2,1)S(1)}, u32[]{:S(2)}, u32[]{:S(2)}) %collective-permute-start.39) | collective-permute-done | bytes 98336 | tf_op jit(solution)/shard_map/ppermute | solution.py:174
  258.6 5.0 %collective-permute-done.48 = bf16[192,512]{1,0:T(8,128)(2,1)S(1)} collective-permute-done((bf16[192,512]{1,0:T(8,128)(2,1)S(1)}, bf16[192,512]{1,0:T(8,128)(2,1)S(1)}, u32[]{:S(2)}, u32[]{:S(2)}) %collective-permute-start.48) | collective-permute-done | bytes 196640 | tf_op jit(solution)/shard_map/ppermute | solution.py:174
  266.8 3.2 %collective-permute-done.57 = bf16[256,512]{1,0:T(8,128)(2,1)S(1)} collective-permute-done((bf16[256,512]{1,0:T(8,128)(2,1)S(1)}, bf16[256,512]{1,0:T(8,128)(2,1)S(1)}, u32[]{:S(2)}, u32[]{:S(2)}) %collective-permute-start.57) | collective-permute-done | bytes 262176 | tf_op jit(solution)/shard_map/ppermute | solution.py:174
  285.4 3.5 %collective-permute-done.6 = bf16[256,512]{0,1:T(8,128)(2,1)S(1)} collective-permute-done((bf16[256,512]{0,1:T(8,128)(2,1)S(1)}, bf16[256,512]{0,1:T(8,128)(2,1)S(1)}, u32[]{:S(2)}, u32[]{:S(2)}) %collective-permute-start.6) | collective-permute-done | bytes 262176 | tf_op jit(solution)/shard_map/ppermute | solution.py:174
  294.1 3.4 %maximum_select_fusion = bf16[4096,512]{1,0:T(8,128)(2,1)S(1)} fusion(bf16[2048,512]{1,0:T(8,128)(2,1)} %collective-permute-done.58, bf16[512,512]{1,0:T(8,128)(2,1)S(1)} %maximum_select_fusion.5, bf16[768,512]{1,0:T(8,128)(2,1)S(1)} %maximum_select_fusion.3, bf16[768,512]{1,0:T(8,128)(2,1)S(1)} %copy-done.8, pred[]{:T(512)S(6)} %eq.111), kind=kLoop, calls=%fused_computation.4 | loop fusion | flops 35651584 | bytes 8388609 | tf_op jit(solution)/shard_map/jit(_where)/select_n | solution.py:192
  297.5 4.6 %slice_convert_fusion = (f32[2048,512]{1,0:T(8,128)}, f32[512,2048]{0,1:T(8,128)}) fusion(bf16[4096,512]{1,0:T(8,128)(2,1)S(1)} %maximum_select_fusion), kind=kLoop, calls=%fused_computation.15 | loop fusion | flops 2097152 | bytes 12582912 | tf_op jit(solution)/shard_map/convert_element_type | solution.py:309
  302.1 5.5 %copy.47 = f32[512,2048]{1,0:T(8,128)} copy(f32[512,2048]{0,1:T(8,128)} %get-tuple-element.61) | data formatting | bytes 8388608
  (345 shorter events, 147.5 us)
Async XLA Ops:
  2.1 9.3 %collective-permute-start = (bf16[256,512]{0,1:T(8,128)(2,1)S(1)}, bf16[256,512]{0,1:T(8,128)(2,1)S(1)}, u32[]{:S(2)}, u32[]{:S(2)}) collective-permute-start(bf16[256,512]{0,1:T(8,128)(2,1)S(1)} %bitcast.78), channel_id=1, source_target_pairs={{0,2},{1,3},{2,0},{3,1},{4,6},{5,7},{6,4},{7,5},{8,10},{9,11},{10,... | collective-permute-start | bytes 786440 | tf_op jit(solution)/shard_map/ppermute | solution.py:174
  5.3 11.0 %collective-permute-start.1 = (bf16[256,512]{0,1:T(8,128)(2,1)S(1)}, bf16[256,512]{0,1:T(8,128)(2,1)S(1)}, u32[]{:S(2)}, u32[]{:S(2)}) collective-permute-start(bf16[256,512]{0,1:T(8,128)(2,1)S(1)} %bitcast.69), channel_id=1, source_target_pairs={{0,1},{1,0},{2,3},{3,2},{4,5},{5,4},{6,7},{7,6},{8,9},{9,8},{10,11... | collective-permute-start | bytes 786440 | tf_op jit(solution)/shard_map/ppermute | solution.py:174
  83.6 22.8 %collective-permute-start.3 = (f32[1,512]{1,0:T(1,128)}, f32[1,512]{1,0:T(1,128)}, u32[]{:S(2)}, u32[]{:S(2)}) collective-permute-start(f32[1,512]{1,0:T(1,128)} %bitcast.9), channel_id=1, source_target_pairs={{0,1},{1,0},{2,3},{3,2},{4,5},{5,4},{6,7},{7,6},{8,9},{9,8},{10,11... | collective-permute-start | bytes 6152 | tf_op jit(solution)/shard_map/ppermute | solution.py:174
  91.4 12.4 %collective-permute-start.5 = (bf16[512,512]{0,1:T(8,128)(2,1)}, bf16[512,512]{0,1:T(8,128)(2,1)}, u32[]{:S(2)}, u32[]{:S(2)}) collective-permute-start(bf16[512,512]{0,1:T(8,128)(2,1)} %bitcast.30), channel_id=1, source_target_pairs={{0,1},{1,0},{2,3},{3,2},{4,5},{5,4},{6,7},{7,6},{8,9},{9,8},{10,11... | collective-permute-start | bytes 1572872 | tf_op jit(solution)/shard_map/ppermute | solution.py:174
  97.9 16.3 %collective-permute-start.7 = (bf16[1024,512]{1,0:T(8,128)(2,1)}, bf16[1024,512]{1,0:T(8,128)(2,1)S(1)}, u32[]{:S(2)}, u32[]{:S(2)}) collective-permute-start(bf16[1024,512]{1,0:T(8,128)(2,1)} %constant_dynamic-slice_fusion.24), channel_id=1, source_target_pairs={{0,1},{1,0},{2,3},{3,2},{4,5},{5,4},{6,7},{7,6},{8,9},{9,8},{10,11... | collective-permute-start | bytes 3145736 | tf_op jit(solution)/shard_map/ppermute | solution.py:174
  103.7 67.1 %collective-permute-start.33 = (bf16[2048,512]{1,0:T(8,128)(2,1)S(1)}, bf16[2048,512]{1,0:T(8,128)(2,1)S(1)}, u32[]{:S(2)}, u32[]{:S(2)}) collective-permute-start(bf16[2048,512]{1,0:T(8,128)(2,1)S(1)} %fusion), channel_id=1, source_target_pairs={{0,1},{1,0},{2,3},{3,2},{4,5},{5,4},{6,7},{7,6},{8,9},{9,8},{10,11... | collective-permute-start | bytes 6291464 | tf_op jit(solution)/shard_map/ppermute | solution.py:174
  112.6 163.1 %collective-permute-start.61 = (f32[4,512]{1,0:T(4,128)S(1)}, f32[4,512]{1,0:T(4,128)S(1)}, u32[]{:S(2)}, u32[]{:S(2)}) collective-permute-start(f32[4,512]{1,0:T(4,128)S(1)} %fusion.79), channel_id=1, source_target_pairs={{0,4},{4,0},{8,12},{12,8},{16,20},{20,16},{24,28},{28,24},{1,5},{5... | collective-permute-start | bytes 24584 | tf_op jit(solution)/shard_map/ppermute | solution.py:174
  116.3 9.5 %collective-permute-start.16 = (bf16[192,512]{1,0:T(8,128)(2,1)S(1)}, bf16[192,512]{1,0:T(8,128)(2,1)S(1)}, u32[]{:S(2)}, u32[]{:S(2)}) collective-permute-start(bf16[192,512]{1,0:T(8,128)(2,1)S(1)} %constant_dynamic-slice_fusion.19), channel_id=1, source_target_pairs={{0,4},{4,0},{8,12},{12,8},{16,20},{20,16},{24,28},{28,24},{1,5},{5... | collective-permute-start | bytes 589832 | tf_op jit(solution)/shard_map/ppermute | solution.py:174
  122.6 10.8 %collective-permute-start.8 = (bf16[192,512]{1,0:T(8,128)(2,1)S(1)}, bf16[192,512]{1,0:T(8,128)(2,1)S(1)}, u32[]{:S(2)}, u32[]{:S(2)}) collective-permute-start(bf16[192,512]{1,0:T(8,128)(2,1)S(1)} %constant_dynamic-slice_fusion.23), channel_id=1, source_target_pairs={{0,2},{1,3},{2,0},{3,1},{4,6},{5,7},{6,4},{7,5},{8,10},{9,11},{10,... | collective-permute-start | bytes 589832 | tf_op jit(solution)/shard_map/ppermute | solution.py:174
  129.6 14.0 %collective-permute-start.17 = (bf16[96,512]{1,0:T(8,128)(2,1)S(1)}, bf16[96,512]{1,0:T(8,128)(2,1)S(1)}, u32[]{:S(2)}, u32[]{:S(2)}) collective-permute-start(bf16[96,512]{1,0:T(8,128)(2,1)S(1)} %constant_dynamic-slice_fusion.18), channel_id=1, source_target_pairs={{0,8},{4,12},{8,0},{12,4},{16,24},{20,28},{24,16},{28,20},{1,9},{5... | collective-permute-start | bytes 294920 | tf_op jit(solution)/shard_map/ppermute | solution.py:174
  137.5 6.3 %collective-permute-start.9 = (bf16[96,512]{1,0:T(8,128)(2,1)S(1)}, bf16[96,512]{1,0:T(8,128)(2,1)S(1)}, u32[]{:S(2)}, u32[]{:S(2)}) collective-permute-start(bf16[96,512]{1,0:T(8,128)(2,1)S(1)} %constant_dynamic-slice_fusion.22), channel_id=1, source_target_pairs={{0,4},{4,0},{8,12},{12,8},{16,20},{20,16},{24,28},{28,24},{1,5},{5... | collective-permute-start | bytes 294920 | tf_op jit(solution)/shard_map/ppermute | solution.py:174
  140.6 11.1 %collective-permute-start.30 = (bf16[64,512]{1,0:T(8,128)(2,1)S(1)}, bf16[64,512]{1,0:T(8,128)(2,1)S(1)}, u32[]{:S(2)}, u32[]{:S(2)}) collective-permute-start(bf16[64,512]{1,0:T(8,128)(2,1)S(1)} %maximum_select_fusion.22), channel_id=1, source_target_pairs={{0,16},{4,20},{8,24},{12,28},{16,0},{20,4},{24,8},{28,12},{1,17},{... | collective-permute-start | bytes 196616 | tf_op jit(solution)/shard_map/ppermute | solution.py:174
  143.8 5.8 %collective-permute-start.10 = (bf16[48,512]{1,0:T(8,128)(2,1)S(1)}, bf16[48,512]{1,0:T(8,128)(2,1)S(1)}, u32[]{:S(2)}, u32[]{:S(2)}) collective-permute-start(bf16[48,512]{1,0:T(8,128)(2,1)S(1)} %constant_dynamic-slice_fusion.21), channel_id=1, source_target_pairs={{0,8},{4,12},{8,0},{12,4},{16,24},{20,28},{24,16},{28,20},{1,9},{5... | collective-permute-start | bytes 147464 | tf_op jit(solution)/shard_map/ppermute | solution.py:174
  151.7 13.7 %collective-permute-start.31 = (bf16[128,512]{1,0:T(8,128)(2,1)S(1)}, bf16[128,512]{1,0:T(8,128)(2,1)S(1)}, u32[]{:S(2)}, u32[]{:S(2)}) collective-permute-start(bf16[128,512]{1,0:T(8,128)(2,1)S(1)} %maximum_select_fusion.16), channel_id=1, source_target_pairs={{0,8},{4,12},{8,0},{12,4},{16,24},{20,28},{24,16},{28,20},{1,9},{5... | collective-permute-start | bytes 393224 | tf_op jit(solution)/shard_map/ppermute | solution.py:174
  158.0 5.7 %collective-permute-start.21 = (bf16[48,512]{1,0:T(8,128)(2,1)S(1)}, bf16[48,512]{1,0:T(8,128)(2,1)S(1)}, u32[]{:S(2)}, u32[]{:S(2)}) collective-permute-start(bf16[48,512]{1,0:T(8,128)(2,1)S(1)} %maximum_select_fusion.25), channel_id=1, source_target_pairs={{0,16},{4,20},{8,24},{12,28},{16,0},{20,4},{24,8},{28,12},{1,17},{... | collective-permute-start | bytes 147464 | tf_op jit(solution)/shard_map/ppermute | solution.py:174
  168.4 96.1 %collective-permute-start.23 = (bf16[192,512]{1,0:T(8,128)(2,1)S(1)}, bf16[192,512]{1,0:T(8,128)(2,1)S(1)}, u32[]{:S(2)}, u32[]{:S(2)}) collective-permute-start(bf16[192,512]{1,0:T(8,128)(2,1)S(1)} %maximum_select_fusion.13), channel_id=1, source_target_pairs={{0,4},{4,0},{8,12},{12,8},{16,20},{20,16},{24,28},{28,24},{1,5},{5... | collective-permute-start | bytes 589832 | tf_op jit(solution)/shard_map/ppermute | solution.py:174
  169.5 97.2 %collective-permute-start.15 = (bf16[192,512]{1,0:T(8,128)(2,1)S(1)}, bf16[192,512]{1,0:T(8,128)(2,1)S(1)}, u32[]{:S(2)}, u32[]{:S(2)}) collective-permute-start(bf16[192,512]{1,0:T(8,128)(2,1)S(1)} %maximum_select_fusion.12), channel_id=1, source_target_pairs={{0,2},{1,3},{2,0},{3,1},{4,6},{5,7},{6,4},{7,5},{8,10},{9,11},{10,... | collective-permute-start | bytes 589832 | tf_op jit(solution)/shard_map/ppermute | solution.py:174
  174.7 6.4 %collective-permute-start.50 = (bf16[256,512]{1,0:T(8,128)(2,1)S(1)}, bf16[256,512]{1,0:T(8,128)(2,1)S(1)}, u32[]{:S(2)}, u32[]{:S(2)}) collective-permute-start(bf16[256,512]{1,0:T(8,128)(2,1)S(1)} %constant_dynamic-slice_fusion.3), channel_id=1, source_target_pairs={{0,8},{4,12},{8,0},{12,4},{16,24},{20,28},{24,16},{28,20},{1,9},{5... | collective-permute-start | bytes 786440 | tf_op jit(solution)/shard_map/ppermute | solution.py:174
  181.3 7.4 %collective-permute-start.51 = (bf16[128,512]{1,0:T(8,128)(2,1)S(1)}, bf16[128,512]{1,0:T(8,128)(2,1)S(1)}, u32[]{:S(2)}, u32[]{:S(2)}) collective-permute-start(bf16[128,512]{1,0:T(8,128)(2,1)S(1)} %constant_dynamic-slice_fusion.2), channel_id=1, source_target_pairs={{0,16},{4,20},{8,24},{12,28},{16,0},{20,4},{24,8},{28,12},{1,17},{... | collective-permute-start | bytes 393224 | tf_op jit(solution)/shard_map/ppermute | solution.py:174
  182.7 8.2 %collective-permute-start.42 = (bf16[384,512]{1,0:T(8,128)(2,1)S(1)}, bf16[384,512]{1,0:T(8,128)(2,1)S(1)}, u32[]{:S(2)}, u32[]{:S(2)}) collective-permute-start(bf16[384,512]{1,0:T(8,128)(2,1)S(1)} %constant_dynamic-slice_fusion.7), channel_id=1, source_target_pairs={{0,4},{4,0},{8,12},{12,8},{16,20},{20,16},{24,28},{28,24},{1,5},{5... | collective-permute-start | bytes 1179656 | tf_op jit(solution)/shard_map/ppermute | solution.py:174
  188.7 13.0 %collective-permute-start.34 = (bf16[384,512]{1,0:T(8,128)(2,1)S(1)}, bf16[384,512]{1,0:T(8,128)(2,1)S(1)}, u32[]{:S(2)}, u32[]{:S(2)}) collective-permute-start(bf16[384,512]{1,0:T(8,128)(2,1)S(1)} %constant_dynamic-slice_fusion.11), channel_id=1, source_target_pairs={{0,2},{1,3},{2,0},{3,1},{4,6},{5,7},{6,4},{7,5},{8,10},{9,11},{10,... | collective-permute-start | bytes 1179656 | tf_op jit(solution)/shard_map/ppermute | solution.py:174
  190.9 6.5 %collective-permute-start.52 = (bf16[64,512]{1,0:T(8,128)(2,1)S(1)}, bf16[64,512]{1,0:T(8,128)(2,1)S(1)}, u32[]{:S(2)}, u32[]{:S(2)}) collective-permute-start(bf16[64,512]{1,0:T(8,128)(2,1)S(1)} %constant_dynamic-slice_fusion.1), channel_id=1, source_target_pairs={{0,2},{1,3},{2,0},{3,1},{4,6},{5,7},{6,4},{7,5},{8,10},{9,11},{10,... | collective-permute-start | bytes 196616 | tf_op jit(solution)/shard_map/ppermute | solution.py:174
  201.5 9.9 %collective-permute-start.43 = (bf16[192,512]{1,0:T(8,128)(2,1)S(1)}, bf16[192,512]{1,0:T(8,128)(2,1)S(1)}, u32[]{:S(2)}, u32[]{:S(2)}) collective-permute-start(bf16[192,512]{1,0:T(8,128)(2,1)S(1)} %constant_dynamic-slice_fusion.6), channel_id=1, source_target_pairs={{0,8},{4,12},{8,0},{12,4},{16,24},{20,28},{24,16},{28,20},{1,9},{5... | collective-permute-start | bytes 589832 | tf_op jit(solution)/shard_map/ppermute | solution.py:174
  211.4 46.5 %collective-permute-start.56 = (bf16[128,512]{1,0:T(8,128)(2,1)S(1)}, bf16[128,512]{1,0:T(8,128)(2,1)S(1)}, u32[]{:S(2)}, u32[]{:S(2)}) collective-permute-start(bf16[128,512]{1,0:T(8,128)(2,1)S(1)} %maximum_select_fusion.17), channel_id=1, source_target_pairs={{0,16},{4,20},{8,24},{12,28},{16,0},{20,4},{24,8},{28,12},{1,17},{... | collective-permute-start | bytes 393224 | tf_op jit(solution)/shard_map/ppermute | solution.py:174
  216.3 7.1 %collective-permute-start.44 = (bf16[96,512]{1,0:T(8,128)(2,1)S(1)}, bf16[96,512]{1,0:T(8,128)(2,1)S(1)}, u32[]{:S(2)}, u32[]{:S(2)}) collective-permute-start(bf16[96,512]{1,0:T(8,128)(2,1)S(1)} %constant_dynamic-slice_fusion.5), channel_id=1, source_target_pairs={{0,16},{4,20},{8,24},{12,28},{16,0},{20,4},{24,8},{28,12},{1,17},{... | collective-permute-start | bytes 294920 | tf_op jit(solution)/shard_map/ppermute | solution.py:174
  258.0 5.8 %collective-permute-start.40 = (bf16[192,512]{1,0:T(8,128)(2,1)S(1)}, bf16[192,512]{1,0:T(8,128)(2,1)S(1)}, u32[]{:S(2)}, u32[]{:S(2)}) collective-permute-start(bf16[192,512]{1,0:T(8,128)(2,1)S(1)} %maximum_select_fusion.14), channel_id=1, source_target_pairs={{0,4},{4,0},{8,12},{12,8},{16,20},{20,16},{24,28},{28,24},{1,5},{5... | collective-permute-start | bytes 589832 | tf_op jit(solution)/shard_map/ppermute | solution.py:174
  263.6 6.4 %collective-permute-start.57 = (bf16[256,512]{1,0:T(8,128)(2,1)S(1)}, bf16[256,512]{1,0:T(8,128)(2,1)S(1)}, u32[]{:S(2)}, u32[]{:S(2)}) collective-permute-start(bf16[256,512]{1,0:T(8,128)(2,1)S(1)} %maximum_select_fusion.11), channel_id=1, source_target_pairs={{0,8},{4,12},{8,0},{12,4},{16,24},{20,28},{24,16},{28,20},{1,9},{5... | collective-permute-start | bytes 786440 | tf_op jit(solution)/shard_map/ppermute | solution.py:174
  263.7 7.8 %collective-permute-start.49 = (bf16[384,512]{1,0:T(8,128)(2,1)S(1)}, bf16[384,512]{1,0:T(8,128)(2,1)S(1)}, u32[]{:S(2)}, u32[]{:S(2)}) collective-permute-start(bf16[384,512]{1,0:T(8,128)(2,1)S(1)} %maximum_select_fusion.9), channel_id=1, source_target_pairs={{0,4},{4,0},{8,12},{12,8},{16,20},{20,16},{24,28},{28,24},{1,5},{5... | collective-permute-start | bytes 1179656 | tf_op jit(solution)/shard_map/ppermute | solution.py:174
  264.5 7.8 %collective-permute-start.41 = (bf16[384,512]{1,0:T(8,128)(2,1)S(1)}, bf16[384,512]{1,0:T(8,128)(2,1)S(1)}, u32[]{:S(2)}, u32[]{:S(2)}) collective-permute-start(bf16[384,512]{1,0:T(8,128)(2,1)S(1)} %maximum_select_fusion.8), channel_id=1, source_target_pairs={{0,2},{1,3},{2,0},{3,1},{4,6},{5,7},{6,4},{7,5},{8,10},{9,11},{10,... | collective-permute-start | bytes 1179656 | tf_op jit(solution)/shard_map/ppermute | solution.py:174
  274.2 19.8 %collective-permute-start.58 = (bf16[2048,512]{1,0:T(8,128)(2,1)}, bf16[2048,512]{1,0:T(8,128)(2,1)}, u32[]{:S(2)}, u32[]{:S(2)}) collective-permute-start(bf16[2048,512]{1,0:T(8,128)(2,1)} %pad_maximum_fusion.1), channel_id=1, source_target_pairs={{0,1},{1,0},{2,3},{3,2},{4,5},{5,4},{6,7},{7,6},{8,9},{9,8},{10,11... | collective-permute-start | bytes 6291464 | tf_op jit(solution)/shard_map/ppermute | solution.py:174
  275.2 14.7 %collective-permute-start.32 = (bf16[1024,512]{1,0:T(8,128)(2,1)}, bf16[1024,512]{1,0:T(8,128)(2,1)}, u32[]{:S(2)}, u32[]{:S(2)}) collective-permute-start(bf16[1024,512]{1,0:T(8,128)(2,1)} %pad_maximum_fusion.3), channel_id=1, source_target_pairs={{0,1},{1,0},{2,3},{3,2},{4,5},{5,4},{6,7},{7,6},{8,9},{9,8},{10,11... | collective-permute-start | bytes 3145736 | tf_op jit(solution)/shard_map/ppermute | solution.py:174
  282.0 6.9 %collective-permute-start.6 = (bf16[256,512]{0,1:T(8,128)(2,1)S(1)}, bf16[256,512]{0,1:T(8,128)(2,1)S(1)}, u32[]{:S(2)}, u32[]{:S(2)}) collective-permute-start(bf16[256,512]{0,1:T(8,128)(2,1)S(1)} %get-tuple-element.71), channel_id=1, source_target_pairs={{0,2},{1,3},{2,0},{3,1},{4,6},{5,7},{6,4},{7,5},{8,10},{9,11},{10,... | collective-permute-start | bytes 786440 | tf_op jit(solution)/shard_map/ppermute | solution.py:174
  (76 other events, 559.6 us)
where the time goes:
time: 313 us; the launch traced here: 308 us
  waiting for transfers between devices  117 us (37%)
  starting transfers between devices  60.6 us (19%)
  matrix products  35.1 us (11%)
  other arithmetic  33.4 us (11%)
  Pallas kernels  33.2 us (11%)
  local copies, waits for them, and re-layouts  24.4 us (8%)
  between operations  3.73 us (1%)
    ppermute x64, waiting for transfers between devices, exchange(): return lax.ppermute(value, axis, [(i, i ^ bit) for i in range(size)])  117 us
    ppermute x64, starting transfers between devices, exchange(): return lax.ppermute(value, axis, [(i, i ^ bit) for i in range(size)])  60.6 us
    dot_general x21, matrix products, mm(): return lax.dot_general(a, b, dims, preferred_element_type=F32)  34.7 us
    pallas_call x1, Pallas kernels, attention_grads(): pl.pallas_call(bwd_kernel, grid=(pairs,), in_specs=[pl.BlockSpec(memory_s...  20.1 us
    unnamed x95, local copies, waits for them, and re-layouts  15.6 us
    pallas_call x1, Pallas kernels, attention(): pl.pallas_call(fwd_kernel, grid=(pairs,), in_specs=[pl.BlockSpec(memory_s...  13.1 us
    select_n x26, other arithmetic, gather_halves(): jnp.where(mine == 0, jnp.concatenate([value, other]), jnp.concatenate([ot...  7.01 us
  transfers between devices with their start and end apart: 64, of which 39 were waited for; matrix products, arithmetic and copies ran while one was open for 13% of the time, Pallas kernels for 0%

commit v1 on v0

--- a/solution.py
+++ b/solution.py
@@ -82,7 +82,7 @@
         name="attn_fwd",
     )(info, ql, qr, kl, kr, vl, vr, table)
 
-def bwd_kernel(info, ql, qr, kl, kr, vl, vr, gout, out, inv, expo, dq, dk, dv, diag, acc, tmp):
+def bwd_kernel(info, ql, qr, kl, kr, vl, vr, gout, out, inv, expo, dq, dk, dv, diag, acc):
     lane = lax.broadcasted_iota(jnp.int32, (1, 128), 1)
     kref = [(kl, 0), (kl, 256), (kr, 0), (kr, 256)]
     vref = [(vl, 0), (vl, 256), (vr, 0), (vr, 256)]
@@ -141,19 +141,19 @@
         dk[b * 256 : (b + 1) * 256, :] = gkeys[b].T.astype(BF16)
         dv[b * 256 : (b + 1) * 256, :] = gvals[b].T.astype(BF16)
 
-def attention_grads(info, ql, qr, kl, kr, vl, vr, gout, out, inv, expo):
-    d = ql.shape[1]
-    pairs = d // 128
-    col = lambda rows: pl.BlockSpec((rows, 128), lambda g: (0, g))
+def attention_grads(info, ql, qr, kl, kr, vl, vr, gout, out, inv, expo, first, pairs):
+    d = pairs * 128
+    col = lambda rows: pl.BlockSpec((rows, 128), lambda g: (0, first + g))
+    made = lambda rows: pl.BlockSpec((rows, 128), lambda g: (0, g))
     return pl.pallas_call(
         bwd_kernel,
         grid=(pairs,),
         in_specs=[pl.BlockSpec(memory_space=pltpu.SMEM), col(256), col(256), col(512), col(512), col(512), col(512),
-                  col(512), col(512), col(512), pl.BlockSpec((2, 512, 1024), lambda g: (g, 0, 0))],
-        out_specs=[col(512), col(1024), col(1024), pl.BlockSpec((None, 2, 2048), lambda g: (g, 0, 0))],
+                  col(512), col(512), col(512), pl.BlockSpec((2, 512, 1024), lambda g: (first + g, 0, 0))],
+        out_specs=[made(512), made(1024), made(1024), pl.BlockSpec((None, 2, 2048), lambda g: (g, 0, 0))],
         out_shape=[jax.ShapeDtypeStruct((512, d), BF16), jax.ShapeDtypeStruct((1024, d), BF16),
                    jax.ShapeDtypeStruct((1024, d), BF16), jax.ShapeDtypeStruct((pairs, 2, 2048), F32)],
-        scratch_shapes=[pltpu.VMEM((128, 2048), F32), pltpu.VMEM((8, 128), F32)],
+        scratch_shapes=[pltpu.VMEM((128, 2048), F32)],
         name="attn_bwd",
     )(info, ql, qr, kl, kr, vl, vr, gout, out, inv, expo)
 
@@ -169,54 +169,85 @@
     grad_in = scale * weighted - scale * scale * scale * values * inner
     return grad_in, jnp.sum(grad_out * values * scale, axis=0)
 
+def project_kernel(mine, other, wq, wk, wv, gain, hidden, query, keys, values):
+    rows = mine.shape[0]
+    for part, raw in enumerate((mine, other)):
+        tokens = raw[...].astype(F32)
+        hidden[part * rows : (part + 1) * rows, :] = (tokens * rms_scale(tokens) * gain[...]).astype(BF16)
+    h = hidden[...]
+    query[...] = dot(h[:rows], wq[...]).astype(BF16)
+    keys[...] = dot(h, wk[...]).astype(BF16)
+    values[...] = dot(h, wv[...]).astype(BF16)
+
+def project(mine, other, wq, wk, wv, gain):
+    rows, width = mine.shape
+    shape = lambda n: jax.ShapeDtypeStruct((n, width), BF16)
+    return pl.pallas_call(
+        project_kernel,
+        out_shape=[shape(2 * rows), shape(rows), shape(2 * rows), shape(2 * rows)],
+        name="project",
+    )(mine, other, wq, wk, wv, gain)
+
 def exchange(value, axis, bit):
     size = lax.axis_size(axis)
     return lax.ppermute(value, axis, [(i, i ^ bit) for i in range(size)])
 
-def side(axis, bit):
+def side(move):
+    axis, bit = move
     return (lax.axis_index(axis) // bit) % 2
 
-def reduce_halves(value, steps):
-    for axis, bit in steps:
-        half = value.shape[0] // 2
-        mine = side(axis, bit)
-        keep = lax.dynamic_slice_in_dim(value, mine * half, half, 0)
-        send = lax.dynamic_slice_in_dim(value, (1 - mine) * half, half, 0)
-        value = (keep.astype(F32) + exchange(send, axis, bit).astype(F32)).astype(BF16)
-    return value
-
-def gather_halves(value, steps):
-    for axis, bit in reversed(steps):
-        other = exchange(value, axis, bit)
-        mine = side(axis, bit)
-        value = jnp.where(mine == 0, jnp.concatenate([value, other]), jnp.concatenate([other, value]))
-    return value
-
-def plans():
-    bits = [("dp", 1 << b) for b in range(lax.axis_size("dp").bit_length() - 1)]
-    near, rest = bits[0], bits[1:]
-    y = ("blk", 2)
-    return [[y, near] + rest, [near] + rest + [y], rest + [y, near]]
-
-def reduce_all(value, cuts):
-    core = [("blk", 1)]
-    value = reduce_halves(value, core)
-    at, pieces = 0, []
-    for rows, steps in zip(cuts, plans()):
-        if rows:
-            piece = lax.slice_in_dim(value, at, at + rows, axis=0)
-            pieces.append(gather_halves(reduce_halves(piece, steps), steps))
-        at += rows
-    return gather_halves(jnp.concatenate(pieces), core)
-
-def reduce_small(value):
-    for axis in ("blk", "dp"):
-        for b in range(lax.axis_size(axis).bit_length() - 1):
-            value = value + exchange(value, axis, 1 << b)
-    return value
+def halves(value, move):
+    half = value.shape[1] // 2
+    mine = side(move)
+    return lax.dynamic_slice_in_dim(value, mine * half, half, 1), lax.dynamic_slice_in_dim(value, (1 - mine) * half, half, 1)
+
+def add(keep, got):
+    return (keep.astype(F32) + got.astype(F32)).astype(BF16)
+
+def join(value, got, move):
+    return jnp.where(side(move) == 0, jnp.concatenate([value, got], 1), jnp.concatenate([got, value], 1))
+
+def scatter(values, moves, extra=None):
+    split = [halves(v, m) for v, m in zip(values, moves)]
+    sends = [s for _, s in split]
+    width = sends[0].shape[2]
+    if extra is not None:
+        count = sends[0].shape[0] * sends[0].shape[1]
+        sends[0] = jnp.concatenate([sends[0].reshape(count, width), extra])
+    def finish(got):
+        got = list(got)
+        new = None
+        if extra is not None:
+            new = add(extra, got[0][count:])
+            got[0] = got[0][:count].reshape(split[0][1].shape)
+        out = [add(k, g) for (k, _), g in zip(split, got)]
+        return out if extra is None else (out, new)
+    return list(zip(sends, moves)), finish
+
+def gather(values, moves):
+    return list(zip(values, moves)), lambda got: [join(v, g, m) for v, g, m in zip(values, got, moves)]
+
+def phase(parts, token, work=None):
+    sends = [s for moves, _ in parts for s, _ in moves]
+    moves = [m for moves, _ in parts for _, m in moves]
+    token, sends = lax.optimization_barrier((token, sends))
+    got = [exchange(s, *m) for s, m in zip(sends, moves)]
+    result = None
+    if work is not None:
+        result, token = work(token)
+    token, got = lax.optimization_barrier((token, got))
+    outs, at = [], 0
+    for part, finish in parts:
+        outs.append(finish(got[at : at + len(part)]))
+        at += len(part)
+    return outs, token, result
 
 def mm(a, b, dims=NN):
     return lax.dot_general(a, b, dims, preferred_element_type=F32)
+
+def pairwise(value):
+    half = value.shape[1] // 2
+    return [value[:, :half], value[:, half:]]
 
 def local(inputs, w_query, w_key, w_value, w_out, w_in, w_back, norm1_gain, norm2_gain, final_gain, bias_table, bucket_table, prefix_len, pad_len, pooled_grad):
     rows, width = inputs.shape[1:]
@@ -232,24 +263,21 @@
     prefix = lax.dynamic_index_in_dim(prefix_len, doc, 0, keepdims=False)
     count = (limit - prefix).astype(F32)
     cotangent = lax.dynamic_index_in_dim(pooled_grad, doc, 0, keepdims=True)
-    info = jnp.stack([limit] + [b * rows for b in block]).astype(jnp.int32)
+    slot = jnp.arange(8, dtype=jnp.int32)
+    info = jnp.where(slot == 0, limit, 0)
+    for i, b in enumerate(block):
+        info = jnp.where(slot == i + 1, b * rows, info)
     picker = (jnp.arange(BUCKETS, dtype=jnp.int32)[:, None] == bucket_table[None, :]).astype(F32)
     picker = jnp.pad(picker, ((0, 0), (0, 1)))
     table = lax.dot_general(bias_table, picker, TN, precision=lax.Precision.HIGHEST)
     table = table.reshape(-1, 2, picker.shape[1])
 
-    def front(raw, own):
-        tokens = raw.astype(F32)
-        scale = rms_scale(tokens)
-        hidden = (tokens * scale * norm1_gain).astype(BF16)
-        return hidden, mm(hidden[:own], w_query).astype(BF16), mm(hidden, w_key).astype(BF16), mm(hidden, w_value).astype(BF16)
-
-    hid_l, q_l, k_l, v_l = front(jnp.concatenate([near, near_other]), rows)
-    hid_r, q_r, k_r, v_r = front(jnp.concatenate([far, far_other]), rows)
+    gain_row = norm1_gain[None, :]
+    hid_l, q_l, k_l, v_l = project(near, near_other, w_query, w_key, w_value, gain_row)
+    hid_r, q_r, k_r, v_r = project(far, far_other, w_query, w_key, w_value, gain_row)
     attended, expo, inverse = attention(info, q_l, q_r, k_l, k_r, v_l, v_r, table)
 
-    raw = jnp.concatenate([near, far])
-    tokens = raw.astype(F32)
+    tokens = jnp.concatenate([near, far]).astype(F32)
     mixed = tokens + mm(attended, w_out)
     scale_two = rms_scale(mixed)
     inner = (mixed * scale_two * norm2_gain).astype(BF16)
@@ -260,44 +288,113 @@
     spots = jnp.concatenate([block[0] * rows + jnp.arange(rows), block[2] * rows + jnp.arange(rows)])
     live = ((spots >= prefix) & (spots < limit)).astype(F32)[:, None]
     pool_part = jnp.sum(result * scale_end * final_gain * live, axis=0, keepdims=True)
-    pool_mine = (pool_part + exchange(pool_part, "blk", 1)) / count
-    pool_other = exchange(pool_mine, "blk", 2)
-    pooled = jnp.where(doc == 0, jnp.concatenate([pool_mine, pool_other]), jnp.concatenate([pool_other, pool_mine]))
 
     grad_final = live * (cotangent / count)
     grad_result, grad_end = norm_back(grad_final, result, scale_end, final_gain)
     grad_branch = grad_result.astype(BF16)
-    grad_back_w = mm(active, grad_branch, TN)
+    grad_back_w = mm(active, grad_branch, TN).astype(BF16)
     grad_lifted = jnp.where(active > 0, mm(grad_branch, w_back, NT).astype(BF16), jnp.zeros_like(active))
-    grad_in_t = mm(grad_lifted, inner, TN)
-    big = reduce_all(jnp.concatenate([grad_back_w.astype(BF16), grad_in_t.astype(BF16)]), (768, 768, 512))
-    grad_inner = mm(grad_lifted, w_in, NT)
-    grad_through, grad_two = norm_back(grad_inner, mixed, scale_two, norm2_gain)
-    grad_mixed = grad_result + grad_through
-    grad_att_out = grad_mixed.astype(BF16)
-    grad_out_w = mm(attended, grad_att_out, TN)
-    grad_attended = mm(grad_att_out, w_out, NT).astype(BF16)
-    dq, dk, dv, offsets = attention_grads(info, q_l, q_r, k_l, k_r, v_l, v_r, grad_attended, attended, inverse, expo)
-    grad_bias = lax.dot_general(picker, offsets.reshape(-1, picker.shape[1]), NT, precision=lax.Precision.HIGHEST)
+    folds = w_in.shape[1] // width
+    grad_in_w = jnp.concatenate([mm(inner, grad_lifted[:, i * width : (i + 1) * width], TN).astype(BF16) for i in range(folds)])
+    big = jnp.concatenate([grad_back_w, grad_in_w])[None]
+
+    c = ("blk", 1)
+    y = ("blk", 2)
+    bits = [("dp", 1 << b) for b in range(lax.axis_size("dp").bit_length() - 1)]
+    x, line = bits[0], bits[1:]
+
+    def middle(token):
+        grad_inner = mm(grad_lifted, w_in, NT)
+        grad_through, grad_two = norm_back(grad_inner, mixed, scale_two, norm2_gain)
+        grad_mixed = grad_result + grad_through
+        grad_att_out = grad_mixed.astype(BF16)
+        grad_out_w = mm(attended, grad_att_out, TN).astype(BF16)
+        grad_attended = mm(grad_att_out, w_out, NT).astype(BF16)
+        return (grad_mixed, grad_two, grad_out_w, grad_attended), token
+
+    (big,), token, (grad_mixed, grad_two, grad_out_w, grad_attended) = phase([scatter([big], [c])], info, middle)
+    big = big[0]
+
+    def back(first, grad_attended):
+        def work(token):
+            made = attention_grads(token, q_l, q_r, k_l, k_r, v_l, v_r, grad_attended, attended, inverse, expo, first, 2)
+            token, last = lax.optimization_barrier((token, made[3]))
+            return list(made[:3]) + [last], token
+        return work
+
     own = jnp.concatenate([hid_l[:rows], hid_r[:rows]])
     everyone = jnp.concatenate([hid_l, hid_r])
-    grad_q_w = mm(own, dq, TN)
-    grad_k_w = mm(everyone, dk, TN)
-    grad_v_w = mm(everyone, dv, TN)
-    rest = reduce_all(jnp.concatenate([g.astype(BF16) for g in (grad_out_w, grad_q_w, grad_k_w, grad_v_w)]), (384, 384, 256))
-    through_kv = mm(dk, w_key, NT) + mm(dv, w_value, NT)
-    through_kv = through_kv.reshape(2, 2, rows, width)
-    sent = exchange(through_kv[:, 1].reshape(2 * rows, width).astype(BF16), "blk", 1).astype(F32)
-    grad_hidden = mm(dq, w_query, NT) + through_kv[:, 0].reshape(2 * rows, width) + sent
-    grad_norm, grad_one = norm_back(grad_hidden, tokens, rms_scale(tokens), norm1_gain)
-    input_grad = (grad_mixed + grad_norm).astype(BF16)
-    away = exchange(input_grad[rows:], "blk", 2)
+    (big,), token, made_a = phase([scatter(pairwise(big), [y, x])], token, back(0, grad_attended))
+    (big,), token, made_b = phase([scatter(big, [x, y])], token, back(2, grad_attended))
+    big = jnp.concatenate(big)
+    dq, dk, dv = (jnp.concatenate([a, b], axis=1) for a, b in zip(made_a[:3], made_b[:3]))
+    offsets = jnp.concatenate([made_a[3], made_b[3]]).reshape(-1, picker.shape[1])
+
+    def weights(token):
+        token, near_dq = lax.optimization_barrier((token, dq))
+        grad_bias = lax.dot_general(picker, offsets, NT, precision=lax.Precision.HIGHEST)
+        made = [mm(own, near_dq, TN), mm(everyone, dk, TN), mm(everyone, dv, TN)]
+        rest = jnp.concatenate([grad_out_w] + [g.astype(BF16) for g in made])[None]
+        through_kv = mm(dk, w_key, NT) + mm(dv, w_value, NT)
+        through_q = mm(near_dq, w_query, NT)
+        raw = jnp.concatenate([near, near_other, far, far_other]).astype(F32)
+        scaled = raw * rms_scale(raw)
+        near_scaled = jnp.concatenate([scaled[:rows], scaled[2 * rows : 3 * rows]])
+        grad_one = jnp.sum(through_kv * scaled, axis=0) + jnp.sum(through_q * near_scaled, axis=0)
+        small = jnp.concatenate([grad_one[None], grad_two[None], grad_end[None], jnp.pad(grad_bias.reshape(1, -1), ((0, 0), (0, width - grad_bias.size)))])
+        small = jnp.pad(small, ((0, 12), (0, 0))).astype(BF16)
+        through_kv = through_kv.reshape(2, 2, rows, width)
+        keep = through_q + through_kv[:, 0].reshape(2 * rows, width)
+        send = through_kv[:, 1].reshape(2 * rows, width).astype(BF16)
+        return (rest, small, keep, send), token
+
+    (big,), token, (rest, small, grad_hidden, sent) = phase([scatter([big], [line[0]])], token, weights)
+    hand = ([(sent, c)], lambda got: got[0])
+    (big, (rest, small), came), token, _ = phase([scatter(big, [line[1]]), scatter([rest], [c], small), hand], token)
+    for step in line[2:]:
+        (big,), token, _ = phase([scatter(big, [step])], token)
+
+    def ending(token):
+        token, kept = lax.optimization_barrier((token, grad_hidden))
+        grad_norm, _ = norm_back(kept + came.astype(F32), tokens, rms_scale(tokens), norm1_gain)
+        return (grad_mixed + grad_norm).astype(BF16), token
+
+    for step in reversed(line[2:]):
+        (big,), token, _ = phase([gather(big, [step])], token)
+    (big, (rest, small)), token, input_grad = phase([gather(big, [line[1]]), scatter(pairwise(rest[0]), [y, x], small)], token, ending)
+    away = ([(input_grad[rows:], y)], lambda got: got[0])
+    (big, (rest, small), away), token, _ = phase([gather(big, [line[0]]), scatter(rest, [x, y], small), away], token)
+    rest = jnp.concatenate(rest)
+    big = [big[0][:1], big[0][1:]]
+    pool = ([(pool_part, c)], lambda got: got[0])
+    (big, (rest, small), pool_got), token, _ = phase([gather(big, [x, y]), scatter([rest], [line[0]], small), pool], token)
+    pool_mine = (pool_part + pool_got) / count
+    pool = ([(pool_mine, y)], lambda got: got[0])
+    (big, (rest, small), pool_other), token, _ = phase([gather(big, [y, x]), scatter(rest, [line[1]], small), pool], token)
+    for step in line[2:]:
+        ((rest, small),), token, _ = phase([scatter(rest, [step], small)], token)
+    for step in reversed(line[2:]):
+        (rest,), token, _ = phase([gather(rest, [step])], token)
+    big = [jnp.concatenate(big, 1)]
+    (big, rest), token, _ = phase([gather(big, [c]), gather(rest, [line[1]])], token)
+
+    def convert(token):
+        token, value = lax.optimization_barrier((token, big[0][0]))
+        split = w_back.shape[0]
+        first = value[:split].astype(F32)
+        second = value[split:].reshape(folds, width, width).swapaxes(0, 1).reshape(width, folds * width).astype(F32)
+        return (first, second), token
+
+    (rest,), token, (out_back, out_in) = phase([gather(rest, [line[0]])], token, convert)
+    rest = [rest[0][:1], rest[0][1:]]
+    (rest,), token, _ = phase([gather(rest, [x, y])], token)
+    (rest,), token, _ = phase([gather(rest, [y, x])], token)
+    (rest,), token, _ = phase([gather([jnp.concatenate(rest, 1)], [c])], token)
+    grads = [rest[0][0, i * width : (i + 1) * width].astype(F32) for i in range(4)]
+    pooled = jnp.where(doc == 0, jnp.concatenate([pool_mine, pool_other]), jnp.concatenate([pool_other, pool_mine]))
     home = input_grad[:rows]
     input_grad = jnp.where(doc == 0, jnp.stack([home, away]), jnp.stack([away, home]))
-    small = jnp.concatenate([jnp.stack([grad_one, grad_two, grad_end]), jnp.pad(grad_bias.reshape(1, -1), ((0, 0), (0, width - grad_bias.size)))])
-    small = reduce_small(small)
-    split = w_in.shape[1]
-    grads = [rest[i * width : (i + 1) * width].astype(F32) for i in range(4)]
+    small = small.astype(F32)
     return (
         pooled,
         input_grad,
@@ -305,12 +402,12 @@
         grads[2],
         grads[3],
         grads[0],
-        big[split:].astype(F32).T,
-        big[:split].astype(F32),
+        out_in,
+        out_back,
         small[0],
         small[1],
         small[2],
-        small[3, : grad_bias.size].reshape(grad_bias.shape),
+        small[3, : bias_table.size].reshape(bias_table.shape),
     )
 
 def solution(mesh):

time: 313 us -> 234 us (0.75)
  waiting for transfers between devices: 117 us -> 49.7 us
  starting transfers between devices: 60.6 us -> 35.2 us
  matrix products: 35.1 us -> 24.9 us
  local copies, waits for them, and re-layouts: 24.4 us -> 34.4 us
  Pallas kernels: 33.2 us -> 42.8 us
  other arithmetic: 33.4 us -> 40.6 us
    ppermute x64 -> x35, waiting for transfers between devices: 117 us -> 49.7 us  [exchange(): return lax.ppermute(value, axis, [(i, i ^ bit) for i in range(size)])]
    ppermute x64 -> x35, starting transfers between devices: 60.6 us -> 35.2 us  [exchange(): return lax.ppermute(value, axis, [(i, i ^ bit) for i in range(size)])]
    dot_general x21 -> x18, matrix products: 34.7 us -> 23 us  [mm(): return lax.dot_general(a, b, dims, preferred_element_type=F32)]
    pallas_call x0 -> x2, Pallas kernels: none -> 6.57 us  [project(): pl.pallas_call(project_kernel, out_shape=[shape(2 * rows), shape(rows), s...]
    unnamed x95 -> x122, local copies, waits for them, and re-layouts: 15.6 us -> 10.3 us
    slice x9 -> x10, local copies, waits for them, and re-layouts: 1.82 us -> 6.94 us  [the longest x2 2.49 us: local(): own = jnp.concatenate([hid_l[:rows], hid_r[:rows]])]
    pallas_call x1 -> x2, Pallas kernels: 20.1 us -> 23 us  [attention_grads(): pl.pallas_call(bwd_kernel, grid=(pairs,), in_specs=[pl.BlockSpec(memory_s...]
    select_n x26 -> x21, other arithmetic: 7.01 us -> 9.57 us  [the longest x20 9.02 us: join(): jnp.where(side(move) == 0, jnp.concatenate([value, got], 1), jnp.concaten...]
  transfers between devices with their start and end apart: 64 -> 35, of which waited for: 39 -> 16; matrix products, arithmetic and copies ran while one was open for 13% -> 20% of each run, Pallas kernels for 0% -> 6%
where the time goes in v1:
time: 234 us; the launch traced here: 231 us
  waiting for transfers between devices  49.7 us (21%)
  Pallas kernels  42.8 us (18%)
  other arithmetic  40.6 us (17%)
  starting transfers between devices  35.2 us (15%)
  local copies, waits for them, and re-layouts  34.4 us (15%)
  matrix products  24.9 us (11%)
  between operations  3.48 us (1%)
    ppermute x35, waiting for transfers between devices, exchange(): return lax.ppermute(value, axis, [(i, i ^ bit) for i in range(size)])  49.7 us
    ppermute x35, starting transfers between devices, exchange(): return lax.ppermute(value, axis, [(i, i ^ bit) for i in range(size)])  35.2 us
    pallas_call x2, Pallas kernels, attention_grads(): pl.pallas_call(bwd_kernel, grid=(pairs,), in_specs=[pl.BlockSpec(memory_s...  23 us
    dot_general x18, matrix products, mm(): return lax.dot_general(a, b, dims, preferred_element_type=F32)  23 us
    pallas_call x1, Pallas kernels, attention(): pl.pallas_call(fwd_kernel, grid=(pairs,), in_specs=[pl.BlockSpec(memory_s...  13.2 us
    unnamed x122, local copies, waits for them, and re-layouts  10.3 us
    convert_element_type x18, other arithmetic, add(): return (keep.astype(F32) + got.astype(F32)).astype(BF16)  9.42 us
    select_n x20, other arithmetic, join(): jnp.where(side(move) == 0, jnp.concatenate([value, got], 1), jnp.concaten...  9.02 us
  transfers between devices with their start and end apart: 35, of which 16 were waited for; matrix products, arithmetic and copies ran while one was open for 20% of the time, Pallas kernels for 6%

profile of v1, /device:TPU:0, one launch (start us, length us, event | category | flops | bytes accessed | tf_op | source)
XLA Modules:
  0.0 231.1 jit_solution(10940919219710428204)
XLA Ops:
  1.9 3.0 %collective-permute-start = (bf16[256,512]{1,0:T(8,128)(2,1)S(1)}, bf16[256,512]{1,0:T(8,128)(2,1)S(1)}, u32[]{:S(2)}, u32[]{:S(2)}) collective-permute-start(bf16[256,512]{1,0:T(8,128)(2,1)S(1)} %get-tuple-element.267), channel_id=1, source_target_pairs={{0,2},{1,3},{2,0},{3,1},{4,6},{5,7},{6,4},{7,5},{8,10},{9,11},{10,... | collective-permute-start | bytes 786440 | tf_op jit(solution)/shard_map/ppermute | solution.py:193
  8.5 2.8 %collective-permute-done.mine = bf16[256,512]{1,0:T(8,128)(2,1)S(1)} collective-permute-done((bf16[256,512]{1,0:T(8,128)(2,1)S(1)}, bf16[256,512]{1,0:T(8,128)(2,1)S(1)}, u32[]{:S(2)}, u32[]{:S(2)}) %collective-permute-start) | collective-permute-done | bytes 262176 | tf_op jit(solution)/shard_map/ppermute | solution.py:193
  16.4 3.3 %project.2 = (bf16[512,512]{1,0:T(8,128)(2,1)}, bf16[256,512]{1,0:T(8,128)(2,1)}, bf16[512,512]{1,0:T(8,128)(2,1)}, bf16[512,512]{1,0:T(8,128)(2,1)}) custom-call(bf16[256,512]{1,0:T(8,128)(2,1)} %copy-done.2, bf16[256,512]{1,0:T(8,128)(2,1)} %copy-done.25, bf16[512,512]{1,0:T(8,128)(2,1)} %wq.3, bf16[512,512]{1,0:T(8,128)(2,1)} %wk.3, bf16[512,512]{1,0:T(8,128)(2,1)} %wv.3, ...), custom_call_target="tpu_custom_call" | custom-call | tf_op jit(solution)/shard_map/project/pallas_call | solution.py:185
  20.5 3.3 %project.3 = (bf16[512,512]{1,0:T(8,128)(2,1)}, bf16[256,512]{1,0:T(8,128)(2,1)}, bf16[512,512]{1,0:T(8,128)(2,1)}, bf16[512,512]{1,0:T(8,128)(2,1)}) custom-call(bf16[256,512]{1,0:T(8,128)(2,1)} %copy-done.5, bf16[256,512]{1,0:T(8,128)(2,1)} %copy-done.27, bf16[512,512]{1,0:T(8,128)(2,1)} %wq.3, bf16[512,512]{1,0:T(8,128)(2,1)} %wk.3, bf16[512,512]{1,0:T(8,128)(2,1)} %wv.3, ...), custom_call_target="tpu_custom_call" | custom-call | tf_op jit(solution)/shard_map/project/pallas_call | solution.py:185
  23.8 13.2 %attn_fwd.1 = (bf16[512,512]{1,0:T(8,128)(2,1)}, bf16[8,512,1024]{2,1,0:T(8,128)(2,1)}, f32[512,512]{1,0:T(8,128)}) custom-call(s32[8]{0:T(128)} %compare_select_fusion.5.info, bf16[256,512]{1,0:T(8,128)(2,1)} %get-tuple-element.113.ql, bf16[256,512]{1,0:T(8,128)(2,1)} %get-tuple-element.114.qr, bf16[512,512]{1,0:T(8,128)(2,1)} %get-tuple-element.115.kl, ...), custom_call_target="tpu_custom_call" | custom-call | tf_op jit(solution)/shard_map/attn_fwd/pallas_call | solution.py:73
  54.0 3.1 %multiply_reduce_fusion.1 = (bf16[512]{0:T(512)(128)(2,1)S(1)}, f32[512]{0:T(512)S(1)}, f32[512,512]{1,0:T(8,128)S(1)}) fusion(f32[512,512]{1,0:T(8,128)S(1)} %copy-done.15, f32[512]{0:T(512)S(1)} %get-tuple-element.279, f32[512]{0:T(512)S(1)} %copy-done.51, bf16[512,2048]{1,0:T(8,128)(2,1)} %copy-done.58, bf16[512,2048]{1,0:T(8,128)(2,1)S(1)} %copy-done), kind=kOutput, calls=%fused_computation.67 | convolution fusion | flops 1075313664 | bytes 6298624 | tf_op jit(solution)/shard_map/dot_general | solution.py:246
  60.7 2.2 fusion
  69.3 11.4 %attn_bwd.2 = (bf16[512,256]{1,0:T(8,128)(2,1)}, bf16[1024,256]{1,0:T(8,128)(2,1)}, bf16[1024,256]{1,0:T(8,128)(2,1)}, f32[2,2,2048]{2,1,0:T(2,128)}) custom-call(s32[8]{0:T(128)} %compare_select_fusion.5.info, bf16[256,512]{1,0:T(8,128)(2,1)} %get-tuple-element.113.ql, bf16[256,512]{1,0:T(8,128)(2,1)} %get-tuple-element.114.qr, ...), custom_call_target="tpu_custom_call" | custom-call | tf_op jit(solution)/shard_map/attn_bwd/pallas_call | solution.py:148
  80.7 2.0 constant_dynamic-update-slice_fusion.5
  82.7 1.9 constant_dynamic-update-slice_fusion.3
  88.7 11.6 %attn_bwd.3 = (bf16[512,256]{1,0:T(8,128)(2,1)}, bf16[1024,256]{1,0:T(8,128)(2,1)}, bf16[1024,256]{1,0:T(8,128)(2,1)}, f32[2,2,2048]{2,1,0:T(2,128)}) custom-call(s32[8]{0:T(128)} %compare_select_fusion.5.info, bf16[256,512]{1,0:T(8,128)(2,1)} %get-tuple-element.113.ql, bf16[256,512]{1,0:T(8,128)(2,1)} %get-tuple-element.114.qr, ...), custom_call_target="tpu_custom_call" | custom-call | tf_op jit(solution)/shard_map/attn_bwd/pallas_call | solution.py:148
  100.4 1.9 pad_maximum_fusion.6
  102.2 1.9 constant_dynamic-update-slice_fusion.2
  104.1 2.1 fusion.60
  115.6 2.0 bitcast_add_fusion
  119.0 2.1 slice.225
  127.8 4.3 %collective-permute-done.8 = bf16[2,128,512]{2,1,0:T(8,128)(2,1)S(1)} collective-permute-done((bf16[2,128,512]{2,1,0:T(8,128)(2,1)S(1)}, bf16[2,128,512]{2,1,0:T(8,128)(2,1)S(1)}, u32[]{:S(2)}, u32[]{:S(2)}) %collective-permute-start.8) | collective-permute-done | bytes 262176 | tf_op jit(solution)/shard_map/ppermute | solution.py:193
  133.4 2.8 %collective-permute-start.9 = (bf16[2,64,512]{2,1,0:T(8,128)(2,1)}, bf16[2,64,512]{2,1,0:T(8,128)(2,1)S(1)}, u32[]{:S(2)}, u32[]{:S(2)}) collective-permute-start(bf16[2,64,512]{2,1,0:T(8,128)(2,1)} %constant_dynamic-slice_fusion.4), channel_id=1, source_target_pairs={{0,16},{4,20},{8,24},{12,28},{16,0},{20,4},{24,8},{28,12},{1,17},{... | collective-permute-start | bytes 393224 | tf_op jit(solution)/shard_map/ppermute | solution.py:193
  136.2 6.7 %collective-permute-done.9 = bf16[2,64,512]{2,1,0:T(8,128)(2,1)S(1)} collective-permute-done((bf16[2,64,512]{2,1,0:T(8,128)(2,1)}, bf16[2,64,512]{2,1,0:T(8,128)(2,1)S(1)}, u32[]{:S(2)}, u32[]{:S(2)}) %collective-permute-start.9) | collective-permute-done | bytes 131104 | tf_op jit(solution)/shard_map/ppermute | solution.py:193
  149.3 7.7 %collective-permute-done.12 = bf16[2,64,512]{2,1,0:T(8,128)(2,1)S(1)} collective-permute-done((bf16[2,64,512]{2,1,0:T(8,128)(2,1)S(1)}, bf16[2,64,512]{2,1,0:T(8,128)(2,1)S(1)}, u32[]{:S(2)}, u32[]{:S(2)}) %collective-permute-start.12) | collective-permute-done | bytes 131104 | tf_op jit(solution)/shard_map/ppermute | solution.py:193
  160.0 6.1 %collective-permute-done.17 = bf16[1,128,512]{2,1,0:T(8,128)(2,1)S(1)} collective-permute-done((bf16[1,128,512]{2,1,0:T(8,128)(2,1)S(1)}, bf16[1,128,512]{2,1,0:T(8,128)(2,1)S(1)}, u32[]{:S(2)}, u32[]{:S(2)}) %collective-permute-start.17) | collective-permute-done | bytes 131104 | tf_op jit(solution)/shard_map/ppermute | solution.py:193
  170.7 3.5 %collective-permute-done.21 = bf16[144,512]{1,0:T(8,128)(2,1)S(1)} collective-permute-done((bf16[144,512]{1,0:T(8,128)(2,1)S(1)}, bf16[144,512]{1,0:T(8,128)(2,1)S(1)}, u32[]{:S(2)}, u32[]{:S(2)}) %collective-permute-start.21) | collective-permute-done | bytes 147488 | tf_op jit(solution)/shard_map/ppermute | solution.py:193
  180.0 3.3 %collective-permute-start.25 = (bf16[80,512]{1,0:T(8,128)(2,1)}, bf16[80,512]{1,0:T(8,128)(2,1)S(1)}, u32[]{:S(2)}, u32[]{:S(2)}) collective-permute-start(bf16[80,512]{1,0:T(8,128)(2,1)} %pad_maximum_fusion.10), channel_id=1, source_target_pairs={{0,16},{4,20},{8,24},{12,28},{16,0},{20,4},{24,8},{28,12},{1,17},{... | collective-permute-start | bytes 245768 | tf_op jit(solution)/shard_map/ppermute | solution.py:193
  184.8 4.3 %collective-permute-done.26 = f32[1,512]{1,0:T(1,128)S(1)} collective-permute-done((f32[1,512]{1,0:T(1,128)}, f32[1,512]{1,0:T(1,128)S(1)}, u32[]{:S(2)}, u32[]{:S(2)}) %collective-permute-start.26) | collective-permute-done | bytes 2080 | tf_op jit(solution)/shard_map/ppermute | solution.py:193
  195.0 3.1 %collective-permute-start.28 = (bf16[2,32,512]{2,1,0:T(8,128)(2,1)S(1)}, bf16[2,32,512]{2,1,0:T(8,128)(2,1)S(1)}, u32[]{:S(2)}, u32[]{:S(2)}) collective-permute-start(bf16[2,32,512]{2,1,0:T(8,128)(2,1)S(1)} %fusion.46), channel_id=1, source_target_pairs={{0,16},{4,20},{8,24},{12,28},{16,0},{20,4},{24,8},{28,12},{1,17},{... | collective-permute-start | bytes 196616 | tf_op jit(solution)/shard_map/ppermute | solution.py:193
  200.1 2.2 collective-permute-done.28
  203.4 4.4 %collective-permute-done.29 = bf16[2,64,512]{2,1,0:T(8,128)(2,1)S(1)} collective-permute-done((bf16[2,64,512]{2,1,0:T(8,128)(2,1)S(1)}, bf16[2,64,512]{2,1,0:T(8,128)(2,1)S(1)}, u32[]{:S(2)}, u32[]{:S(2)}) %collective-permute-start.29) | collective-permute-done | bytes 131104 | tf_op jit(solution)/shard_map/ppermute | solution.py:193
  209.8 3.1 %collective-permute-done.30 = bf16[1,128,512]{2,1,0:T(8,128)(2,1)S(1)} collective-permute-done((bf16[1,128,512]{2,1,0:T(8,128)(2,1)S(1)}, bf16[1,128,512]{2,1,0:T(8,128)(2,1)S(1)}, u32[]{:S(2)}, u32[]{:S(2)}) %collective-permute-start.30) | collective-permute-done | bytes 131104 | tf_op jit(solution)/shard_map/ppermute | solution.py:193
  216.0 3.1 %maximum_select_fusion = bf16[4096,512]{1,0:T(8,128)(2,1)S(1)} fusion(bf16[2048,512]{1,0:T(8,128)(2,1)} %bitcast.46, bf16[1024,512]{1,0:T(8,128)(2,1)S(1)} %maximum_select_fusion.5, bf16[1024,512]{1,0:T(8,128)(2,1)S(1)} %maximum_select_fusion.4, pred[]{:T(512)S(6)} %eq.99), kind=kLoop, calls=%fused_computation | loop fusion | flops 27262976 | bytes 8388609 | tf_op jit(solution)/shard_map/jit(_where)/select_n | solution.py:208
  221.4 2.7 %slice_convert_fusion = (f32[2048,512]{1,0:T(8,128)}, bf16[2048,512]{1,0:T(8,128)(2,1)S(1)}) fusion(bf16[4096,512]{1,0:T(8,128)(2,1)S(1)} %maximum_select_fusion), kind=kLoop, calls=%fused_computation.13 | loop fusion | flops 1048576 | bytes 10485760 | tf_op jit(solution)/shard_map/convert_element_type | solution.py:384
  224.8 2.7 %copy.36 = f32[4,64,8,512]{3,2,0,1:T(8,128)} copy(f32[4,64,8,512]{3,2,1,0:T(8,128)S(1)} %convert_bitcast_fusion) | data formatting | bytes 8388608 | tf_op jit(solution)/shard_map/convert_element_type | solution.py:385
  228.6 2.2 fusion.22
  (306 shorter events, 97.8 us)
Async XLA Ops:
  1.9 9.3 %collective-permute-start = (bf16[256,512]{1,0:T(8,128)(2,1)S(1)}, bf16[256,512]{1,0:T(8,128)(2,1)S(1)}, u32[]{:S(2)}, u32[]{:S(2)}) collective-permute-start(bf16[256,512]{1,0:T(8,128)(2,1)S(1)} %get-tuple-element.267), channel_id=1, source_target_pairs={{0,2},{1,3},{2,0},{3,1},{4,6},{5,7},{6,4},{7,5},{8,10},{9,11},{10,... | collective-permute-start | bytes 786440 | tf_op jit(solution)/shard_map/ppermute | solution.py:193
  4.9 10.8 %collective-permute-start.1 = (bf16[256,512]{1,0:T(8,128)(2,1)S(1)}, bf16[256,512]{1,0:T(8,128)(2,1)S(1)}, u32[]{:S(2)}, u32[]{:S(2)}) collective-permute-start(bf16[256,512]{1,0:T(8,128)(2,1)S(1)} %get-tuple-element.268.mine), channel_id=1, source_target_pairs={{0,1},{1,0},{2,3},{3,2},{4,5},{5,4},{6,7},{7,6},{8,9},{9,8},{10,11... | collective-permute-start | bytes 786440 | tf_op jit(solution)/shard_map/ppermute | solution.py:193
  11.3 8.5 %collective-permute-start.2 = (bf16[256,512]{1,0:T(8,128)(2,1)S(1)}, bf16[256,512]{1,0:T(8,128)(2,1)S(1)}, u32[]{:S(2)}, u32[]{:S(2)}) collective-permute-start(bf16[256,512]{1,0:T(8,128)(2,1)S(1)} %collective-permute-done.mine), channel_id=1, source_target_pairs={{0,1},{1,0},{2,3},{3,2},{4,5},{5,4},{6,7},{7,6},{8,9},{9,8},{10,11... | collective-permute-start | bytes 786440 | tf_op jit(solution)/shard_map/ppermute | solution.py:193
  49.9 10.7 %collective-permute-start.3 = (bf16[1,2048,512]{2,1,0:T(8,128)(2,1)}, bf16[1,2048,512]{2,1,0:T(8,128)(2,1)}, u32[]{:S(2)}, u32[]{:S(2)}) collective-permute-start(bf16[1,2048,512]{2,1,0:T(8,128)(2,1)} %dynamic-slice_bitcast_fusion), channel_id=1, source_target_pairs={{0,1},{1,0},{2,3},{3,2},{4,5},{5,4},{6,7},{7,6},{8,9},{9,8},{10,11... | collective-permute-start | bytes 6291464 | tf_op jit(solution)/shard_map/ppermute | solution.py:193
  64.8 19.8 %collective-permute-start.4 = (bf16[1,512,512]{2,1,0:T(8,128)(2,1)}, bf16[1,512,512]{2,1,0:T(8,128)(2,1)}, u32[]{:S(2)}, u32[]{:S(2)}) collective-permute-start(bf16[1,512,512]{2,1,0:T(8,128)(2,1)} %constant_dynamic-slice_fusion.8), channel_id=1, source_target_pairs={{0,2},{1,3},{2,0},{3,1},{4,6},{5,7},{6,4},{7,5},{8,10},{9,11},{10,... | collective-permute-start | bytes 1572872 | tf_op jit(solution)/shard_map/ppermute | solution.py:193
  66.5 18.1 %collective-permute-start.5 = (bf16[1,512,512]{2,1,0:T(8,128)(2,1)}, bf16[1,512,512]{2,1,0:T(8,128)(2,1)}, u32[]{:S(2)}, u32[]{:S(2)}) collective-permute-start(bf16[1,512,512]{2,1,0:T(8,128)(2,1)} %constant_dynamic-slice_fusion.7), channel_id=1, source_target_pairs={{0,4},{4,0},{8,12},{12,8},{16,20},{20,16},{24,28},{28,24},{1,5},{5... | collective-permute-start | bytes 1572872 | tf_op jit(solution)/shard_map/ppermute | solution.py:193
  114.1 8.6 %collective-permute-start.6 = (bf16[1,256,512]{2,1,0:T(8,128)(2,1)}, bf16[1,256,512]{2,1,0:T(8,128)(2,1)}, u32[]{:S(2)}, u32[]{:S(2)}) collective-permute-start(bf16[1,256,512]{2,1,0:T(8,128)(2,1)} %constant_dynamic-slice_fusion.6), channel_id=1, source_target_pairs={{0,4},{4,0},{8,12},{12,8},{16,20},{20,16},{24,28},{28,24},{1,5},{5... | collective-permute-start | bytes 786440 | tf_op jit(solution)/shard_map/ppermute | solution.py:193
  114.7 8.0 %collective-permute-start.7 = (bf16[1,256,512]{2,1,0:T(8,128)(2,1)S(1)}, bf16[1,256,512]{2,1,0:T(8,128)(2,1)}, u32[]{:S(2)}, u32[]{:S(2)}) collective-permute-start(bf16[1,256,512]{2,1,0:T(8,128)(2,1)S(1)} %constant_dynamic-slice_fusion.5), channel_id=1, source_target_pairs={{0,2},{1,3},{2,0},{3,1},{4,6},{5,7},{6,4},{7,5},{8,10},{9,11},{10,... | collective-permute-start | bytes 786440 | tf_op jit(solution)/shard_map/ppermute | solution.py:193
  124.9 7.3 %collective-permute-start.8 = (bf16[2,128,512]{2,1,0:T(8,128)(2,1)S(1)}, bf16[2,128,512]{2,1,0:T(8,128)(2,1)S(1)}, u32[]{:S(2)}, u32[]{:S(2)}) collective-permute-start(bf16[2,128,512]{2,1,0:T(8,128)(2,1)S(1)} %fusion.36), channel_id=1, source_target_pairs={{0,8},{4,12},{8,0},{12,4},{16,24},{20,28},{24,16},{28,20},{1,9},{5... | collective-permute-start | bytes 786440 | tf_op jit(solution)/shard_map/ppermute | solution.py:193
  132.9 10.0 %collective-permute-start.10 = (bf16[1040,512]{1,0:T(8,128)(2,1)}, bf16[1040,512]{1,0:T(8,128)(2,1)}, u32[]{:S(2)}, u32[]{:S(2)}) collective-permute-start(bf16[1040,512]{1,0:T(8,128)(2,1)} %pad_maximum_fusion.2), channel_id=1, source_target_pairs={{0,1},{1,0},{2,3},{3,2},{4,5},{5,4},{6,7},{7,6},{8,9},{9,8},{10,11... | collective-permute-start | bytes 3194888 | tf_op jit(solution)/shard_map/ppermute | solution.py:193
  132.9 9.9 %collective-permute-start.11 = (bf16[512,512]{1,0:T(8,128)(2,1)}, bf16[512,512]{1,0:T(8,128)(2,1)S(1)}, u32[]{:S(2)}, u32[]{:S(2)}) collective-permute-start(bf16[512,512]{1,0:T(8,128)(2,1)} %bitcast.11), channel_id=1, source_target_pairs={{0,1},{1,0},{2,3},{3,2},{4,5},{5,4},{6,7},{7,6},{8,9},{9,8},{10,11... | collective-permute-start | bytes 1572872 | tf_op jit(solution)/shard_map/ppermute | solution.py:193
  133.4 9.4 %collective-permute-start.9 = (bf16[2,64,512]{2,1,0:T(8,128)(2,1)}, bf16[2,64,512]{2,1,0:T(8,128)(2,1)S(1)}, u32[]{:S(2)}, u32[]{:S(2)}) collective-permute-start(bf16[2,64,512]{2,1,0:T(8,128)(2,1)} %constant_dynamic-slice_fusion.4), channel_id=1, source_target_pairs={{0,16},{4,20},{8,24},{12,28},{16,0},{20,4},{24,8},{28,12},{1,17},{... | collective-permute-start | bytes 393224 | tf_op jit(solution)/shard_map/ppermute | solution.py:193
  145.7 11.2 %collective-permute-start.13 = (bf16[272,512]{1,0:T(8,128)(2,1)S(1)}, bf16[272,512]{1,0:T(8,128)(2,1)S(1)}, u32[]{:S(2)}, u32[]{:S(2)}) collective-permute-start(bf16[272,512]{1,0:T(8,128)(2,1)S(1)} %pad_maximum_fusion.7), channel_id=1, source_target_pairs={{0,2},{1,3},{2,0},{3,1},{4,6},{5,7},{6,4},{7,5},{8,10},{9,11},{10,... | collective-permute-start | bytes 835592 | tf_op jit(solution)/shard_map/ppermute | solution.py:193
  147.4 9.6 %collective-permute-start.14 = (bf16[1,256,512]{2,1,0:T(8,128)(2,1)S(1)}, bf16[1,256,512]{2,1,0:T(8,128)(2,1)S(1)}, u32[]{:S(2)}, u32[]{:S(2)}) collective-permute-start(bf16[1,256,512]{2,1,0:T(8,128)(2,1)S(1)} %constant_dynamic-slice_fusion.2), channel_id=1, source_target_pairs={{0,4},{4,0},{8,12},{12,8},{16,20},{20,16},{24,28},{28,24},{1,5},{5... | collective-permute-start | bytes 786440 | tf_op jit(solution)/shard_map/ppermute | solution.py:193
  148.9 8.1 %collective-permute-start.12 = (bf16[2,64,512]{2,1,0:T(8,128)(2,1)S(1)}, bf16[2,64,512]{2,1,0:T(8,128)(2,1)S(1)}, u32[]{:S(2)}, u32[]{:S(2)}) collective-permute-start(bf16[2,64,512]{2,1,0:T(8,128)(2,1)S(1)} %add_convert_fusion.8), channel_id=1, source_target_pairs={{0,16},{4,20},{8,24},{12,28},{16,0},{20,4},{24,8},{28,12},{1,17},{... | collective-permute-start | bytes 393224 | tf_op jit(solution)/shard_map/ppermute | solution.py:193
  157.3 8.8 %collective-permute-start.15 = (bf16[2,128,512]{2,1,0:T(8,128)(2,1)S(1)}, bf16[2,128,512]{2,1,0:T(8,128)(2,1)S(1)}, u32[]{:S(2)}, u32[]{:S(2)}) collective-permute-start(bf16[2,128,512]{2,1,0:T(8,128)(2,1)S(1)} %maximum_select_fusion.16), channel_id=1, source_target_pairs={{0,8},{4,12},{8,0},{12,4},{16,24},{20,28},{24,16},{28,20},{1,9},{5... | collective-permute-start | bytes 786440 | tf_op jit(solution)/shard_map/ppermute | solution.py:193
  157.3 8.7 %collective-permute-start.18 = (bf16[256,512]{1,0:T(8,128)(2,1)S(1)}, bf16[256,512]{1,0:T(8,128)(2,1)S(1)}, u32[]{:S(2)}, u32[]{:S(2)}) collective-permute-start(bf16[256,512]{1,0:T(8,128)(2,1)S(1)} %get-tuple-element.180), channel_id=1, source_target_pairs={{0,2},{1,3},{2,0},{3,1},{4,6},{5,7},{6,4},{7,5},{8,10},{9,11},{10,... | collective-permute-start | bytes 786440 | tf_op jit(solution)/shard_map/ppermute | solution.py:193
  157.9 8.2 %collective-permute-start.16 = (bf16[144,512]{1,0:T(8,128)(2,1)S(1)}, bf16[144,512]{1,0:T(8,128)(2,1)S(1)}, u32[]{:S(2)}, u32[]{:S(2)}) collective-permute-start(bf16[144,512]{1,0:T(8,128)(2,1)S(1)} %pad_maximum_fusion.8), channel_id=1, source_target_pairs={{0,4},{4,0},{8,12},{12,8},{16,20},{20,16},{24,28},{28,24},{1,5},{5... | collective-permute-start | bytes 442376 | tf_op jit(solution)/shard_map/ppermute | solution.py:193
  158.6 7.5 %collective-permute-start.17 = (bf16[1,128,512]{2,1,0:T(8,128)(2,1)S(1)}, bf16[1,128,512]{2,1,0:T(8,128)(2,1)S(1)}, u32[]{:S(2)}, u32[]{:S(2)}) collective-permute-start(bf16[1,128,512]{2,1,0:T(8,128)(2,1)S(1)} %constant_dynamic-slice_fusion.1), channel_id=1, source_target_pairs={{0,2},{1,3},{2,0},{3,1},{4,6},{5,7},{6,4},{7,5},{8,10},{9,11},{10,... | collective-permute-start | bytes 393224 | tf_op jit(solution)/shard_map/ppermute | solution.py:193
  166.6 7.7 %collective-permute-start.19 = (bf16[1,256,512]{2,1,0:T(8,128)(2,1)S(1)}, bf16[1,256,512]{2,1,0:T(8,128)(2,1)S(1)}, u32[]{:S(2)}, u32[]{:S(2)}) collective-permute-start(bf16[1,256,512]{2,1,0:T(8,128)(2,1)S(1)} %get-tuple-element.185), channel_id=1, source_target_pairs={{0,4},{4,0},{8,12},{12,8},{16,20},{20,16},{24,28},{28,24},{1,5},{5... | collective-permute-start | bytes 786440 | tf_op jit(solution)/shard_map/ppermute | solution.py:193
  168.1 6.4 %collective-permute-start.20 = (bf16[1,256,512]{2,1,0:T(8,128)(2,1)S(1)}, bf16[1,256,512]{2,1,0:T(8,128)(2,1)S(1)}, u32[]{:S(2)}, u32[]{:S(2)}) collective-permute-start(bf16[1,256,512]{2,1,0:T(8,128)(2,1)S(1)} %get-tuple-element.186), channel_id=1, source_target_pairs={{0,2},{1,3},{2,0},{3,1},{4,6},{5,7},{6,4},{7,5},{8,10},{9,11},{10,... | collective-permute-start | bytes 786440 | tf_op jit(solution)/shard_map/ppermute | solution.py:193
  169.1 5.1 %collective-permute-start.21 = (bf16[144,512]{1,0:T(8,128)(2,1)S(1)}, bf16[144,512]{1,0:T(8,128)(2,1)S(1)}, u32[]{:S(2)}, u32[]{:S(2)}) collective-permute-start(bf16[144,512]{1,0:T(8,128)(2,1)S(1)} %pad_maximum_fusion.9), channel_id=1, source_target_pairs={{0,8},{4,12},{8,0},{12,4},{16,24},{20,28},{24,16},{28,20},{1,9},{5... | collective-permute-start | bytes 442376 | tf_op jit(solution)/shard_map/ppermute | solution.py:193
  178.5 10.6 %collective-permute-start.23 = (bf16[1,512,512]{2,1,0:T(8,128)(2,1)}, bf16[1,512,512]{2,1,0:T(8,128)(2,1)S(1)}, u32[]{:S(2)}, u32[]{:S(2)}) collective-permute-start(bf16[1,512,512]{2,1,0:T(8,128)(2,1)} %maximum_select_fusion.7), channel_id=1, source_target_pairs={{0,2},{1,3},{2,0},{3,1},{4,6},{5,7},{6,4},{7,5},{8,10},{9,11},{10,... | collective-permute-start | bytes 1572872 | tf_op jit(solution)/shard_map/ppermute | solution.py:193
  179.4 10.7 %collective-permute-start.24 = (bf16[1,512,512]{2,1,0:T(8,128)(2,1)}, bf16[1,512,512]{2,1,0:T(8,128)(2,1)S(1)}, u32[]{:S(2)}, u32[]{:S(2)}) collective-permute-start(bf16[1,512,512]{2,1,0:T(8,128)(2,1)} %maximum_select_fusion.8), channel_id=1, source_target_pairs={{0,4},{4,0},{8,12},{12,8},{16,20},{20,16},{24,28},{28,24},{1,5},{5... | collective-permute-start | bytes 1572872 | tf_op jit(solution)/shard_map/ppermute | solution.py:193
  180.0 9.1 %collective-permute-start.25 = (bf16[80,512]{1,0:T(8,128)(2,1)}, bf16[80,512]{1,0:T(8,128)(2,1)S(1)}, u32[]{:S(2)}, u32[]{:S(2)}) collective-permute-start(bf16[80,512]{1,0:T(8,128)(2,1)} %pad_maximum_fusion.10), channel_id=1, source_target_pairs={{0,16},{4,20},{8,24},{12,28},{16,0},{20,4},{24,8},{28,12},{1,17},{... | collective-permute-start | bytes 245768 | tf_op jit(solution)/shard_map/ppermute | solution.py:193
  183.3 5.9 %collective-permute-start.26 = (f32[1,512]{1,0:T(1,128)}, f32[1,512]{1,0:T(1,128)S(1)}, u32[]{:S(2)}, u32[]{:S(2)}) collective-permute-start(f32[1,512]{1,0:T(1,128)} %add_divide_fusion), channel_id=1, source_target_pairs={{0,2},{1,3},{2,0},{3,1},{4,6},{5,7},{6,4},{7,5},{8,10},{9,11},{10,... | collective-permute-start | bytes 6152 | tf_op jit(solution)/shard_map/ppermute | solution.py:193
  192.6 9.7 %collective-permute-start.27 = (bf16[1,2048,512]{2,1,0:T(8,128)(2,1)}, bf16[1,2048,512]{2,1,0:T(8,128)(2,1)}, u32[]{:S(2)}, u32[]{:S(2)}) collective-permute-start(bf16[1,2048,512]{2,1,0:T(8,128)(2,1)} %pad_maximum_fusion.1), channel_id=1, source_target_pairs={{0,1},{1,0},{2,3},{3,2},{4,5},{5,4},{6,7},{7,6},{8,9},{9,8},{10,11... | collective-permute-start | bytes 6291464 | tf_op jit(solution)/shard_map/ppermute | solution.py:193
  195.0 7.3 %collective-permute-start.28 = (bf16[2,32,512]{2,1,0:T(8,128)(2,1)S(1)}, bf16[2,32,512]{2,1,0:T(8,128)(2,1)S(1)}, u32[]{:S(2)}, u32[]{:S(2)}) collective-permute-start(bf16[2,32,512]{2,1,0:T(8,128)(2,1)S(1)} %fusion.46), channel_id=1, source_target_pairs={{0,16},{4,20},{8,24},{12,28},{16,0},{20,4},{24,8},{28,12},{1,17},{... | collective-permute-start | bytes 196616 | tf_op jit(solution)/shard_map/ppermute | solution.py:193
  202.3 5.4 %collective-permute-start.29 = (bf16[2,64,512]{2,1,0:T(8,128)(2,1)S(1)}, bf16[2,64,512]{2,1,0:T(8,128)(2,1)S(1)}, u32[]{:S(2)}, u32[]{:S(2)}) collective-permute-start(bf16[2,64,512]{2,1,0:T(8,128)(2,1)S(1)} %maximum_select_fusion.22), channel_id=1, source_target_pairs={{0,8},{4,12},{8,0},{12,4},{16,24},{20,28},{24,16},{28,20},{1,9},{5... | collective-permute-start | bytes 393224 | tf_op jit(solution)/shard_map/ppermute | solution.py:193
  213.5 6.4 %collective-permute-start.32 = (bf16[1,256,512]{2,1,0:T(8,128)(2,1)S(1)}, bf16[1,256,512]{2,1,0:T(8,128)(2,1)S(1)}, u32[]{:S(2)}, u32[]{:S(2)}) collective-permute-start(bf16[1,256,512]{2,1,0:T(8,128)(2,1)S(1)} %maximum_select_fusion.19), channel_id=1, source_target_pairs={{0,2},{1,3},{2,0},{3,1},{4,6},{5,7},{6,4},{7,5},{8,10},{9,11},{10,... | collective-permute-start | bytes 786440 | tf_op jit(solution)/shard_map/ppermute | solution.py:193
  214.5 6.4 %collective-permute-start.33 = (bf16[1,256,512]{2,1,0:T(8,128)(2,1)S(1)}, bf16[1,256,512]{2,1,0:T(8,128)(2,1)S(1)}, u32[]{:S(2)}, u32[]{:S(2)}) collective-permute-start(bf16[1,256,512]{2,1,0:T(8,128)(2,1)S(1)} %maximum_select_fusion.20), channel_id=1, source_target_pairs={{0,4},{4,0},{8,12},{12,8},{16,20},{20,16},{24,28},{28,24},{1,5},{5... | collective-permute-start | bytes 786440 | tf_op jit(solution)/shard_map/ppermute | solution.py:193
  221.4 6.5 %collective-permute-start.34 = (bf16[1,1024,512]{2,1,0:T(8,128)(2,1)S(1)}, bf16[1,1024,512]{2,1,0:T(8,128)(2,1)S(1)}, u32[]{:S(2)}, u32[]{:S(2)}) collective-permute-start(bf16[1,1024,512]{2,1,0:T(8,128)(2,1)S(1)} %pad_maximum_fusion.4), channel_id=1, source_target_pairs={{0,1},{1,0},{2,3},{3,2},{4,5},{5,4},{6,7},{7,6},{8,9},{9,8},{10,11... | collective-permute-start | bytes 3145736 | tf_op jit(solution)/shard_map/ppermute | solution.py:193
  (62 other events, 419.7 us)

commit v2 on v0

--- a/solution.py
+++ b/solution.py
@@ -82,7 +82,7 @@
         name="attn_fwd",
     )(info, ql, qr, kl, kr, vl, vr, table)
 
-def bwd_kernel(info, ql, qr, kl, kr, vl, vr, gout, out, inv, expo, dq, dk, dv, diag, acc, tmp):
+def bwd_kernel(info, ql, qr, kl, kr, vl, vr, gout, out, inv, expo, dq, dk, dv, diag, acc):
     lane = lax.broadcasted_iota(jnp.int32, (1, 128), 1)
     kref = [(kl, 0), (kl, 256), (kr, 0), (kr, 256)]
     vref = [(vl, 0), (vl, 256), (vr, 0), (vr, 256)]
@@ -153,12 +153,13 @@
         out_specs=[col(512), col(1024), col(1024), pl.BlockSpec((None, 2, 2048), lambda g: (g, 0, 0))],
         out_shape=[jax.ShapeDtypeStruct((512, d), BF16), jax.ShapeDtypeStruct((1024, d), BF16),
                    jax.ShapeDtypeStruct((1024, d), BF16), jax.ShapeDtypeStruct((pairs, 2, 2048), F32)],
-        scratch_shapes=[pltpu.VMEM((128, 2048), F32), pltpu.VMEM((8, 128), F32)],
+        scratch_shapes=[pltpu.VMEM((128, 2048), F32)],
         name="attn_bwd",
     )(info, ql, qr, kl, kr, vl, vr, gout, out, inv, expo)
 
 BUCKETS = 32
 EPS = 1e-06
+CORE, ROW, NEAR_X = 1, 2, 4
 
 def rms_scale(values):
     return lax.rsqrt(jnp.mean(values * values, axis=-1, keepdims=True) + EPS)
@@ -167,150 +168,405 @@
     weighted = grad_out * gain
     inner = jnp.mean(weighted * values, axis=-1, keepdims=True)
     grad_in = scale * weighted - scale * scale * scale * values * inner
-    return grad_in, jnp.sum(grad_out * values * scale, axis=0)
-
-def exchange(value, axis, bit):
-    size = lax.axis_size(axis)
-    return lax.ppermute(value, axis, [(i, i ^ bit) for i in range(size)])
-
-def side(axis, bit):
-    return (lax.axis_index(axis) // bit) % 2
-
-def reduce_halves(value, steps):
-    for axis, bit in steps:
-        half = value.shape[0] // 2
-        mine = side(axis, bit)
-        keep = lax.dynamic_slice_in_dim(value, mine * half, half, 0)
-        send = lax.dynamic_slice_in_dim(value, (1 - mine) * half, half, 0)
-        value = (keep.astype(F32) + exchange(send, axis, bit).astype(F32)).astype(BF16)
-    return value
-
-def gather_halves(value, steps):
-    for axis, bit in reversed(steps):
-        other = exchange(value, axis, bit)
-        mine = side(axis, bit)
-        value = jnp.where(mine == 0, jnp.concatenate([value, other]), jnp.concatenate([other, value]))
-    return value
-
-def plans():
-    bits = [("dp", 1 << b) for b in range(lax.axis_size("dp").bit_length() - 1)]
-    near, rest = bits[0], bits[1:]
-    y = ("blk", 2)
-    return [[y, near] + rest, [near] + rest + [y], rest + [y, near]]
-
-def reduce_all(value, cuts):
-    core = [("blk", 1)]
-    value = reduce_halves(value, core)
-    at, pieces = 0, []
-    for rows, steps in zip(cuts, plans()):
-        if rows:
-            piece = lax.slice_in_dim(value, at, at + rows, axis=0)
-            pieces.append(gather_halves(reduce_halves(piece, steps), steps))
-        at += rows
-    return gather_halves(jnp.concatenate(pieces), core)
-
-def reduce_small(value):
-    for axis in ("blk", "dp"):
-        for b in range(lax.axis_size(axis).bit_length() - 1):
-            value = value + exchange(value, axis, 1 << b)
-    return value
-
-def mm(a, b, dims=NN):
-    return lax.dot_general(a, b, dims, preferred_element_type=F32)
+    return grad_in, jnp.sum(grad_out * values * scale, axis=0, keepdims=True)
+
+def two_terms(value):
+    high = value.astype(BF16)
+    low = (value - high.astype(F32)).astype(BF16)
+    fill = jnp.zeros((8 - value.shape[0], value.shape[1]), BF16)
+    return jnp.concatenate([high, fill, low, fill])
+
+def one_value(terms, count):
+    return terms[:count].astype(F32) + terms[8 : 8 + count].astype(F32)
+
+def project_kernel(mine, other, wq, wk, wv, gain, hidden, query, keys, values):
+    rows = mine.shape[0]
+    for part, raw in enumerate((mine, other)):
+        tokens = raw[...].astype(F32)
+        hidden[part * rows : (part + 1) * rows, :] = (tokens * rms_scale(tokens) * gain[...]).astype(BF16)
+    h = hidden[...]
+    query[...] = dot(h[:rows], wq[...]).astype(BF16)
+    keys[...] = dot(h, wk[...]).astype(BF16)
+    values[...] = dot(h, wv[...]).astype(BF16)
+
+def project(mine, other, wq, wk, wv, gain):
+    rows, width = mine.shape
+    shape = lambda n: jax.ShapeDtypeStruct((n, width), BF16)
+    return pl.pallas_call(
+        project_kernel,
+        out_shape=[shape(2 * rows), shape(rows), shape(2 * rows), shape(2 * rows)],
+        name="project",
+    )(mine, other, wq, wk, wv, gain)
+
+def dense_kernel(info, near, far, attended, wo, win, wback, gain2, gain3, cot, keep, send, slopes, mixed, steep, rows, active, turned):
+    count, width = near.shape
+    hidden = win.shape[1]
+    for part, raw in enumerate((near, far)):
+        spot = slice(part * count, (part + 1) * count)
+        mixed[spot, :] = raw[...].astype(F32) + dot(attended[spot, :], wo[...])
+    values = mixed[...]
+    inner = (values * rms_scale(values) * gain2[...]).astype(BF16)
+    turned[...] = inner.T
+    total = values
+    for at in range(0, hidden, 512):
+        lifted = jnp.maximum(dot(inner, win[:, at : at + 512]), 0.0).astype(BF16)
+        active[:, at : at + 512] = lifted
+        total = total + dot(lifted, wback[at : at + 512, :])
+    scale = rms_scale(total)
+    place = lax.broadcasted_iota(jnp.int32, (2 * count, 1), 0)
+    place = jnp.where(place < count, place + info[1], place + (info[3] - count))
+    live = jnp.where((place >= info[5]) & (place < info[0]), 1.0, 0.0)
+    pool = jnp.sum(total * scale * gain3[...] * live, axis=0, keepdims=True)
+    slope, grad_end = norm_back(live * cot[...], total, scale, gain3[...])
+    steep[...] = slope
+    rows[...] = jnp.concatenate([pool, grad_end, jnp.zeros((6, width), F32)])
+    low = slope.astype(BF16)
+    for at in range(0, hidden, 512):
+        through = dot(low, wback[at : at + 512, :], NT).astype(BF16)
+        slopes[:, at : at + 512] = jnp.where(active[:, at : at + 512] > 0, through, jnp.zeros_like(through))
+    mine = info[6] & 15
+
+    def backs(to):
+        @pl.loop(0, hidden // 256)
+        def _(pair):
+            made = dot(active[:, pl.ds(pl.multiple_of(pair * 256, 256), 256)], low, TN).astype(BF16)
+            for b in range(2):
+                to[(2 * pair + b) ^ mine] = jnp.concatenate([made[b * 128 : (b + 1) * 128, q * 128 : (q + 1) * 128] for q in range(4)])
+
+    def ins(to):
+        @pl.loop(0, hidden // 256)
+        def _(pair):
+            made = dot(turned[...], slopes[:, pl.ds(pl.multiple_of(pair * 256, 256), 256)]).astype(BF16)
+            for b in range(2):
+                to[(2 * pair + b) ^ mine] = made[:, b * 128 : (b + 1) * 128]
+
+    @pl.when(info[7] == 0)
+    def _():
+        ins(send)
+        backs(keep)
+
+    @pl.when(info[7] == 1)
+    def _():
+        backs(send)
+        ins(keep)
+
+def dense(info, near, far, attended, wo, win, wback, gain2, gain3, cot):
+    count, width = near.shape
+    hidden = win.shape[1]
+    smem, vmem = pl.BlockSpec(memory_space=pltpu.SMEM), pl.BlockSpec(memory_space=pltpu.VMEM)
+    shape = jax.ShapeDtypeStruct
+    return pl.pallas_call(
+        dense_kernel,
+        in_specs=[smem] + [vmem] * 9,
+        out_specs=[vmem] * 6,
+        out_shape=[shape((16, width, 128), BF16), shape((16, width, 128), BF16), shape((2 * count, hidden), BF16),
+                   shape((2 * count, width), F32), shape((2 * count, width), F32), shape((8, width), F32)],
+        scratch_shapes=[pltpu.VMEM((2 * count, hidden), BF16), pltpu.VMEM((width, 2 * count), BF16)],
+        name="dense",
+    )(info, near, far, attended, wo, win, wback, gain2, gain3, cot)
+
+def through_kernel(info, slopes, win, mixed, steep, attended, wo, gain2, grad_mixed, grad_out, grad_attended, rows):
+    width = mixed.shape[1]
+    grad_inner = None
+    for at in range(0, slopes.shape[1], 512):
+        part = dot(slopes[:, at : at + 512], win[:, at : at + 512], NT)
+        grad_inner = part if grad_inner is None else grad_inner + part
+    values = mixed[...]
+    more, grad_two = norm_back(grad_inner, values, rms_scale(values), gain2[...])
+    total = steep[...] + more
+    grad_mixed[...] = total
+    low = total.astype(BF16)
+    grad_attended[...] = dot(low, wo[...], NT).astype(BF16)
+    grad_out[...] = dot(attended[...], low, TN).astype(BF16)
+    rows[...] = jnp.concatenate([grad_two, jnp.zeros((7, width), F32)])
+
+def through(info, slopes, win, mixed, steep, attended, wo, gain2):
+    n, width = mixed.shape
+    smem, vmem = pl.BlockSpec(memory_space=pltpu.SMEM), pl.BlockSpec(memory_space=pltpu.VMEM)
+    shape = jax.ShapeDtypeStruct
+    return pl.pallas_call(
+        through_kernel,
+        in_specs=[smem] + [vmem] * 7,
+        out_specs=[vmem] * 4,
+        out_shape=[shape((n, width), F32), shape((width, width), BF16), shape((n, width), BF16), shape((8, width), F32)],
+        name="through",
+    )(info, slopes, win, mixed, steep, attended, wo, gain2)
+
+def weights_kernel(info, hid_l, hid_r, near, near_other, far, far_other, dq, dk, dv, grad_out, wq, wk, wv, dense_rows, keep, send, stay, leave, rows, made):
+    count, width = near.shape
+    made[0:width, :] = grad_out[...]
+    made[width : 2 * width, :] = (dot(hid_l[:count, :], dq[:count, :], TN) + dot(hid_r[:count, :], dq[count:, :], TN)).astype(BF16)
+    for at, grads in ((2 * width, dk), (3 * width, dv)):
+        made[at : at + width, :] = (dot(hid_l[...], grads[: 2 * count, :], TN) + dot(hid_r[...], grads[2 * count :, :], TN)).astype(BF16)
+    mine = info[6]
+    size = made.shape[0] // 32
+
+    @pl.loop(0, 16)
+    def _(r):
+        keep[r] = made[pl.ds(pl.multiple_of((r ^ mine) * size, size), size), :]
+        send[r] = made[pl.ds(pl.multiple_of(((r + 16) ^ mine) * size, size), size), :]
+
+    gain = jnp.zeros((1, width), F32)
+    for b, raw in enumerate((near, near_other, far, far_other)):
+        spot = slice(b * count, (b + 1) * count)
+        grad = dot(dk[spot, :], wk[...], NT) + dot(dv[spot, :], wv[...], NT)
+        half = slice((b // 2) * count, (b // 2 + 1) * count)
+        if b % 2 == 0:
+            grad = grad + dot(dq[half, :], wq[...], NT)
+            stay[half, :] = grad
+        else:
+            leave[half, :] = grad.astype(BF16)
+        tokens = raw[...].astype(F32)
+        gain = gain + jnp.sum(grad * (tokens * rms_scale(tokens)), axis=0, keepdims=True)
+    leave[2 * count :, :] = two_terms(dense_rows[0:1, :])
+    rows[...] = jnp.concatenate([gain, jnp.zeros((7, width), F32)])
+
+def weights(info, hid_l, hid_r, near, near_other, far, far_other, dq, dk, dv, grad_out, wq, wk, wv, dense_rows):
+    count, width = near.shape
+    smem, vmem = pl.BlockSpec(memory_space=pltpu.SMEM), pl.BlockSpec(memory_space=pltpu.VMEM)
+    shape = jax.ShapeDtypeStruct
+    size = 4 * width // 32
+    return pl.pallas_call(
+        weights_kernel,
+        in_specs=[smem] + [vmem] * 14,
+        out_specs=[vmem] * 5,
+        out_shape=[shape((16, size, width), BF16), shape((16, size, width), BF16), shape((2 * count, width), F32),
+                   shape((2 * count + 16, width), BF16), shape((8, width), F32)],
+        scratch_shapes=[pltpu.VMEM((4 * width, width), BF16)],
+        name="weights",
+    )(info, hid_l, hid_r, near, near_other, far, far_other, dq, dk, dv, grad_out, wq, wk, wv, dense_rows)
+
+def ending_kernel(info, stay, came, near, far, grad_mixed, gain, dense_rows, home, away):
+    count, width = near.shape
+    for part, raw in enumerate((near, far)):
+        spot = slice(part * count, (part + 1) * count)
+        tokens = raw[...].astype(F32)
+        grad = stay[spot, :] + came[spot, :].astype(F32)
+        more, _ = norm_back(grad, tokens, rms_scale(tokens), gain[...])
+        value = (grad_mixed[spot, :] + more).astype(BF16)
+        if part == 0:
+            home[:count, :] = value
+        else:
+            away[:count, :] = value
+    alive = (info[0] - info[5]).astype(F32)
+    pool = two_terms((dense_rows[0:1, :] + one_value(came[2 * count :, :], 1)) / alive)
+    home[count:, :] = pool
+    away[count:, :] = pool
+
+def ending(info, stay, came, near, far, grad_mixed, gain, dense_rows):
+    count, width = near.shape
+    smem, vmem = pl.BlockSpec(memory_space=pltpu.SMEM), pl.BlockSpec(memory_space=pltpu.VMEM)
+    shape = jax.ShapeDtypeStruct((count + 16, width), BF16)
+    return pl.pallas_call(
+        ending_kernel, in_specs=[smem] + [vmem] * 7, out_specs=[vmem] * 2, out_shape=[shape, shape], name="ending"
+    )(info, stay, came, near, far, grad_mixed, gain, dense_rows)
+
+def place_kernel(info, *refs):
+    parts, (back, front) = refs[:8], refs[8:]
+    mine = info[6] & 15
+
+    def backs(half):
+        for i in range(4):
+            for j in range(4):
+                to = (4 * i + j) ^ mine
+                for q in range(4):
+                    back[pl.ds(pl.multiple_of(to * 128, 128), 128), q * 128 : (q + 1) * 128] = half[i][j, q * 128 : (q + 1) * 128, :].astype(F32)
+
+    def ins(half):
+        for i in range(4):
+            for j in range(4):
+                to = (4 * i + j) ^ mine
+                front[:, pl.ds(pl.multiple_of(to * 128, 128), 128)] = half[i][j].astype(F32)
+
+    @pl.when(info[7] == 0)
+    def _():
+        backs(parts[:4])
+        ins(parts[4:])
+
+    @pl.when(info[7] == 1)
+    def _():
+        ins(parts[:4])
+        backs(parts[4:])
+
+def place(info, parts, width):
+    hidden = 16 * 128
+    smem, vmem = pl.BlockSpec(memory_space=pltpu.SMEM), pl.BlockSpec(memory_space=pltpu.VMEM)
+    shape = jax.ShapeDtypeStruct
+    return pl.pallas_call(
+        place_kernel, in_specs=[smem] + [vmem] * 8, out_specs=[vmem] * 2,
+        out_shape=[shape((hidden, width), F32), shape((width, hidden), F32)], name="place",
+    )(info, *parts)
+
+def sort_kernel(info, *refs):
+    parts, made = refs[:8], refs[8:]
+    size, width = parts[0].shape[1:]
+    per = width // size
+    mine = info[6]
+
+    for half in range(2):
+        for top in range(2):
+            @pl.when(((mine >> 4) ^ half) == top)
+            def _(half=half, top=top):
+                for i in range(4):
+                    for j in range(4):
+                        to = ((4 * i + j) ^ mine) & 15
+                        value = parts[4 * half + i][j].astype(F32)
+                        spot = pl.ds(pl.multiple_of((to % per) * size, size), size)
+
+                        @pl.when(to < per)
+                        def _():
+                            made[2 * top][spot, :] = value
+
+                        @pl.when(to >= per)
+                        def _():
+                            made[2 * top + 1][spot, :] = value
+
+def sort(info, parts, width):
+    smem, vmem = pl.BlockSpec(memory_space=pltpu.SMEM), pl.BlockSpec(memory_space=pltpu.VMEM)
+    shape = jax.ShapeDtypeStruct((width, width), F32)
+    return pl.pallas_call(
+        sort_kernel, in_specs=[smem] + [vmem] * 8, out_specs=[vmem] * 4, out_shape=[shape] * 4, name="sort"
+    )(info, *parts)
+
+def exchange(value, bits):
+    size = lax.axis_size("dp") * lax.axis_size("blk")
+    return lax.ppermute(value, ("dp", "blk"), [(i, i ^ bits) for i in range(size)])
+
+def wait(*values):
+    return lax.optimization_barrier(values)
+
+def added(*terms):
+    total = terms[0].astype(F32)
+    for term in terms[1:]:
+        total = total + term.astype(F32)
+    return total.astype(BF16)
 
 def local(inputs, w_query, w_key, w_value, w_out, w_in, w_back, norm1_gain, norm2_gain, final_gain, bias_table, bucket_table, prefix_len, pad_len, pooled_grad):
     rows, width = inputs.shape[1:]
-    place = lax.axis_index("blk")
+    spot, far_off = lax.axis_index("blk"), lax.axis_index("dp")
     length = rows * lax.axis_size("blk")
-    doc, core = place // 2, place % 2
+    doc, core = spot // 2, spot % 2
     block = [doc * 2 + core, doc * 2 + 1 - core, (1 - doc) * 2 + core, (1 - doc) * 2 + 1 - core]
+    line = [8, 16]
+    further = [32 << b for b in range((lax.axis_size("dp") // 8).bit_length() - 1)]
+    piece = core * 16 + doc * 4 + (far_off % 2) * 8 + (far_off // 2) % 4
     near = lax.dynamic_index_in_dim(inputs, doc, 0, keepdims=False)
-    far = exchange(lax.dynamic_index_in_dim(inputs, 1 - doc, 0, keepdims=False), "blk", 2)
-    near_other = exchange(near, "blk", 1)
-    far_other = exchange(far, "blk", 1)
+    far = exchange(lax.dynamic_index_in_dim(inputs, 1 - doc, 0, keepdims=False), ROW)
+    near_other = exchange(near, CORE)
+    far_other = exchange(far, CORE)
     limit = length - lax.dynamic_index_in_dim(pad_len, doc, 0, keepdims=False)
     prefix = lax.dynamic_index_in_dim(prefix_len, doc, 0, keepdims=False)
-    count = (limit - prefix).astype(F32)
-    cotangent = lax.dynamic_index_in_dim(pooled_grad, doc, 0, keepdims=True)
-    info = jnp.stack([limit] + [b * rows for b in block]).astype(jnp.int32)
+    cot = lax.dynamic_index_in_dim(pooled_grad, doc, 0, keepdims=True) / (limit - prefix).astype(F32)
+    slot = jnp.arange(8, dtype=jnp.int32)
+    info = jnp.where(slot == 0, limit, 0)
+    for i, value in enumerate([b * rows for b in block] + [prefix, piece, core]):
+        info = jnp.where(slot == i + 1, value, info)
     picker = (jnp.arange(BUCKETS, dtype=jnp.int32)[:, None] == bucket_table[None, :]).astype(F32)
     picker = jnp.pad(picker, ((0, 0), (0, 1)))
     table = lax.dot_general(bias_table, picker, TN, precision=lax.Precision.HIGHEST)
     table = table.reshape(-1, 2, picker.shape[1])
 
-    def front(raw, own):
-        tokens = raw.astype(F32)
-        scale = rms_scale(tokens)
-        hidden = (tokens * scale * norm1_gain).astype(BF16)
-        return hidden, mm(hidden[:own], w_query).astype(BF16), mm(hidden, w_key).astype(BF16), mm(hidden, w_value).astype(BF16)
-
-    hid_l, q_l, k_l, v_l = front(jnp.concatenate([near, near_other]), rows)
-    hid_r, q_r, k_r, v_r = front(jnp.concatenate([far, far_other]), rows)
+    gain1, gain2, gain3 = norm1_gain[None, :], norm2_gain[None, :], final_gain[None, :]
+    hid_l, q_l, k_l, v_l = project(near, near_other, w_query, w_key, w_value, gain1)
+    hid_r, q_r, k_r, v_r = project(far, far_other, w_query, w_key, w_value, gain1)
     attended, expo, inverse = attention(info, q_l, q_r, k_l, k_r, v_l, v_r, table)
-
-    raw = jnp.concatenate([near, far])
-    tokens = raw.astype(F32)
-    mixed = tokens + mm(attended, w_out)
-    scale_two = rms_scale(mixed)
-    inner = (mixed * scale_two * norm2_gain).astype(BF16)
-    lifted = mm(inner, w_in)
-    active = jnp.maximum(lifted, 0.0).astype(BF16)
-    result = mixed + mm(active, w_back)
-    scale_end = rms_scale(result)
-    spots = jnp.concatenate([block[0] * rows + jnp.arange(rows), block[2] * rows + jnp.arange(rows)])
-    live = ((spots >= prefix) & (spots < limit)).astype(F32)[:, None]
-    pool_part = jnp.sum(result * scale_end * final_gain * live, axis=0, keepdims=True)
-    pool_mine = (pool_part + exchange(pool_part, "blk", 1)) / count
-    pool_other = exchange(pool_mine, "blk", 2)
+    keep, send, slopes, mixed, steep, dense_rows = dense(info, near, far, attended, w_out, w_in, w_back, gain2, gain3, cot)
+
+    xy = [ROW, NEAR_X, ROW ^ NEAR_X]
+    zz = [line[0], line[1], line[0] ^ line[1]]
+
+    token, send = wait(info, send)
+    got = exchange(send, CORE)
+    grad_mixed, grad_out_w, grad_attended, through_rows = through(token, slopes, w_in, mixed, steep, attended, w_out, gain2)
+    token, through_rows, got = wait(token, through_rows, got)
+
+    sends = [added(keep[4 * k : 4 * k + 4], got[4 * k : 4 * k + 4]) for k in (1, 2, 3)]
+    token, sends = wait(token, sends)
+    came = [exchange(s, m) for s, m in zip(sends, xy)]
+    dq, dk, dv, offsets = attention_grads(token, q_l, q_r, k_l, k_r, v_l, v_r, grad_attended, attended, inverse, expo)
+    rest_keep, rest_send, stay, leave, first_rows = weights(
+        token, hid_l, hid_r, near, near_other, far, far_other, dq, dk, dv, grad_out_w, w_query, w_key, w_value, dense_rows)
+    grad_bias = lax.dot_general(picker, offsets.reshape(-1, picker.shape[1]), NT, precision=lax.Precision.HIGHEST)
+    grad_bias = jnp.pad(grad_bias.reshape(1, -1), ((0, 0), (0, width - grad_bias.size)))
+    small = jnp.concatenate([first_rows[:1], through_rows[:1], dense_rows[1:2], grad_bias])
+    token, first_rows, came = wait(token, first_rows, came)
+
+    lines = [added(keep[k], got[k], *[c[k] for c in came]) for k in range(4)]
+    first = jnp.concatenate([rest_send.reshape(-1, width), two_terms(small)])
+    token, lines, leave, first = wait(token, lines, leave, first)
+    took = [exchange(lines[k + 1], m) for k, m in enumerate(zz)]
+    rest_got = exchange(first, CORE)
+    hidden_got = exchange(leave, CORE)
+    token, took, rest_got, hidden_got = wait(token, took, rest_got, hidden_got)
+    whole = added(lines[0], *took)
+    for bit in further:
+        whole = added(whole, exchange(whole, bit))
+
+    count = rest_keep.shape[0] * rest_keep.shape[1]
+    small = small + one_value(rest_got[count:], 4)
+    rest_got = rest_got[:count].reshape(rest_keep.shape)
+    terms = two_terms(small)
+    sends = [jnp.concatenate([added(rest_keep[4 * k : 4 * k + 4], rest_got[4 * k : 4 * k + 4]).reshape(-1, width), terms]) for k in (1, 2, 3)]
+    token, whole, sends = wait(token, whole, sends)
+    back_line = [exchange(whole, m) for m in zz]
+    rest_came = [exchange(s, m) for s, m in zip(sends, xy)]
+    home, away = ending(token, stay, hidden_got, near, far, grad_mixed, gain1, dense_rows)
+    token, back_line, rest_came, away = wait(token, back_line, rest_came, away)
+
+    quarter = jnp.stack([whole] + back_line)
+    count = count // 4
+    for part in rest_came:
+        small = small + one_value(part[count:], 4)
+    rest_came = [part[:count].reshape((4,) + rest_keep.shape[1:]) for part in rest_came]
+    terms = two_terms(small)
+    lines = [added(rest_keep[k], rest_got[k], *[c[k] for c in rest_came]) for k in range(4)]
+    sends = [jnp.concatenate([lines[k], terms]) for k in (1, 2, 3)]
+    token, quarter, sends, away = wait(token, quarter, sends, away)
+    quarters = [exchange(quarter, m) for m in xy]
+    took = [exchange(s, m) for s, m in zip(sends, zz)]
+    away_got = exchange(away, ROW)
+    token, took = wait(token, took)
+    count = count // 4
+    for part in took:
+        small = small + one_value(part[count:], 4)
+    rest = added(lines[0], *[part[:count] for part in took])
+    for bit in further:
+        rest = added(rest, exchange(rest, bit))
+        small = small + exchange(small, bit)
+    token, rest = wait(token, rest)
+    back_line = [exchange(rest, m) for m in zz]
+    token, back_line = wait(token, back_line)
+    rest_quarter = jnp.stack([rest] + back_line)
+
+    token, rest_quarter = wait(token, rest_quarter)
+    rest_quarters = [exchange(rest_quarter, m) for m in xy]
+    token, quarters, away_got = wait(token, quarters, away_got)
+    mine = [quarter] + quarters
+    others = [exchange(value, CORE) for value in mine]
+    token, others = wait(token, others)
+    out_back, out_in = place(token, mine + others, width)
+    token, out_back, rest_quarters = wait(token, out_back, rest_quarters)
+    mine = [rest_quarter] + rest_quarters
+    others = [exchange(value, CORE) for value in mine]
+    out_out, out_query, out_key, out_value = sort(info, mine + others, width)
+
+    pool_mine, pool_other = one_value(home[rows:], 1), one_value(away_got[rows:], 1)
     pooled = jnp.where(doc == 0, jnp.concatenate([pool_mine, pool_other]), jnp.concatenate([pool_other, pool_mine]))
-
-    grad_final = live * (cotangent / count)
-    grad_result, grad_end = norm_back(grad_final, result, scale_end, final_gain)
-    grad_branch = grad_result.astype(BF16)
-    grad_back_w = mm(active, grad_branch, TN)
-    grad_lifted = jnp.where(active > 0, mm(grad_branch, w_back, NT).astype(BF16), jnp.zeros_like(active))
-    grad_in_t = mm(grad_lifted, inner, TN)
-    big = reduce_all(jnp.concatenate([grad_back_w.astype(BF16), grad_in_t.astype(BF16)]), (768, 768, 512))
-    grad_inner = mm(grad_lifted, w_in, NT)
-    grad_through, grad_two = norm_back(grad_inner, mixed, scale_two, norm2_gain)
-    grad_mixed = grad_result + grad_through
-    grad_att_out = grad_mixed.astype(BF16)
-    grad_out_w = mm(attended, grad_att_out, TN)
-    grad_attended = mm(grad_att_out, w_out, NT).astype(BF16)
-    dq, dk, dv, offsets = attention_grads(info, q_l, q_r, k_l, k_r, v_l, v_r, grad_attended, attended, inverse, expo)
-    grad_bias = lax.dot_general(picker, offsets.reshape(-1, picker.shape[1]), NT, precision=lax.Precision.HIGHEST)
-    own = jnp.concatenate([hid_l[:rows], hid_r[:rows]])
-    everyone = jnp.concatenate([hid_l, hid_r])
-    grad_q_w = mm(own, dq, TN)
-    grad_k_w = mm(everyone, dk, TN)
-    grad_v_w = mm(everyone, dv, TN)
-    rest = reduce_all(jnp.concatenate([g.astype(BF16) for g in (grad_out_w, grad_q_w, grad_k_w, grad_v_w)]), (384, 384, 256))
-    through_kv = mm(dk, w_key, NT) + mm(dv, w_value, NT)
-    through_kv = through_kv.reshape(2, 2, rows, width)
-    sent = exchange(through_kv[:, 1].reshape(2 * rows, width).astype(BF16), "blk", 1).astype(F32)
-    grad_hidden = mm(dq, w_query, NT) + through_kv[:, 0].reshape(2 * rows, width) + sent
-    grad_norm, grad_one = norm_back(grad_hidden, tokens, rms_scale(tokens), norm1_gain)
-    input_grad = (grad_mixed + grad_norm).astype(BF16)
-    away = exchange(input_grad[rows:], "blk", 2)
-    home = input_grad[:rows]
-    input_grad = jnp.where(doc == 0, jnp.stack([home, away]), jnp.stack([away, home]))
-    small = jnp.concatenate([jnp.stack([grad_one, grad_two, grad_end]), jnp.pad(grad_bias.reshape(1, -1), ((0, 0), (0, width - grad_bias.size)))])
-    small = reduce_small(small)
-    split = w_in.shape[1]
-    grads = [rest[i * width : (i + 1) * width].astype(F32) for i in range(4)]
+    home, away_got = home[:rows], away_got[:rows]
+    input_grad = jnp.where(doc == 0, jnp.stack([home, away_got]), jnp.stack([away_got, home]))
     return (
         pooled,
         input_grad,
-        grads[1],
-        grads[2],
-        grads[3],
-        grads[0],
-        big[split:].astype(F32).T,
-        big[:split].astype(F32),
+        out_query,
+        out_key,
+        out_value,
+        out_out,
+        out_in,
+        out_back,
         small[0],
         small[1],
         small[2],
-        small[3, : grad_bias.size].reshape(grad_bias.shape),
+        small[3, : bias_table.size].reshape(bias_table.shape),
     )
 
 def solution(mesh):

time: 313 us -> 207 us (0.66); the launches traced: 308 us -> 206 us
  waiting for transfers between devices: 117 us -> 39.3 us
  Pallas kernels: 33.2 us -> 82.6 us
  matrix products: 35.1 us -> 0.38 us
  starting transfers between devices: 60.6 us -> 42.6 us
  other arithmetic: 33.4 us -> 17.4 us
  local copies, waits for them, and re-layouts: 24.4 us -> 21 us
    ppermute x64 -> x39, waiting for transfers between devices: 117 us -> 39.3 us  [exchange(): lax.ppermute(value, ('dp', 'blk'), [(i, i ^ bits) for i in range(size)])]
    pallas_call x0 -> x8, Pallas kernels: none -> 49.9 us  [the longest x1 15.9 us: dense(): pl.pallas_call(dense_kernel, in_specs=[smem] + [vmem] * 9, out_specs=[vme...]
    dot_general x21 -> x0, matrix products: 34.7 us -> none  [mm(): return lax.dot_general(a, b, dims, preferred_element_type=F32)]
    ppermute x64 -> x39, starting transfers between devices: 60.6 us -> 42.6 us  [exchange(): lax.ppermute(value, ('dp', 'blk'), [(i, i ^ bits) for i in range(size)])]
    unnamed x95 -> x73, local copies, waits for them, and re-layouts: 15.6 us -> 5.58 us
    concatenate x5 -> x0, other arithmetic: 7.08 us -> none  [the longest x1 4.32 us: local(): jnp.concatenate([grad_back_w.astype(BF16), grad_in_t.astype(BF16)])]
    convert_element_type x31 -> x11, other arithmetic: 15.3 us -> 8.62 us  [the longest x7 8.54 us: added(): return total.astype(BF16)]
    concatenate x0 -> x7, local copies, waits for them, and re-layouts: none -> 6.22 us  [the longest x1 3.84 us: local(): first = jnp.concatenate([rest_send.reshape(-1, width), two_terms(small)])]
  transfers between devices with their start and end apart: 64 -> 39, of which waited for: 39 -> 9; matrix products, arithmetic and copies ran while one was open for 13% -> 11% of each run, Pallas kernels for 0% -> 23%
where the time goes in v2:
time: 207 us; the launch traced here: 206 us
  Pallas kernels  82.6 us (40%)
  starting transfers between devices  42.6 us (21%)
  waiting for transfers between devices  39.3 us (19%)
  local copies, waits for them, and re-layouts  21 us (10%)
  other arithmetic  17.4 us (8%)
  between operations  2.53 us (1%)
    ppermute x39, starting transfers between devices, exchange(): lax.ppermute(value, ('dp', 'blk'), [(i, i ^ bits) for i in range(size)])  42.6 us
    ppermute x39, waiting for transfers between devices, exchange(): lax.ppermute(value, ('dp', 'blk'), [(i, i ^ bits) for i in range(size)])  39.3 us
    pallas_call x1, Pallas kernels, attention_grads(): pl.pallas_call(bwd_kernel, grid=(pairs,), in_specs=[pl.BlockSpec(memory_s...  20 us
    pallas_call x1, Pallas kernels, dense(): pl.pallas_call(dense_kernel, in_specs=[smem] + [vmem] * 9, out_specs=[vme...  15.9 us
    pallas_call x1, Pallas kernels, attention(): pl.pallas_call(fwd_kernel, grid=(pairs,), in_specs=[pl.BlockSpec(memory_s...  12.7 us
    convert_element_type x7, other arithmetic, added(): return total.astype(BF16)  8.54 us
    pallas_call x1, Pallas kernels, weights(): pl.pallas_call(weights_kernel, in_specs=[smem] + [vmem] * 14, out_specs=[...  7.18 us
    pallas_call x2, Pallas kernels, project(): pl.pallas_call(project_kernel, out_shape=[shape(2 * rows), shape(rows), s...  6.56 us
  transfers between devices with their start and end apart: 39, of which 9 were waited for; matrix products, arithmetic and copies ran while one was open for 11% of the time, Pallas kernels for 23%

profile of v2, /device:TPU:0, one launch (start us, length us, event | category | flops | bytes accessed | tf_op | source)
XLA Modules:
  0.0 205.9 jit_solution(5715745649655610708)
XLA Ops:
  1.8 3.0 %collective-permute-start = (bf16[256,512]{1,0:T(8,128)(2,1)S(1)}, bf16[256,512]{1,0:T(8,128)(2,1)S(1)}, u32[]{:S(2)}, u32[]{:S(2)}) collective-permute-start(bf16[256,512]{1,0:T(8,128)(2,1)S(1)} %get-tuple-element.274), channel_id=1, source_target_pairs={{0,2},{1,3},{2,0},{3,1},{4,6},{5,7},{6,4},{7,5},{8,10},{9,11},{10,... | collective-permute-start | bytes 786440 | tf_op jit(solution)/shard_map/ppermute | solution.py:433
  5.5 5.6 %collective-permute-done.mine.far = bf16[256,512]{1,0:T(8,128)(2,1)S(1)} collective-permute-done((bf16[256,512]{1,0:T(8,128)(2,1)S(1)}, bf16[256,512]{1,0:T(8,128)(2,1)S(1)}, u32[]{:S(2)}, u32[]{:S(2)}) %collective-permute-start) | collective-permute-done | bytes 262176 | tf_op jit(solution)/shard_map/ppermute | solution.py:433
  18.9 3.3 %project.2 = (bf16[512,512]{1,0:T(8,128)(2,1)}, bf16[256,512]{1,0:T(8,128)(2,1)}, bf16[512,512]{1,0:T(8,128)(2,1)}, bf16[512,512]{1,0:T(8,128)(2,1)}) custom-call(bf16[256,512]{1,0:T(8,128)(2,1)} %copy-done.2, bf16[256,512]{1,0:T(8,128)(2,1)} %copy-done.6, bf16[512,512]{1,0:T(8,128)(2,1)} %wq.5, bf16[512,512]{1,0:T(8,128)(2,1)} %wk.5, bf16[512,512]{1,0:T(8,128)(2,1)} %wv.5, ...), custom_call_target="tpu_custom_call" | custom-call | tf_op jit(solution)/shard_map/project/pallas_call | solution.py:195
  23.0 3.3 %project.3 = (bf16[512,512]{1,0:T(8,128)(2,1)}, bf16[256,512]{1,0:T(8,128)(2,1)}, bf16[512,512]{1,0:T(8,128)(2,1)}, bf16[512,512]{1,0:T(8,128)(2,1)}) custom-call(bf16[256,512]{1,0:T(8,128)(2,1)} %copy-done.3, bf16[256,512]{1,0:T(8,128)(2,1)} %copy-done.7, bf16[512,512]{1,0:T(8,128)(2,1)} %wq.5, bf16[512,512]{1,0:T(8,128)(2,1)} %wk.5, bf16[512,512]{1,0:T(8,128)(2,1)} %wv.5, ...), custom_call_target="tpu_custom_call" | custom-call | tf_op jit(solution)/shard_map/project/pallas_call | solution.py:195
  26.2 12.7 %attn_fwd.1 = (bf16[512,512]{1,0:T(8,128)(2,1)}, bf16[8,512,1024]{2,1,0:T(8,128)(2,1)}, f32[512,512]{1,0:T(8,128)}) custom-call(s32[8]{0:T(128)} %compare_select_fusion.7.info, bf16[256,512]{1,0:T(8,128)(2,1)} %get-tuple-element.121.ql, bf16[256,512]{1,0:T(8,128)(2,1)} %get-tuple-element.122.qr, bf16[512,512]{1,0:T(8,128)(2,1)} %get-tuple-element.123.kl, ...), custom_call_target="tpu_custom_call" | custom-call | tf_op jit(solution)/shard_map/attn_fwd/pallas_call | solution.py:73
  38.9 15.9 %dense.1 = (bf16[16,512,128]{2,1,0:T(8,128)(2,1)}, bf16[16,512,128]{2,1,0:T(8,128)(2,1)}, bf16[512,2048]{1,0:T(8,128)(2,1)}, f32[512,512]{1,0:T(8,128)}, f32[512,512]{1,0:T(8,128)}, /*index=5*/f32[8,512]{1,0:T(8,128)}) custom-call(s32[8]{0:T(128)} %compare_select_fusion.7.info, bf16[256,512]{1,0:T(8,128)(2,1)} %copy-done.2, bf16[256,512]{1,0:T(8,128)(2,1)} %copy-done.3, ...), custom_call_target="tpu_custom_call" | custom-call | tf_op jit(solution)/shard_map/dense/pallas_call | solution.py:258
  55.4 6.4 %through.1 = (f32[512,512]{1,0:T(8,128)}, bf16[512,512]{1,0:T(8,128)(2,1)}, bf16[512,512]{1,0:T(8,128)(2,1)}, f32[8,512]{1,0:T(8,128)}) custom-call(s32[8]{0:T(128)} %compare_select_fusion.7.info, bf16[512,2048]{1,0:T(8,128)(2,1)} %get-tuple-element.130.slopes, bf16[512,2048]{1,0:T(8,128)(2,1)} %win.3, f32[512,512]{1,0:T(8,128)} %get-tuple-element.131.mixed, ...), custom_call_target="tpu_custom_call" | custom-call | tf_op jit(solution)/shard_map/through/pallas_call | solution.py:287
  61.8 2.9 %add_convert_fusion = (bf16[4,512,128]{2,1,0:T(8,128)(2,1)}, bf16[4,512,128]{2,1,0:T(8,128)(2,1)}, bf16[4,512,128]{2,1,0:T(8,128)(2,1)}) fusion(bf16[16,512,128]{2,1,0:T(8,128)(2,1)} %collective-permute-done.3, bf16[16,512,128]{2,1,0:T(8,128)(2,1)S(1)} %copy-done.5), kind=kLoop, calls=%fused_computation.1 | loop fusion | flops 3145728 | bytes 4718592 | tf_op jit(solution)/shard_map/convert_element_type | solution.py:442
  69.6 20.0 %attn_bwd.1 = (bf16[512,512]{1,0:T(8,128)(2,1)}, bf16[1024,512]{1,0:T(8,128)(2,1)}, bf16[1024,512]{1,0:T(8,128)(2,1)}, f32[4,2,2048]{2,1,0:T(2,128)}) custom-call(s32[8]{0:T(128)} %compare_select_fusion.7.info, bf16[256,512]{1,0:T(8,128)(2,1)} %get-tuple-element.121.ql, bf16[256,512]{1,0:T(8,128)(2,1)} %get-tuple-element.122.qr, ...), custom_call_target="tpu_custom_call" | custom-call | tf_op jit(solution)/shard_map/attn_bwd/pallas_call | solution.py:148
  89.6 7.2 %weights.1 = (bf16[16,64,512]{2,1,0:T(8,128)(2,1)}, bf16[16,64,512]{2,1,0:T(8,128)(2,1)}, f32[512,512]{1,0:T(8,128)}, bf16[528,512]{1,0:T(8,128)(2,1)}, f32[8,512]{1,0:T(8,128)}) custom-call(s32[8]{0:T(128)} %compare_select_fusion.7.info, bf16[512,512]{1,0:T(8,128)(2,1)} %get-tuple-element.139.hid_l, bf16[512,512]{1,0:T(8,128)(2,1)} %get-tuple-element.140.hid_r, ...), custom_call_target="tpu_custom_call" | custom-call | tf_op jit(solution)/shard_map/weights/pallas_call | solution.py:329
  97.9 3.8 %concatenate.39 = bf16[1040,512]{1,0:T(8,128)(2,1)S(1)} concatenate(bf16[1024,512]{1,0:T(8,128)(2,1)} %bitcast.61, bf16[4,512]{1,0:T(4,128)(2,1)S(1)} %fusion.29, bf16[4,512]{1,0:T(4,128)(2,1)S(1)} %broadcast.45, bf16[4,512]{1,0:T(4,128)(2,1)S(1)} %subtract_convert_fusion.2, bf16[4,512]{1,0:T(4,128)(2,1)S(1)} %broadcast.45), dimensions={0} | concatenate | bytes 2129920 | tf_op jit(solution)/shard_map/concatenate | solution.py:495
  103.1 1.8 fusion.9
  105.5 1.8 collective-permute-start.7
  107.3 2.6 %collective-permute-start.8 = (bf16[512,128]{1,0:T(8,128)(2,1)S(1)}, bf16[512,128]{1,0:T(8,128)(2,1)S(1)}, u32[]{:S(2)}, u32[]{:S(2)}) collective-permute-start(bf16[512,128]{1,0:T(8,128)(2,1)S(1)} %get-tuple-element.163), channel_id=1, source_target_pairs={{0,16},{1,17},{2,18},{3,19},{4,20},{5,21},{6,22},{7,23},{8,24},{9,... | collective-permute-start | bytes 393224 | tf_op jit(solution)/shard_map/ppermute | solution.py:433
  109.9 3.0 %collective-permute-done.7 = bf16[512,128]{1,0:T(8,128)(2,1)S(1)} collective-permute-done((bf16[512,128]{1,0:T(8,128)(2,1)S(1)}, bf16[512,128]{1,0:T(8,128)(2,1)S(1)}, u32[]{:S(2)}, u32[]{:S(2)}) %collective-permute-start.7) | collective-permute-done | bytes 131104 | tf_op jit(solution)/shard_map/ppermute | solution.py:433
  112.8 7.3 %collective-permute-done.8 = bf16[512,128]{1,0:T(8,128)(2,1)S(1)} collective-permute-done((bf16[512,128]{1,0:T(8,128)(2,1)S(1)}, bf16[512,128]{1,0:T(8,128)(2,1)S(1)}, u32[]{:S(2)}, u32[]{:S(2)}) %collective-permute-start.8) | collective-permute-done | bytes 131104 | tf_op jit(solution)/shard_map/ppermute | solution.py:433
  125.7 2.4 %collective-permute-start.14 = (bf16[512,128]{1,0:T(8,128)(2,1)S(1)}, bf16[512,128]{1,0:T(8,128)(2,1)S(1)}, u32[]{:S(2)}, u32[]{:S(2)}) collective-permute-start(bf16[512,128]{1,0:T(8,128)(2,1)S(1)} %add_convert_fusion.7), channel_id=1, source_target_pairs={{0,24},{1,25},{2,26},{3,27},{4,28},{5,29},{6,30},{7,31},{8,16},{9,... | collective-permute-start | bytes 393224 | tf_op jit(solution)/shard_map/ppermute | solution.py:433
  129.3 3.8 %collective-permute-done.14 = bf16[512,128]{1,0:T(8,128)(2,1)S(1)} collective-permute-done((bf16[512,128]{1,0:T(8,128)(2,1)S(1)}, bf16[512,128]{1,0:T(8,128)(2,1)S(1)}, u32[]{:S(2)}, u32[]{:S(2)}) %collective-permute-start.14) | collective-permute-done | bytes 131104 | tf_op jit(solution)/shard_map/ppermute | solution.py:433
  133.2 4.3 %collective-permute-start.12 = (bf16[512,128]{1,0:T(8,128)(2,1)S(1)}, bf16[512,128]{1,0:T(8,128)(2,1)S(1)}, u32[]{:S(2)}, u32[]{:S(2)}) collective-permute-start(bf16[512,128]{1,0:T(8,128)(2,1)S(1)} %add_convert_fusion.7), channel_id=1, source_target_pairs={{0,8},{1,9},{2,10},{3,11},{4,12},{5,13},{6,14},{7,15},{8,0},{9,1},... | collective-permute-start | bytes 393224 | tf_op jit(solution)/shard_map/ppermute | solution.py:433
  137.5 3.2 %ending.1 = (bf16[272,512]{1,0:T(8,128)(2,1)}, bf16[272,512]{1,0:T(8,128)(2,1)}) custom-call(s32[8]{0:T(128)} %compare_select_fusion.7.info, f32[512,512]{1,0:T(8,128)} %get-tuple-element.175.stay, bf16[528,512]{1,0:T(8,128)(2,1)} %copy-done.10, bf16[256,512]{1,0:T(8,128)(2,1)} %copy-done.2, bf16[256,512]{1,0:T(8,128)(2,1)} %copy-done.3, ...), custom_call_target="tpu_custom_call" | custom-call | tf_op jit(solution)/shard_map/ending/pallas_call | solution.py:360
  142.1 1.9 concatenate.44
  145.0 1.8 collective-permute-start.18
  149.5 2.5 %collective-permute-start.26 = (bf16[4,512,128]{2,1,0:T(8,128)(2,1)S(1)}, bf16[4,512,128]{2,1,0:T(8,128)(2,1)S(1)}, u32[]{:S(2)}, u32[]{:S(2)}) collective-permute-start(bf16[4,512,128]{2,1,0:T(8,128)(2,1)S(1)} %pad_maximum_fusion.refs_0_), channel_id=1, source_target_pairs={{0,6},{1,7},{2,4},{3,5},{4,2},{5,3},{6,0},{7,1},{8,14},{9,15},{10,... | collective-permute-start | bytes 1572872 | tf_op jit(solution)/shard_map/ppermute | solution.py:433
  153.0 1.9 collective-permute-done.19
  155.9 2.4 %collective-permute-start.23 = (bf16[64,512]{1,0:T(8,128)(2,1)S(1)}, bf16[64,512]{1,0:T(8,128)(2,1)S(1)}, u32[]{:S(2)}, u32[]{:S(2)}) collective-permute-start(bf16[64,512]{1,0:T(8,128)(2,1)S(1)} %add_convert_fusion.8), channel_id=1, source_target_pairs={{0,24},{1,25},{2,26},{3,27},{4,28},{5,29},{6,30},{7,31},{8,16},{9,... | collective-permute-start | bytes 196616 | tf_op jit(solution)/shard_map/ppermute | solution.py:433
  159.5 2.6 %collective-permute-done.23 = bf16[64,512]{1,0:T(8,128)(2,1)S(1)} collective-permute-done((bf16[64,512]{1,0:T(8,128)(2,1)S(1)}, bf16[64,512]{1,0:T(8,128)(2,1)S(1)}, u32[]{:S(2)}, u32[]{:S(2)}) %collective-permute-start.23) | collective-permute-done | bytes 65568 | tf_op jit(solution)/shard_map/ppermute | solution.py:433
  165.9 2.0 collective-permute-done.21
  168.8 10.4 %collective-permute-done.27 = bf16[272,512]{1,0:T(8,128)(2,1)S(1)} collective-permute-done((bf16[272,512]{1,0:T(8,128)(2,1)}, bf16[272,512]{1,0:T(8,128)(2,1)S(1)}, u32[]{:S(2)}, u32[]{:S(2)}) %collective-permute-start.27) | collective-permute-done | bytes 278560 | tf_op jit(solution)/shard_map/ppermute | solution.py:433
  182.1 2.5 %collective-permute-start.34 = (bf16[4,64,512]{2,1,0:T(8,128)(2,1)S(1)}, bf16[4,64,512]{2,1,0:T(8,128)(2,1)S(1)}, u32[]{:S(2)}, u32[]{:S(2)}) collective-permute-start(bf16[4,64,512]{2,1,0:T(8,128)(2,1)S(1)} %pad_maximum_fusion.1.refs_0_), channel_id=1, source_target_pairs={{0,6},{1,7},{2,4},{3,5},{4,2},{5,3},{6,0},{7,1},{8,14},{9,15},{10,... | collective-permute-start | bytes 786440 | tf_op jit(solution)/shard_map/ppermute | solution.py:433
  188.3 6.5 %place.1 = (f32[2048,512]{1,0:T(8,128)}, f32[512,2048]{1,0:T(8,128)}) custom-call(s32[8]{0:T(128)} %compare_select_fusion.7.info, bf16[4,512,128]{2,1,0:T(8,128)(2,1)} %copy-done.4, bf16[4,512,128]{2,1,0:T(8,128)(2,1)} %copy-done.13, bf16[4,512,128]{2,1,0:T(8,128)(2,1)} %copy-done.12, bf16[4,512,128]{2,1,0:T(8,128)(2,1)} %copy-done.11, ...), custom_call_target="tpu_custom_call" | custom-call | tf_op jit(solution)/shard_map/place/pallas_call | solution.py:395
  194.9 2.6 %collective-permute-done.33.refs_2_ = bf16[4,64,512]{2,1,0:T(8,128)(2,1)} collective-permute-done((bf16[4,64,512]{2,1,0:T(8,128)(2,1)S(1)}, bf16[4,64,512]{2,1,0:T(8,128)(2,1)}, u32[]{:S(2)}, u32[]{:S(2)}) %collective-permute-start.33) | collective-permute-done | bytes 262176 | tf_op jit(solution)/shard_map/ppermute | solution.py:433
  201.8 4.1 %sort.1 = (f32[512,512]{1,0:T(8,128)}, f32[512,512]{1,0:T(8,128)}, f32[512,512]{1,0:T(8,128)}, f32[512,512]{1,0:T(8,128)}) custom-call(s32[8]{0:T(128)} %compare_select_fusion.7.info, bf16[4,64,512]{2,1,0:T(8,128)(2,1)} %copy-done.8, bf16[4,64,512]{2,1,0:T(8,128)(2,1)} %collective-permute-done.32.refs_1_, ...), custom_call_target="tpu_custom_call" | custom-call | tf_op jit(solution)/shard_map/sort/pallas_call | solution.py:427
  (175 shorter events, 47.8 us)
Async XLA Ops:
  1.8 9.3 %collective-permute-start = (bf16[256,512]{1,0:T(8,128)(2,1)S(1)}, bf16[256,512]{1,0:T(8,128)(2,1)S(1)}, u32[]{:S(2)}, u32[]{:S(2)}) collective-permute-start(bf16[256,512]{1,0:T(8,128)(2,1)S(1)} %get-tuple-element.274), channel_id=1, source_target_pairs={{0,2},{1,3},{2,0},{3,1},{4,6},{5,7},{6,4},{7,5},{8,10},{9,11},{10,... | collective-permute-start | bytes 786440 | tf_op jit(solution)/shard_map/ppermute | solution.py:433
  4.8 13.4 %collective-permute-start.1 = (bf16[256,512]{1,0:T(8,128)(2,1)S(1)}, bf16[256,512]{1,0:T(8,128)(2,1)S(1)}, u32[]{:S(2)}, u32[]{:S(2)}) collective-permute-start(bf16[256,512]{1,0:T(8,128)(2,1)S(1)} %get-tuple-element.275.mine.near), channel_id=1, source_target_pairs={{0,1},{1,0},{2,3},{3,2},{4,5},{5,4},{6,7},{7,6},{8,9},{9,8},{10,11... | collective-permute-start | bytes 786440 | tf_op jit(solution)/shard_map/ppermute | solution.py:433
  11.1 11.1 %collective-permute-start.2 = (bf16[256,512]{1,0:T(8,128)(2,1)S(1)}, bf16[256,512]{1,0:T(8,128)(2,1)S(1)}, u32[]{:S(2)}, u32[]{:S(2)}) collective-permute-start(bf16[256,512]{1,0:T(8,128)(2,1)S(1)} %collective-permute-done.mine.far), channel_id=1, source_target_pairs={{0,1},{1,0},{2,3},{3,2},{4,5},{5,4},{6,7},{7,6},{8,9},{9,8},{10,11... | collective-permute-start | bytes 786440 | tf_op jit(solution)/shard_map/ppermute | solution.py:433
  54.9 6.9 %collective-permute-start.3 = (bf16[16,512,128]{2,1,0:T(8,128)(2,1)}, bf16[16,512,128]{2,1,0:T(8,128)(2,1)}, u32[]{:S(2)}, u32[]{:S(2)}) collective-permute-start(bf16[16,512,128]{2,1,0:T(8,128)(2,1)} %get-tuple-element.134), channel_id=1, source_target_pairs={{0,1},{1,0},{2,3},{3,2},{4,5},{5,4},{6,7},{7,6},{8,9},{9,8},{10,11... | collective-permute-start | bytes 6291464 | tf_op jit(solution)/shard_map/ppermute | solution.py:433
  64.7 37.1 %collective-permute-start.4 = (bf16[4,512,128]{2,1,0:T(8,128)(2,1)}, bf16[4,512,128]{2,1,0:T(8,128)(2,1)}, u32[]{:S(2)}, u32[]{:S(2)}) collective-permute-start(bf16[4,512,128]{2,1,0:T(8,128)(2,1)} %get-tuple-element.150), channel_id=1, source_target_pairs={{0,2},{1,3},{2,0},{3,1},{4,6},{5,7},{6,4},{7,5},{8,10},{9,11},{10,... | collective-permute-start | bytes 1572872 | tf_op jit(solution)/shard_map/ppermute | solution.py:433
  66.4 35.4 %collective-permute-start.5 = (bf16[4,512,128]{2,1,0:T(8,128)(2,1)}, bf16[4,512,128]{2,1,0:T(8,128)(2,1)}, u32[]{:S(2)}, u32[]{:S(2)}) collective-permute-start(bf16[4,512,128]{2,1,0:T(8,128)(2,1)} %get-tuple-element.151), channel_id=1, source_target_pairs={{0,4},{1,5},{2,6},{3,7},{4,0},{5,1},{6,2},{7,3},{8,12},{9,13},{10,... | collective-permute-start | bytes 1572872 | tf_op jit(solution)/shard_map/ppermute | solution.py:433
  67.9 33.9 %collective-permute-start.6 = (bf16[4,512,128]{2,1,0:T(8,128)(2,1)}, bf16[4,512,128]{2,1,0:T(8,128)(2,1)}, u32[]{:S(2)}, u32[]{:S(2)}) collective-permute-start(bf16[4,512,128]{2,1,0:T(8,128)(2,1)} %get-tuple-element.152), channel_id=1, source_target_pairs={{0,6},{1,7},{2,4},{3,5},{4,2},{5,3},{6,0},{7,1},{8,14},{9,15},{10,... | collective-permute-start | bytes 1572872 | tf_op jit(solution)/shard_map/ppermute | solution.py:433
  104.9 15.3 %collective-permute-start.10 = (bf16[1040,512]{1,0:T(8,128)(2,1)S(1)}, bf16[1040,512]{1,0:T(8,128)(2,1)S(1)}, u32[]{:S(2)}, u32[]{:S(2)}) collective-permute-start(bf16[1040,512]{1,0:T(8,128)(2,1)S(1)} %concatenate.39), channel_id=1, source_target_pairs={{0,1},{1,0},{2,3},{3,2},{4,5},{5,4},{6,7},{7,6},{8,9},{9,8},{10,11... | collective-permute-start | bytes 3194888 | tf_op jit(solution)/shard_map/ppermute | solution.py:433
  105.0 15.2 %collective-permute-start.11 = (bf16[528,512]{1,0:T(8,128)(2,1)S(1)}, bf16[528,512]{1,0:T(8,128)(2,1)S(1)}, u32[]{:S(2)}, u32[]{:S(2)}) collective-permute-start(bf16[528,512]{1,0:T(8,128)(2,1)S(1)} %copy-done.35), channel_id=1, source_target_pairs={{0,1},{1,0},{2,3},{3,2},{4,5},{5,4},{6,7},{7,6},{8,9},{9,8},{10,11... | collective-permute-start | bytes 1622024 | tf_op jit(solution)/shard_map/ppermute | solution.py:433
  105.5 7.4 %collective-permute-start.7 = (bf16[512,128]{1,0:T(8,128)(2,1)S(1)}, bf16[512,128]{1,0:T(8,128)(2,1)S(1)}, u32[]{:S(2)}, u32[]{:S(2)}) collective-permute-start(bf16[512,128]{1,0:T(8,128)(2,1)S(1)} %get-tuple-element.162), channel_id=1, source_target_pairs={{0,8},{1,9},{2,10},{3,11},{4,12},{5,13},{6,14},{7,15},{8,0},{9,1},... | collective-permute-start | bytes 393224 | tf_op jit(solution)/shard_map/ppermute | solution.py:433
  107.3 12.9 %collective-permute-start.8 = (bf16[512,128]{1,0:T(8,128)(2,1)S(1)}, bf16[512,128]{1,0:T(8,128)(2,1)S(1)}, u32[]{:S(2)}, u32[]{:S(2)}) collective-permute-start(bf16[512,128]{1,0:T(8,128)(2,1)S(1)} %get-tuple-element.163), channel_id=1, source_target_pairs={{0,16},{1,17},{2,18},{3,19},{4,20},{5,21},{6,22},{7,23},{8,24},{9,... | collective-permute-start | bytes 393224 | tf_op jit(solution)/shard_map/ppermute | solution.py:433
  109.9 10.3 %collective-permute-start.9 = (bf16[512,128]{1,0:T(8,128)(2,1)S(1)}, bf16[512,128]{1,0:T(8,128)(2,1)S(1)}, u32[]{:S(2)}, u32[]{:S(2)}) collective-permute-start(bf16[512,128]{1,0:T(8,128)(2,1)S(1)} %get-tuple-element.164), channel_id=1, source_target_pairs={{0,24},{1,25},{2,26},{3,27},{4,28},{5,29},{6,30},{7,31},{8,16},{9,... | collective-permute-start | bytes 393224 | tf_op jit(solution)/shard_map/ppermute | solution.py:433
  122.1 18.6 %collective-permute-start.15 = (bf16[272,512]{1,0:T(8,128)(2,1)S(1)}, bf16[272,512]{1,0:T(8,128)(2,1)S(1)}, u32[]{:S(2)}, u32[]{:S(2)}) collective-permute-start(bf16[272,512]{1,0:T(8,128)(2,1)S(1)} %concatenate.40), channel_id=1, source_target_pairs={{0,2},{1,3},{2,0},{3,1},{4,6},{5,7},{6,4},{7,5},{8,10},{9,11},{10,... | collective-permute-start | bytes 835592 | tf_op jit(solution)/shard_map/ppermute | solution.py:433
  123.7 17.1 %collective-permute-start.16 = (bf16[272,512]{1,0:T(8,128)(2,1)S(1)}, bf16[272,512]{1,0:T(8,128)(2,1)S(1)}, u32[]{:S(2)}, u32[]{:S(2)}) collective-permute-start(bf16[272,512]{1,0:T(8,128)(2,1)S(1)} %concatenate.41), channel_id=1, source_target_pairs={{0,4},{1,5},{2,6},{3,7},{4,0},{5,1},{6,2},{7,3},{8,12},{9,13},{10,... | collective-permute-start | bytes 835592 | tf_op jit(solution)/shard_map/ppermute | solution.py:433
  125.2 15.6 %collective-permute-start.17 = (bf16[272,512]{1,0:T(8,128)(2,1)S(1)}, bf16[272,512]{1,0:T(8,128)(2,1)S(1)}, u32[]{:S(2)}, u32[]{:S(2)}) collective-permute-start(bf16[272,512]{1,0:T(8,128)(2,1)S(1)} %concatenate.42), channel_id=1, source_target_pairs={{0,6},{1,7},{2,4},{3,5},{4,2},{5,3},{6,0},{7,1},{8,14},{9,15},{10,... | collective-permute-start | bytes 835592 | tf_op jit(solution)/shard_map/ppermute | solution.py:433
  125.7 7.5 %collective-permute-start.14 = (bf16[512,128]{1,0:T(8,128)(2,1)S(1)}, bf16[512,128]{1,0:T(8,128)(2,1)S(1)}, u32[]{:S(2)}, u32[]{:S(2)}) collective-permute-start(bf16[512,128]{1,0:T(8,128)(2,1)S(1)} %add_convert_fusion.7), channel_id=1, source_target_pairs={{0,24},{1,25},{2,26},{3,27},{4,28},{5,29},{6,30},{7,31},{8,16},{9,... | collective-permute-start | bytes 393224 | tf_op jit(solution)/shard_map/ppermute | solution.py:433
  128.1 12.6 %collective-permute-start.13 = (bf16[512,128]{1,0:T(8,128)(2,1)S(1)}, bf16[512,128]{1,0:T(8,128)(2,1)S(1)}, u32[]{:S(2)}, u32[]{:S(2)}) collective-permute-start(bf16[512,128]{1,0:T(8,128)(2,1)S(1)} %add_convert_fusion.7), channel_id=1, source_target_pairs={{0,16},{1,17},{2,18},{3,19},{4,20},{5,21},{6,22},{7,23},{8,24},{9,... | collective-permute-start | bytes 393224 | tf_op jit(solution)/shard_map/ppermute | solution.py:433
  133.2 7.6 %collective-permute-start.12 = (bf16[512,128]{1,0:T(8,128)(2,1)S(1)}, bf16[512,128]{1,0:T(8,128)(2,1)S(1)}, u32[]{:S(2)}, u32[]{:S(2)}) collective-permute-start(bf16[512,128]{1,0:T(8,128)(2,1)S(1)} %add_convert_fusion.7), channel_id=1, source_target_pairs={{0,8},{1,9},{2,10},{3,11},{4,12},{5,13},{6,14},{7,15},{8,0},{9,1},... | collective-permute-start | bytes 393224 | tf_op jit(solution)/shard_map/ppermute | solution.py:433
  145.0 7.4 %collective-permute-start.18 = (bf16[80,512]{1,0:T(8,128)(2,1)S(1)}, bf16[80,512]{1,0:T(8,128)(2,1)S(1)}, u32[]{:S(2)}, u32[]{:S(2)}) collective-permute-start(bf16[80,512]{1,0:T(8,128)(2,1)S(1)} %concatenate.43), channel_id=1, source_target_pairs={{0,8},{1,9},{2,10},{3,11},{4,12},{5,13},{6,14},{7,15},{8,0},{9,1},... | collective-permute-start | bytes 245768 | tf_op jit(solution)/shard_map/ppermute | solution.py:433
  146.8 8.0 %collective-permute-start.19 = (bf16[80,512]{1,0:T(8,128)(2,1)}, bf16[80,512]{1,0:T(8,128)(2,1)S(1)}, u32[]{:S(2)}, u32[]{:S(2)}) collective-permute-start(bf16[80,512]{1,0:T(8,128)(2,1)} %concatenate.44), channel_id=1, source_target_pairs={{0,16},{1,17},{2,18},{3,19},{4,20},{5,21},{6,22},{7,23},{8,24},{9,... | collective-permute-start | bytes 245768 | tf_op jit(solution)/shard_map/ppermute | solution.py:433
  148.3 6.5 %collective-permute-start.20 = (bf16[80,512]{1,0:T(8,128)(2,1)S(1)}, bf16[80,512]{1,0:T(8,128)(2,1)S(1)}, u32[]{:S(2)}, u32[]{:S(2)}) collective-permute-start(bf16[80,512]{1,0:T(8,128)(2,1)S(1)} %concatenate.45), channel_id=1, source_target_pairs={{0,24},{1,25},{2,26},{3,27},{4,28},{5,29},{6,30},{7,31},{8,16},{9,... | collective-permute-start | bytes 245768 | tf_op jit(solution)/shard_map/ppermute | solution.py:433
  149.5 29.7 %collective-permute-start.26 = (bf16[4,512,128]{2,1,0:T(8,128)(2,1)S(1)}, bf16[4,512,128]{2,1,0:T(8,128)(2,1)S(1)}, u32[]{:S(2)}, u32[]{:S(2)}) collective-permute-start(bf16[4,512,128]{2,1,0:T(8,128)(2,1)S(1)} %pad_maximum_fusion.refs_0_), channel_id=1, source_target_pairs={{0,6},{1,7},{2,4},{3,5},{4,2},{5,3},{6,0},{7,1},{8,14},{9,15},{10,... | collective-permute-start | bytes 1572872 | tf_op jit(solution)/shard_map/ppermute | solution.py:433
  151.9 27.3 %collective-permute-start.25 = (bf16[4,512,128]{2,1,0:T(8,128)(2,1)S(1)}, bf16[4,512,128]{2,1,0:T(8,128)(2,1)S(1)}, u32[]{:S(2)}, u32[]{:S(2)}) collective-permute-start(bf16[4,512,128]{2,1,0:T(8,128)(2,1)S(1)} %pad_maximum_fusion.refs_0_), channel_id=1, source_target_pairs={{0,4},{1,5},{2,6},{3,7},{4,0},{5,1},{6,2},{7,3},{8,12},{9,13},{10,... | collective-permute-start | bytes 1572872 | tf_op jit(solution)/shard_map/ppermute | solution.py:433
  152.5 26.8 %collective-permute-start.24 = (bf16[4,512,128]{2,1,0:T(8,128)(2,1)S(1)}, bf16[4,512,128]{2,1,0:T(8,128)(2,1)S(1)}, u32[]{:S(2)}, u32[]{:S(2)}) collective-permute-start(bf16[4,512,128]{2,1,0:T(8,128)(2,1)S(1)} %pad_maximum_fusion.refs_0_), channel_id=1, source_target_pairs={{0,2},{1,3},{2,0},{3,1},{4,6},{5,7},{6,4},{7,5},{8,10},{9,11},{10,... | collective-permute-start | bytes 1572872 | tf_op jit(solution)/shard_map/ppermute | solution.py:433
  162.1 17.1 %collective-permute-start.27 = (bf16[272,512]{1,0:T(8,128)(2,1)}, bf16[272,512]{1,0:T(8,128)(2,1)S(1)}, u32[]{:S(2)}, u32[]{:S(2)}) collective-permute-start(bf16[272,512]{1,0:T(8,128)(2,1)} %get-tuple-element.208), channel_id=1, source_target_pairs={{0,2},{1,3},{2,0},{3,1},{4,6},{5,7},{6,4},{7,5},{8,10},{9,11},{10,... | collective-permute-start | bytes 835592 | tf_op jit(solution)/shard_map/ppermute | solution.py:433
  167.9 16.7 %collective-permute-start.28 = (bf16[4,512,128]{2,1,0:T(8,128)(2,1)S(1)}, bf16[4,512,128]{2,1,0:T(8,128)(2,1)S(1)}, u32[]{:S(2)}, u32[]{:S(2)}) collective-permute-start(bf16[4,512,128]{2,1,0:T(8,128)(2,1)S(1)} %pad_maximum_fusion.refs_0_), channel_id=1, source_target_pairs={{0,1},{1,0},{2,3},{3,2},{4,5},{5,4},{6,7},{7,6},{8,9},{9,8},{10,11... | collective-permute-start | bytes 1572872 | tf_op jit(solution)/shard_map/ppermute | solution.py:433
  180.9 7.2 %collective-permute-start.30 = (bf16[4,512,128]{2,1,0:T(8,128)(2,1)S(1)}, bf16[4,512,128]{2,1,0:T(8,128)(2,1)}, u32[]{:S(2)}, u32[]{:S(2)}) collective-permute-start(bf16[4,512,128]{2,1,0:T(8,128)(2,1)S(1)} %collective-permute-done.25.refs_2_), channel_id=1, source_target_pairs={{0,1},{1,0},{2,3},{3,2},{4,5},{5,4},{6,7},{7,6},{8,9},{9,8},{10,11... | collective-permute-start | bytes 1572872 | tf_op jit(solution)/shard_map/ppermute | solution.py:433
  181.4 6.8 %collective-permute-start.31 = (bf16[4,512,128]{2,1,0:T(8,128)(2,1)S(1)}, bf16[4,512,128]{2,1,0:T(8,128)(2,1)}, u32[]{:S(2)}, u32[]{:S(2)}) collective-permute-start(bf16[4,512,128]{2,1,0:T(8,128)(2,1)S(1)} %collective-permute-done.26.refs_3_), channel_id=1, source_target_pairs={{0,1},{1,0},{2,3},{3,2},{4,5},{5,4},{6,7},{7,6},{8,9},{9,8},{10,11... | collective-permute-start | bytes 1572872 | tf_op jit(solution)/shard_map/ppermute | solution.py:433
  182.1 12.7 %collective-permute-start.34 = (bf16[4,64,512]{2,1,0:T(8,128)(2,1)S(1)}, bf16[4,64,512]{2,1,0:T(8,128)(2,1)S(1)}, u32[]{:S(2)}, u32[]{:S(2)}) collective-permute-start(bf16[4,64,512]{2,1,0:T(8,128)(2,1)S(1)} %pad_maximum_fusion.1.refs_0_), channel_id=1, source_target_pairs={{0,6},{1,7},{2,4},{3,5},{4,2},{5,3},{6,0},{7,1},{8,14},{9,15},{10,... | collective-permute-start | bytes 786440 | tf_op jit(solution)/shard_map/ppermute | solution.py:433
  184.6 12.9 %collective-permute-start.33 = (bf16[4,64,512]{2,1,0:T(8,128)(2,1)S(1)}, bf16[4,64,512]{2,1,0:T(8,128)(2,1)}, u32[]{:S(2)}, u32[]{:S(2)}) collective-permute-start(bf16[4,64,512]{2,1,0:T(8,128)(2,1)S(1)} %pad_maximum_fusion.1.refs_0_), channel_id=1, source_target_pairs={{0,4},{1,5},{2,6},{3,7},{4,0},{5,1},{6,2},{7,3},{8,12},{9,13},{10,... | collective-permute-start | bytes 786440 | tf_op jit(solution)/shard_map/ppermute | solution.py:433
  185.9 11.6 %collective-permute-start.32 = (bf16[4,64,512]{2,1,0:T(8,128)(2,1)S(1)}, bf16[4,64,512]{2,1,0:T(8,128)(2,1)}, u32[]{:S(2)}, u32[]{:S(2)}) collective-permute-start(bf16[4,64,512]{2,1,0:T(8,128)(2,1)S(1)} %pad_maximum_fusion.1.refs_0_), channel_id=1, source_target_pairs={{0,2},{1,3},{2,0},{3,1},{4,6},{5,7},{6,4},{7,5},{8,10},{9,11},{10,... | collective-permute-start | bytes 786440 | tf_op jit(solution)/shard_map/ppermute | solution.py:433
  188.2 12.0 %collective-permute-start.35 = (bf16[4,64,512]{2,1,0:T(8,128)(2,1)S(1)}, bf16[4,64,512]{2,1,0:T(8,128)(2,1)S(1)}, u32[]{:S(2)}, u32[]{:S(2)}) collective-permute-start(bf16[4,64,512]{2,1,0:T(8,128)(2,1)S(1)} %pad_maximum_fusion.1.refs_0_), channel_id=1, source_target_pairs={{0,1},{1,0},{2,3},{3,2},{4,5},{5,4},{6,7},{7,6},{8,9},{9,8},{10,11... | collective-permute-start | bytes 786440 | tf_op jit(solution)/shard_map/ppermute | solution.py:433
  (43 other events, 274.7 us)

commit v3 on v2

--- a/solution.py
+++ b/solution.py
@@ -1,3 +1,4 @@
+import functools
 import jax, jax.numpy as jnp
 from jax import lax
 from jax.experimental import pallas as pl
@@ -172,12 +173,14 @@
 
 def two_terms(value):
     high = value.astype(BF16)
-    low = (value - high.astype(F32)).astype(BF16)
-    fill = jnp.zeros((8 - value.shape[0], value.shape[1]), BF16)
-    return jnp.concatenate([high, fill, low, fill])
-
-def one_value(terms, count):
-    return terms[:count].astype(F32) + terms[8 : 8 + count].astype(F32)
+    return jnp.concatenate([high, (value - high.astype(F32)).astype(BF16)])
+
+def one_value(terms):
+    return terms[:16].astype(F32) + terms[16:32].astype(F32)
+
+def rows_of(*values):
+    count = sum(v.shape[0] for v in values)
+    return jnp.concatenate(list(values) + [jnp.zeros((16 - count, values[0].shape[1]), F32)])
 
 def project_kernel(mine, other, wq, wk, wv, gain, hidden, query, keys, values):
     rows = mine.shape[0]
@@ -292,7 +295,7 @@
         name="through",
     )(info, slopes, win, mixed, steep, attended, wo, gain2)
 
-def weights_kernel(info, hid_l, hid_r, near, near_other, far, far_other, dq, dk, dv, grad_out, wq, wk, wv, dense_rows, keep, send, stay, leave, rows, made):
+def weights_kernel(info, hid_l, hid_r, near, near_other, far, far_other, dq, dk, dv, grad_out, wq, wk, wv, dense_rows, through_rows, offsets, buckets, keep, send, stay, leave, small, made):
     count, width = near.shape
     made[0:width, :] = grad_out[...]
     made[width : 2 * width, :] = (dot(hid_l[:count, :], dq[:count, :], TN) + dot(hid_r[:count, :], dq[count:, :], TN)).astype(BF16)
@@ -304,7 +307,7 @@
     @pl.loop(0, 16)
     def _(r):
         keep[r] = made[pl.ds(pl.multiple_of((r ^ mine) * size, size), size), :]
-        send[r] = made[pl.ds(pl.multiple_of(((r + 16) ^ mine) * size, size), size), :]
+        send[pl.ds(pl.multiple_of(r * size, size), size), :] = made[pl.ds(pl.multiple_of(((r + 16) ^ mine) * size, size), size), :]
 
     gain = jnp.zeros((1, width), F32)
     for b, raw in enumerate((near, near_other, far, far_other)):
@@ -318,23 +321,32 @@
             leave[half, :] = grad.astype(BF16)
         tokens = raw[...].astype(F32)
         gain = gain + jnp.sum(grad * (tokens * rms_scale(tokens)), axis=0, keepdims=True)
-    leave[2 * count :, :] = two_terms(dense_rows[0:1, :])
-    rows[...] = jnp.concatenate([gain, jnp.zeros((7, width), F32)])
-
-def weights(info, hid_l, hid_r, near, near_other, far, far_other, dq, dk, dv, grad_out, wq, wk, wv, dense_rows):
+    leave[2 * count :, :] = two_terms(rows_of(dense_rows[0:1, :]))
+    picker = jnp.where(lax.broadcasted_iota(jnp.int32, (width, 1), 0) == buckets[...], 1.0, 0.0).astype(BF16)
+    lines = jnp.concatenate([offsets[g] for g in range(offsets.shape[0])])
+    bias = None
+    for _ in range(3):
+        part = lines.astype(BF16)
+        lines = lines - part.astype(F32)
+        bias = dot(part, picker, NT) if bias is None else bias + dot(part, picker, NT)
+    sums = jnp.concatenate([gain, through_rows[0:1, :], dense_rows[1:2, :], jnp.zeros((5, width), F32), bias])
+    small[...] = sums
+    send[16 * size :, :] = two_terms(sums)
+
+def weights(info, hid_l, hid_r, near, near_other, far, far_other, dq, dk, dv, grad_out, wq, wk, wv, dense_rows, through_rows, offsets, buckets):
     count, width = near.shape
     smem, vmem = pl.BlockSpec(memory_space=pltpu.SMEM), pl.BlockSpec(memory_space=pltpu.VMEM)
     shape = jax.ShapeDtypeStruct
     size = 4 * width // 32
     return pl.pallas_call(
         weights_kernel,
-        in_specs=[smem] + [vmem] * 14,
+        in_specs=[smem] + [vmem] * 17,
         out_specs=[vmem] * 5,
-        out_shape=[shape((16, size, width), BF16), shape((16, size, width), BF16), shape((2 * count, width), F32),
-                   shape((2 * count + 16, width), BF16), shape((8, width), F32)],
+        out_shape=[shape((16, size, width), BF16), shape((16 * size + 32, width), BF16), shape((2 * count, width), F32),
+                   shape((2 * count + 32, width), BF16), shape((16, width), F32)],
         scratch_shapes=[pltpu.VMEM((4 * width, width), BF16)],
         name="weights",
-    )(info, hid_l, hid_r, near, near_other, far, far_other, dq, dk, dv, grad_out, wq, wk, wv, dense_rows)
+    )(info, hid_l, hid_r, near, near_other, far, far_other, dq, dk, dv, grad_out, wq, wk, wv, dense_rows, through_rows, offsets, buckets)
 
 def ending_kernel(info, stay, came, near, far, grad_mixed, gain, dense_rows, home, away):
     count, width = near.shape
@@ -349,84 +361,101 @@
         else:
             away[:count, :] = value
     alive = (info[0] - info[5]).astype(F32)
-    pool = two_terms((dense_rows[0:1, :] + one_value(came[2 * count :, :], 1)) / alive)
+    pool = two_terms((rows_of(dense_rows[0:1, :]) + one_value(came[2 * count :, :])) / alive)
     home[count:, :] = pool
     away[count:, :] = pool
 
 def ending(info, stay, came, near, far, grad_mixed, gain, dense_rows):
     count, width = near.shape
     smem, vmem = pl.BlockSpec(memory_space=pltpu.SMEM), pl.BlockSpec(memory_space=pltpu.VMEM)
-    shape = jax.ShapeDtypeStruct((count + 16, width), BF16)
+    shape = jax.ShapeDtypeStruct((count + 32, width), BF16)
     return pl.pallas_call(
         ending_kernel, in_specs=[smem] + [vmem] * 7, out_specs=[vmem] * 2, out_shape=[shape, shape], name="ending"
     )(info, stay, came, near, far, grad_mixed, gain, dense_rows)
 
-def place_kernel(info, *refs):
-    parts, (back, front) = refs[:8], refs[8:]
+def place_kernel(half, info, *refs):
+    parts, (back, front), (tall, sems) = refs[:4], refs[-4:-2], refs[-2:]
     mine = info[6] & 15
 
-    def backs(half):
-        for i in range(4):
-            for j in range(4):
-                to = (4 * i + j) ^ mine
-                for q in range(4):
-                    back[pl.ds(pl.multiple_of(to * 128, 128), 128), q * 128 : (q + 1) * 128] = half[i][j, q * 128 : (q + 1) * 128, :].astype(F32)
-
-    def ins(half):
-        for i in range(4):
-            for j in range(4):
-                to = (4 * i + j) ^ mine
-                front[:, pl.ds(pl.multiple_of(to * 128, 128), 128)] = half[i][j].astype(F32)
-
-    @pl.when(info[7] == 0)
+    @pl.when(info[7] == half)
     def _():
-        backs(parts[:4])
-        ins(parts[4:])
-
-    @pl.when(info[7] == 1)
+        copies = []
+        for r in range(16):
+            to = pl.ds(pl.multiple_of((r ^ mine) * 128, 128), 128)
+            for q in range(4):
+                tall[r, :128, q * 128 : (q + 1) * 128] = parts[r // 4][r % 4, q * 128 : (q + 1) * 128, :].astype(F32)
+            copies.append(pltpu.make_async_copy(tall.at[r, :128, :], back.at[to, :], sems.at[r]))
+            copies[-1].start()
+        for copy in copies:
+            copy.wait()
+
+    @pl.when(info[7] != half)
     def _():
-        ins(parts[:4])
-        backs(parts[4:])
-
-def place(info, parts, width):
-    hidden = 16 * 128
-    smem, vmem = pl.BlockSpec(memory_space=pltpu.SMEM), pl.BlockSpec(memory_space=pltpu.VMEM)
+        copies = []
+        for r in range(16):
+            to = pl.ds(pl.multiple_of((r ^ mine) * 128, 128), 128)
+            tall[r, :, :128] = parts[r // 4][r % 4].astype(F32)
+            copies.append(pltpu.make_async_copy(tall.at[r, :, :128], front.at[:, to], sems.at[r]))
+            copies[-1].start()
+        for copy in copies:
+            copy.wait()
+
+def place(info, half, parts, made, width):
+    smem, vmem, free = (pl.BlockSpec(memory_space=m) for m in (pltpu.SMEM, pltpu.VMEM, pl.ANY))
     shape = jax.ShapeDtypeStruct
     return pl.pallas_call(
-        place_kernel, in_specs=[smem] + [vmem] * 8, out_specs=[vmem] * 2,
-        out_shape=[shape((hidden, width), F32), shape((width, hidden), F32)], name="place",
-    )(info, *parts)
-
-def sort_kernel(info, *refs):
-    parts, made = refs[:8], refs[8:]
-    size, width = parts[0].shape[1:]
-    per = width // size
-    mine = info[6]
-
-    for half in range(2):
-        for top in range(2):
-            @pl.when(((mine >> 4) ^ half) == top)
-            def _(half=half, top=top):
-                for i in range(4):
-                    for j in range(4):
-                        to = ((4 * i + j) ^ mine) & 15
-                        value = parts[4 * half + i][j].astype(F32)
-                        spot = pl.ds(pl.multiple_of((to % per) * size, size), size)
-
-                        @pl.when(to < per)
-                        def _():
-                            made[2 * top][spot, :] = value
-
-                        @pl.when(to >= per)
-                        def _():
-                            made[2 * top + 1][spot, :] = value
-
-def sort(info, parts, width):
-    smem, vmem = pl.BlockSpec(memory_space=pltpu.SMEM), pl.BlockSpec(memory_space=pltpu.VMEM)
+        functools.partial(place_kernel, half),
+        in_specs=[smem] + [vmem] * 4 + [free] * len(made),
+        out_specs=[free] * 2,
+        out_shape=[shape((16 * 128, width), F32), shape((width, 16 * 128), F32)],
+        scratch_shapes=[pltpu.VMEM((16, width, width), F32), pltpu.SemaphoreType.DMA((16,))],
+        input_output_aliases={5 + i: i for i in range(len(made))},
+        name="place",
+    )(info, *parts, *made)
+
+def sort_kernel(half, info, *refs):
+    parts, made, (tall, sems) = refs[:4], refs[-6:-2], refs[-2:]
+    size = parts[0].shape[1]
+    per = tall.shape[1] // size
+    mine = info[6] & 15
+    for r in range(16):
+        to = r ^ mine
+        tall[to // per, pl.ds(pl.multiple_of((to % per) * size, size), size), :] = parts[r // 4][r % 4].astype(F32)
+    for top in range(2):
+        @pl.when((info[7] ^ half) == top)
+        def _(top=top):
+            copies = [pltpu.make_async_copy(tall.at[w], made[2 * top + w], sems.at[w]) for w in range(2)]
+            for copy in copies:
+                copy.start()
+            for copy in copies:
+                copy.wait()
+
+def sort(info, half, parts, made, width):
+    smem, vmem, free = (pl.BlockSpec(memory_space=m) for m in (pltpu.SMEM, pltpu.VMEM, pl.ANY))
     shape = jax.ShapeDtypeStruct((width, width), F32)
     return pl.pallas_call(
-        sort_kernel, in_specs=[smem] + [vmem] * 8, out_specs=[vmem] * 4, out_shape=[shape] * 4, name="sort"
-    )(info, *parts)
+        functools.partial(sort_kernel, half),
+        in_specs=[smem] + [vmem] * 4 + [free] * len(made),
+        out_specs=[free] * 4,
+        out_shape=[shape] * 4,
+        scratch_shapes=[pltpu.VMEM((2, width, width), F32), pltpu.SemaphoreType.DMA((2,))],
+        input_output_aliases={5 + i: i for i in range(len(made))},
+        name="sort",
+    )(info, *parts, *made)
+
+def mix_kernel(*refs):
+    ins, outs = refs[: -4], refs[-4:]
+    for k in range(4):
+        outs[k][...] = added(*[term[k] for term in ins])
+
+def mix(terms):
+    block = terms[0].shape[1:]
+    spec = pl.BlockSpec((4,) + block, lambda i: (0,) * (1 + len(block)))
+    out = pl.BlockSpec(block, lambda i: (0,) * len(block))
+    return pl.pallas_call(
+        mix_kernel, grid=(1,), in_specs=[spec] * len(terms), out_specs=[out] * 4,
+        out_shape=[jax.ShapeDtypeStruct(block, BF16)] * 4, name="mix",
+    )(*terms)
 
 def exchange(value, bits):
     size = lax.axis_size("dp") * lax.axis_size("blk")
@@ -450,24 +479,27 @@
     line = [8, 16]
     further = [32 << b for b in range((lax.axis_size("dp") // 8).bit_length() - 1)]
     piece = core * 16 + doc * 4 + (far_off % 2) * 8 + (far_off // 2) % 4
-    near = lax.dynamic_index_in_dim(inputs, doc, 0, keepdims=False)
-    far = exchange(lax.dynamic_index_in_dim(inputs, 1 - doc, 0, keepdims=False), ROW)
+    near = jnp.where(doc == 0, inputs[0], inputs[1])
+    far_send = jnp.where(doc == 0, inputs[1], inputs[0])
+    near, far_send = wait(near, far_send)
+    far = exchange(far_send, ROW)
     near_other = exchange(near, CORE)
-    far_other = exchange(far, CORE)
-    limit = length - lax.dynamic_index_in_dim(pad_len, doc, 0, keepdims=False)
-    prefix = lax.dynamic_index_in_dim(prefix_len, doc, 0, keepdims=False)
-    cot = lax.dynamic_index_in_dim(pooled_grad, doc, 0, keepdims=True) / (limit - prefix).astype(F32)
+    limit = length - jnp.where(doc == 0, pad_len[0], pad_len[1])
+    prefix = jnp.where(doc == 0, prefix_len[0], prefix_len[1])
+    cot = jnp.where(doc == 0, pooled_grad[:1], pooled_grad[1:]) / (limit - prefix).astype(F32)
     slot = jnp.arange(8, dtype=jnp.int32)
     info = jnp.where(slot == 0, limit, 0)
     for i, value in enumerate([b * rows for b in block] + [prefix, piece, core]):
         info = jnp.where(slot == i + 1, value, info)
-    picker = (jnp.arange(BUCKETS, dtype=jnp.int32)[:, None] == bucket_table[None, :]).astype(F32)
-    picker = jnp.pad(picker, ((0, 0), (0, 1)))
+    buckets = jnp.pad(bucket_table, (0, 1), constant_values=-1)[None, :]
+    picker = (jnp.arange(BUCKETS, dtype=jnp.int32)[:, None] == buckets).astype(F32)
     table = lax.dot_general(bias_table, picker, TN, precision=lax.Precision.HIGHEST)
     table = table.reshape(-1, 2, picker.shape[1])
 
     gain1, gain2, gain3 = norm1_gain[None, :], norm2_gain[None, :], final_gain[None, :]
     hid_l, q_l, k_l, v_l = project(near, near_other, w_query, w_key, w_value, gain1)
+    far, q_l, info, table, cot, buckets = wait(far, q_l, info, table, cot, buckets)
+    far_other = exchange(far, CORE)
     hid_r, q_r, k_r, v_r = project(far, far_other, w_query, w_key, w_value, gain1)
     attended, expo, inverse = attention(info, q_l, q_r, k_l, k_r, v_l, v_r, table)
     keep, send, slopes, mixed, steep, dense_rows = dense(info, near, far, attended, w_out, w_in, w_back, gain2, gain3, cot)
@@ -480,55 +512,59 @@
     grad_mixed, grad_out_w, grad_attended, through_rows = through(token, slopes, w_in, mixed, steep, attended, w_out, gain2)
     token, through_rows, got = wait(token, through_rows, got)
 
-    sends = [added(keep[4 * k : 4 * k + 4], got[4 * k : 4 * k + 4]) for k in (1, 2, 3)]
+    sends = [added(keep[4 * k : 4 * k + 4], got[4 * k : 4 * k + 4]) for k in (3, 1, 2)]
+    came = [exchange(s, m) for s, m in zip(sends, (xy[2], xy[0], xy[1]))]
     token, sends = wait(token, sends)
-    came = [exchange(s, m) for s, m in zip(sends, xy)]
     dq, dk, dv, offsets = attention_grads(token, q_l, q_r, k_l, k_r, v_l, v_r, grad_attended, attended, inverse, expo)
-    rest_keep, rest_send, stay, leave, first_rows = weights(
-        token, hid_l, hid_r, near, near_other, far, far_other, dq, dk, dv, grad_out_w, w_query, w_key, w_value, dense_rows)
-    grad_bias = lax.dot_general(picker, offsets.reshape(-1, picker.shape[1]), NT, precision=lax.Precision.HIGHEST)
-    grad_bias = jnp.pad(grad_bias.reshape(1, -1), ((0, 0), (0, width - grad_bias.size)))
-    small = jnp.concatenate([first_rows[:1], through_rows[:1], dense_rows[1:2], grad_bias])
-    token, first_rows, came = wait(token, first_rows, came)
-
-    lines = [added(keep[k], got[k], *[c[k] for c in came]) for k in range(4)]
-    first = jnp.concatenate([rest_send.reshape(-1, width), two_terms(small)])
-    token, lines, leave, first = wait(token, lines, leave, first)
+    rest_keep, rest_send, stay, leave, small = weights(
+        token, hid_l, hid_r, near, near_other, far, far_other, dq, dk, dv, grad_out_w, w_query, w_key, w_value, dense_rows,
+        through_rows, offsets, buckets)
+    token, small, rest_send, leave, came = wait(token, small, rest_send, leave, came)
+
+    rest_got = exchange(rest_send, CORE)
+    hidden_got = exchange(leave, CORE)
+    lines = mix([keep, got] + list(came))
+    token, lines = wait(token, lines)
     took = [exchange(lines[k + 1], m) for k, m in enumerate(zz)]
-    rest_got = exchange(first, CORE)
-    hidden_got = exchange(leave, CORE)
-    token, took, rest_got, hidden_got = wait(token, took, rest_got, hidden_got)
+    token, rest_got, hidden_got = wait(token, rest_got, hidden_got)
+
+    count = rest_keep.shape[0] * rest_keep.shape[1]
+    small = small + one_value(rest_got[count:])
+    rest_got = rest_got[:count].reshape(rest_keep.shape)
+    terms = two_terms(small)
+    sends = [jnp.concatenate([added(rest_keep[4 * k : 4 * k + 4], rest_got[4 * k : 4 * k + 4]).reshape(-1, width), terms]) for k in (1, 2, 3)]
+    token, sends = wait(token, sends)
+    rest_came = [exchange(s, m) for s, m in zip(sends, xy)]
+    home, away = ending(token, stay, hidden_got, near, far, grad_mixed, gain1, dense_rows)
+    token, took, away = wait(token, took, away)
+
     whole = added(lines[0], *took)
     for bit in further:
         whole = added(whole, exchange(whole, bit))
-
-    count = rest_keep.shape[0] * rest_keep.shape[1]
-    small = small + one_value(rest_got[count:], 4)
-    rest_got = rest_got[:count].reshape(rest_keep.shape)
-    terms = two_terms(small)
-    sends = [jnp.concatenate([added(rest_keep[4 * k : 4 * k + 4], rest_got[4 * k : 4 * k + 4]).reshape(-1, width), terms]) for k in (1, 2, 3)]
-    token, whole, sends = wait(token, whole, sends)
+    token, whole = wait(token, whole)
     back_line = [exchange(whole, m) for m in zz]
-    rest_came = [exchange(s, m) for s, m in zip(sends, xy)]
-    home, away = ending(token, stay, hidden_got, near, far, grad_mixed, gain1, dense_rows)
-    token, back_line, rest_came, away = wait(token, back_line, rest_came, away)
-
-    quarter = jnp.stack([whole] + back_line)
+    away_got = exchange(away, ROW)
+    token, rest_came = wait(token, rest_came)
+
     count = count // 4
     for part in rest_came:
-        small = small + one_value(part[count:], 4)
+        small = small + one_value(part[count:])
     rest_came = [part[:count].reshape((4,) + rest_keep.shape[1:]) for part in rest_came]
     terms = two_terms(small)
     lines = [added(rest_keep[k], rest_got[k], *[c[k] for c in rest_came]) for k in range(4)]
     sends = [jnp.concatenate([lines[k], terms]) for k in (1, 2, 3)]
-    token, quarter, sends, away = wait(token, quarter, sends, away)
+    token, sends = wait(token, sends)
+    took = [exchange(s, m) for s, m in zip(sends, zz)]
+    token, back_line = wait(token, back_line)
+
+    quarter = jnp.stack([whole] + back_line)
+    token, quarter = wait(token, quarter)
     quarters = [exchange(quarter, m) for m in xy]
-    took = [exchange(s, m) for s, m in zip(sends, zz)]
-    away_got = exchange(away, ROW)
     token, took = wait(token, took)
+
     count = count // 4
     for part in took:
-        small = small + one_value(part[count:], 4)
+        small = small + one_value(part[count:])
     rest = added(lines[0], *[part[:count] for part in took])
     for bit in further:
         rest = added(rest, exchange(rest, bit))
@@ -537,20 +573,23 @@
     back_line = [exchange(rest, m) for m in zz]
     token, back_line = wait(token, back_line)
     rest_quarter = jnp.stack([rest] + back_line)
-
     token, rest_quarter = wait(token, rest_quarter)
     rest_quarters = [exchange(rest_quarter, m) for m in xy]
-    token, quarters, away_got = wait(token, quarters, away_got)
+
+    token, quarters = wait(token, quarters)
     mine = [quarter] + quarters
     others = [exchange(value, CORE) for value in mine]
-    token, others = wait(token, others)
-    out_back, out_in = place(token, mine + others, width)
-    token, out_back, rest_quarters = wait(token, out_back, rest_quarters)
+    out_big = place(token, 0, mine, [], width)
+    token, out_big, others = wait(token, out_big, others)
+    out_back, out_in = place(token, 1, others, out_big, width)
+    token, out_back, out_in, rest_quarters, away_got = wait(token, out_back, out_in, rest_quarters, away_got)
     mine = [rest_quarter] + rest_quarters
     others = [exchange(value, CORE) for value in mine]
-    out_out, out_query, out_key, out_value = sort(info, mine + others, width)
-
-    pool_mine, pool_other = one_value(home[rows:], 1), one_value(away_got[rows:], 1)
+    out_rest = sort(token, 0, mine, [], width)
+    token, out_rest, others = wait(token, out_rest, others)
+    out_out, out_query, out_key, out_value = sort(token, 1, others, out_rest, width)
+
+    pool_mine, pool_other = one_value(home[rows:])[:1], one_value(away_got[rows:])[:1]
     pooled = jnp.where(doc == 0, jnp.concatenate([pool_mine, pool_other]), jnp.concatenate([pool_other, pool_mine]))
     home, away_got = home[:rows], away_got[:rows]
     input_grad = jnp.where(doc == 0, jnp.stack([home, away_got]), jnp.stack([away_got, home]))
@@ -566,7 +605,7 @@
         small[0],
         small[1],
         small[2],
-        small[3, : bias_table.size].reshape(bias_table.shape),
+        small[8:, :BUCKETS].T,
     )
 
 def solution(mesh):

time: 207 us -> 183 us (0.88)
  local copies, waits for them, and re-layouts: 21 us -> 8.68 us
  waiting for transfers between devices: 39.3 us -> 29.6 us
  Pallas kernels: 82.6 us -> 89.5 us
  other arithmetic: 17.4 us -> 10.8 us
  starting transfers between devices: 42.6 us -> 39.5 us
    ppermute x39, waiting for transfers between devices: 39.3 us -> 29.6 us  [exchange(): lax.ppermute(value, ('dp', 'blk'), [(i, i ^ bits) for i in range(size)])]
    pallas_call x3 -> x6, Pallas kernels: 17.8 us -> 24.8 us  [the longest x1 9.24 us: weights(): pl.pallas_call(weights_kernel, in_specs=[smem] + [vmem] * 17, out_specs=[...]
    concatenate x7 -> x0, local copies, waits for them, and re-layouts: 6.22 us -> none  [the longest x1 3.84 us: local(): first = jnp.concatenate([rest_send.reshape(-1, width), two_terms(small)])]
    convert_element_type x7 -> x5, other arithmetic: 8.54 us -> 5.19 us  [added(): return total.astype(BF16)]
    ppermute x39, starting transfers between devices: 42.6 us -> 39.5 us  [exchange(): lax.ppermute(value, ('dp', 'blk'), [(i, i ^ bits) for i in range(size)])]
    dynamic_slice x2 -> x0, local copies, waits for them, and re-layouts: 2.48 us -> none  [the longest x1 1.24 us: local(): limit = length - lax.dynamic_index_in_dim(pad_len, doc, 0, keepdims=False)]
    add x3, other arithmetic: 2.32 us -> 0.03 us  [the longest x1 0.02 us: local(): small = small + one_value(part[count:])]
    unnamed x73 -> x60, local copies, waits for them, and re-layouts: 5.58 us -> 3.4 us
  transfers between devices with their start and end apart: 39 -> 39, of which waited for: 9 -> 12; matrix products, arithmetic and copies ran while one was open for 11% -> 7% of each run, Pallas kernels for 23% -> 30%
where the time goes in v3:
time: 183 us; the launch traced here: 182 us
  Pallas kernels  89.5 us (49%)
  starting transfers between devices  39.5 us (22%)
  waiting for transfers between devices  29.6 us (16%)
  other arithmetic  10.8 us (6%)
  local copies, waits for them, and re-layouts  8.68 us (5%)
  between operations  3.88 us (2%)
    ppermute x39, starting transfers between devices, exchange(): lax.ppermute(value, ('dp', 'blk'), [(i, i ^ bits) for i in range(size)])  39.5 us
    ppermute x39, waiting for transfers between devices, exchange(): lax.ppermute(value, ('dp', 'blk'), [(i, i ^ bits) for i in range(size)])  29.6 us
    pallas_call x1, Pallas kernels, attention_grads(): pl.pallas_call(bwd_kernel, grid=(pairs,), in_specs=[pl.BlockSpec(memory_s...  20.1 us
    pallas_call x1, Pallas kernels, dense(): pl.pallas_call(dense_kernel, in_specs=[smem] + [vmem] * 9, out_specs=[vme...  15.8 us
    pallas_call x1, Pallas kernels, attention(): pl.pallas_call(fwd_kernel, grid=(pairs,), in_specs=[pl.BlockSpec(memory_s...  12.7 us
    pallas_call x1, Pallas kernels, weights(): pl.pallas_call(weights_kernel, in_specs=[smem] + [vmem] * 17, out_specs=[...  9.24 us
    pallas_call x2, Pallas kernels, place(): pl.pallas_call(functools.partial(place_kernel, half), in_specs=[smem] + [...  7.4 us
    pallas_call x2, Pallas kernels, project(): pl.pallas_call(project_kernel, out_shape=[shape(2 * rows), shape(rows), s...  6.52 us
  transfers between devices with their start and end apart: 39, of which 12 were waited for; matrix products, arithmetic and copies ran while one was open for 7% of the time, Pallas kernels for 30%

profile of v3, /device:TPU:0, one launch (start us, length us, event | category | flops | bytes accessed | tf_op | source)
XLA Modules:
  0.0 182.2 jit_solution(16653634059612699393)
XLA Ops:
  1.8 3.0 %collective-permute-start = (bf16[256,512]{1,0:T(8,128)(2,1)S(1)}, bf16[256,512]{1,0:T(8,128)(2,1)S(1)}, u32[]{:S(2)}, u32[]{:S(2)}) collective-permute-start(bf16[256,512]{1,0:T(8,128)(2,1)S(1)} %get-tuple-element.153), channel_id=1, source_target_pairs={{0,2},{1,3},{2,0},{3,1},{4,6},{5,7},{6,4},{7,5},{8,10},{9,11},{10,... | collective-permute-start | bytes 786440 | tf_op jit(solution)/shard_map/ppermute | solution.py:462
  14.3 3.3 %project.2 = (bf16[512,512]{1,0:T(8,128)(2,1)}, bf16[256,512]{1,0:T(8,128)(2,1)}, bf16[512,512]{1,0:T(8,128)(2,1)}, bf16[512,512]{1,0:T(8,128)(2,1)}) custom-call(bf16[256,512]{1,0:T(8,128)(2,1)} %copy-done.2, bf16[256,512]{1,0:T(8,128)(2,1)} %copy-done.6, bf16[512,512]{1,0:T(8,128)(2,1)} %wq.5, bf16[512,512]{1,0:T(8,128)(2,1)} %wk.5, bf16[512,512]{1,0:T(8,128)(2,1)} %wv.5, ...), custom_call_target="tpu_custom_call" | custom-call | tf_op jit(solution)/shard_map/project/pallas_call | solution.py:198
  20.0 3.3 %project.3 = (bf16[512,512]{1,0:T(8,128)(2,1)}, bf16[256,512]{1,0:T(8,128)(2,1)}, bf16[512,512]{1,0:T(8,128)(2,1)}, bf16[512,512]{1,0:T(8,128)(2,1)}) custom-call(bf16[256,512]{1,0:T(8,128)(2,1)} %copy-done.4, bf16[256,512]{1,0:T(8,128)(2,1)} %copy-done.7, bf16[512,512]{1,0:T(8,128)(2,1)} %wq.5, bf16[512,512]{1,0:T(8,128)(2,1)} %wk.5, bf16[512,512]{1,0:T(8,128)(2,1)} %wv.5, ...), custom_call_target="tpu_custom_call" | custom-call | tf_op jit(solution)/shard_map/project/pallas_call | solution.py:198
  23.3 12.7 %attn_fwd.1 = (bf16[512,512]{1,0:T(8,128)(2,1)}, bf16[8,512,1024]{2,1,0:T(8,128)(2,1)}, f32[512,512]{1,0:T(8,128)}) custom-call(s32[8]{0:T(128)} %compare_select_fusion.7.info, bf16[256,512]{1,0:T(8,128)(2,1)} %get-tuple-element.158.ql, bf16[256,512]{1,0:T(8,128)(2,1)} %get-tuple-element.159.qr, bf16[512,512]{1,0:T(8,128)(2,1)} %get-tuple-element.160.kl, ...), custom_call_target="tpu_custom_call" | custom-call | tf_op jit(solution)/shard_map/attn_fwd/pallas_call | solution.py:74
  35.9 15.8 %dense.1 = (bf16[16,512,128]{2,1,0:T(8,128)(2,1)}, bf16[16,512,128]{2,1,0:T(8,128)(2,1)}, bf16[512,2048]{1,0:T(8,128)(2,1)}, f32[512,512]{1,0:T(8,128)}, f32[512,512]{1,0:T(8,128)}, /*index=5*/f32[8,512]{1,0:T(8,128)}) custom-call(s32[8]{0:T(128)} %compare_select_fusion.7.info, bf16[256,512]{1,0:T(8,128)(2,1)} %copy-done.2, bf16[256,512]{1,0:T(8,128)(2,1)} %copy-done.4, ...), custom_call_target="tpu_custom_call" | custom-call | tf_op jit(solution)/shard_map/dense/pallas_call | solution.py:261
  52.1 6.4 %through.1 = (f32[512,512]{1,0:T(8,128)}, bf16[512,512]{1,0:T(8,128)(2,1)}, bf16[512,512]{1,0:T(8,128)(2,1)}, f32[8,512]{1,0:T(8,128)}) custom-call(s32[8]{0:T(128)} %compare_select_fusion.7.info, bf16[512,2048]{1,0:T(8,128)(2,1)} %get-tuple-element.169.slopes, bf16[512,2048]{1,0:T(8,128)(2,1)} %win.3, f32[512,512]{1,0:T(8,128)} %get-tuple-element.170.mixed, ...), custom_call_target="tpu_custom_call" | custom-call | tf_op jit(solution)/shard_map/through/pallas_call | solution.py:290
  58.5 2.7 %add_convert_fusion = (bf16[4,512,128]{2,1,0:T(8,128)(2,1)}, bf16[4,512,128]{2,1,0:T(8,128)(2,1)S(1)}, bf16[4,512,128]{2,1,0:T(8,128)(2,1)S(1)}) fusion(bf16[16,512,128]{2,1,0:T(8,128)(2,1)} %collective-permute-done.3.refs_1_, bf16[16,512,128]{2,1,0:T(8,128)(2,1)S(1)} %copy-done.3), kind=kLoop, calls=%fused_computation.1 | loop fusion | flops 3145728 | bytes 4718592 | tf_op jit(solution)/shard_map/convert_element_type | solution.py:471
  64.7 20.1 %attn_bwd.1 = (bf16[512,512]{1,0:T(8,128)(2,1)}, bf16[1024,512]{1,0:T(8,128)(2,1)}, bf16[1024,512]{1,0:T(8,128)(2,1)}, f32[4,2,2048]{2,1,0:T(2,128)}) custom-call(s32[8]{0:T(128)} %compare_select_fusion.7.info, bf16[256,512]{1,0:T(8,128)(2,1)} %get-tuple-element.158.ql, bf16[256,512]{1,0:T(8,128)(2,1)} %get-tuple-element.159.qr, ...), custom_call_target="tpu_custom_call" | custom-call | tf_op jit(solution)/shard_map/attn_bwd/pallas_call | solution.py:149
  84.9 9.2 %weights.1 = (bf16[16,64,512]{2,1,0:T(8,128)(2,1)}, bf16[1056,512]{1,0:T(8,128)(2,1)}, f32[512,512]{1,0:T(8,128)}, bf16[544,512]{1,0:T(8,128)(2,1)}, f32[16,512]{1,0:T(8,128)}) custom-call(s32[8]{0:T(128)} %compare_select_fusion.7.info, bf16[512,512]{1,0:T(8,128)(2,1)} %get-tuple-element.178.hid_l, bf16[512,512]{1,0:T(8,128)(2,1)} %get-tuple-element.179.hid_r, ...), custom_call_target="tpu_custom_call" | custom-call | tf_op jit(solution)/shard_map/weights/pallas_call | solution.py:341
  95.7 2.6 %mix.1 = (bf16[512,128]{1,0:T(8,128)(2,1)}, bf16[512,128]{1,0:T(8,128)(2,1)}, bf16[512,128]{1,0:T(8,128)(2,1)}, bf16[512,128]{1,0:T(8,128)(2,1)}) custom-call(bf16[16,512,128]{2,1,0:T(8,128)(2,1)} %get-tuple-element.175.refs_0_, bf16[16,512,128]{2,1,0:T(8,128)(2,1)} %collective-permute-done.3.refs_1_, bf16[4,512,128]{2,1,0:T(8,128)(2,1)} %copy-done.16, ...), custom_call_target="tpu_custom_call" | custom-call | tf_op jit(solution)/shard_map/mix/pallas_call | solution.py:455
  98.3 1.6 collective-permute-start.9
  99.9 2.6 %collective-permute-start.10 = (bf16[512,128]{1,0:T(8,128)(2,1)}, bf16[512,128]{1,0:T(8,128)(2,1)}, u32[]{:S(2)}, u32[]{:S(2)}) collective-permute-start(bf16[512,128]{1,0:T(8,128)(2,1)} %get-tuple-element.215), channel_id=1, source_target_pairs={{0,16},{1,17},{2,18},{3,19},{4,20},{5,21},{6,22},{7,23},{8,24},{9,... | collective-permute-start | bytes 393224 | tf_op jit(solution)/shard_map/ppermute | solution.py:462
  104.2 1.7 collective-permute-start.13
  107.4 3.2 %ending.1 = (bf16[288,512]{1,0:T(8,128)(2,1)}, bf16[288,512]{1,0:T(8,128)(2,1)}) custom-call(s32[8]{0:T(128)} %compare_select_fusion.7.info, f32[512,512]{1,0:T(8,128)} %get-tuple-element.210.stay, bf16[544,512]{1,0:T(8,128)(2,1)} %copy-done.10, bf16[256,512]{1,0:T(8,128)(2,1)} %copy-done.2, bf16[256,512]{1,0:T(8,128)(2,1)} %copy-done.4, ...), custom_call_target="tpu_custom_call" | custom-call | tf_op jit(solution)/shard_map/ending/pallas_call | solution.py:372
  110.7 2.4 %collective-permute-done.10 = bf16[512,128]{1,0:T(8,128)(2,1)} collective-permute-done((bf16[512,128]{1,0:T(8,128)(2,1)}, bf16[512,128]{1,0:T(8,128)(2,1)}, u32[]{:S(2)}, u32[]{:S(2)}) %collective-permute-start.10) | collective-permute-done | bytes 131104 | tf_op jit(solution)/shard_map/ppermute | solution.py:462
  114.3 2.4 %collective-permute-start.17 = (bf16[512,128]{1,0:T(8,128)(2,1)S(1)}, bf16[512,128]{1,0:T(8,128)(2,1)S(1)}, u32[]{:S(2)}, u32[]{:S(2)}) collective-permute-start(bf16[512,128]{1,0:T(8,128)(2,1)S(1)} %add_convert_fusion.3), channel_id=1, source_target_pairs={{0,24},{1,25},{2,26},{3,27},{4,28},{5,29},{6,30},{7,31},{8,16},{9,... | collective-permute-start | bytes 393224 | tf_op jit(solution)/shard_map/ppermute | solution.py:462
  120.0 2.6 %collective-permute-done.17 = bf16[512,128]{1,0:T(8,128)(2,1)S(1)} collective-permute-done((bf16[512,128]{1,0:T(8,128)(2,1)S(1)}, bf16[512,128]{1,0:T(8,128)(2,1)S(1)}, u32[]{:S(2)}, u32[]{:S(2)}) %collective-permute-start.17) | collective-permute-done | bytes 131104 | tf_op jit(solution)/shard_map/ppermute | solution.py:462
  122.6 5.1 %collective-permute-done.16 = bf16[512,128]{1,0:T(8,128)(2,1)S(1)} collective-permute-done((bf16[512,128]{1,0:T(8,128)(2,1)S(1)}, bf16[512,128]{1,0:T(8,128)(2,1)S(1)}, u32[]{:S(2)}, u32[]{:S(2)}) %collective-permute-start.16) | collective-permute-done | bytes 131104 | tf_op jit(solution)/shard_map/ppermute | solution.py:462
  127.7 3.0 %collective-permute-start.19 = (bf16[96,512]{1,0:T(8,128)(2,1)S(1)}, bf16[96,512]{1,0:T(8,128)(2,1)S(1)}, u32[]{:S(2)}, u32[]{:S(2)}) collective-permute-start(bf16[96,512]{1,0:T(8,128)(2,1)S(1)} %get-tuple-element.239), channel_id=1, source_target_pairs={{0,16},{1,17},{2,18},{3,19},{4,20},{5,21},{6,22},{7,23},{8,24},{9,... | collective-permute-start | bytes 294920 | tf_op jit(solution)/shard_map/ppermute | solution.py:462
  132.2 1.5 collective-permute-start.26
  134.2 1.5 collective-permute-start.24
  135.8 2.3 %collective-permute-done.19 = bf16[96,512]{1,0:T(8,128)(2,1)S(1)} collective-permute-done((bf16[96,512]{1,0:T(8,128)(2,1)S(1)}, bf16[96,512]{1,0:T(8,128)(2,1)S(1)}, u32[]{:S(2)}, u32[]{:S(2)}) %collective-permute-start.19) | collective-permute-done | bytes 98336 | tf_op jit(solution)/shard_map/ppermute | solution.py:462
  139.0 2.5 %collective-permute-start.23 = (bf16[64,512]{1,0:T(8,128)(2,1)S(1)}, bf16[64,512]{1,0:T(8,128)(2,1)S(1)}, u32[]{:S(2)}, u32[]{:S(2)}) collective-permute-start(bf16[64,512]{1,0:T(8,128)(2,1)S(1)} %add_convert_fusion.4), channel_id=1, source_target_pairs={{0,24},{1,25},{2,26},{3,27},{4,28},{5,29},{6,30},{7,31},{8,16},{9,... | collective-permute-start | bytes 196616 | tf_op jit(solution)/shard_map/ppermute | solution.py:462
  142.2 3.1 %collective-permute-done.23 = bf16[64,512]{1,0:T(8,128)(2,1)S(1)} collective-permute-done((bf16[64,512]{1,0:T(8,128)(2,1)S(1)}, bf16[64,512]{1,0:T(8,128)(2,1)S(1)}, u32[]{:S(2)}, u32[]{:S(2)}) %collective-permute-start.23) | collective-permute-done | bytes 65568 | tf_op jit(solution)/shard_map/ppermute | solution.py:462
  147.2 1.5 collective-permute-start.34
  149.6 6.1 %collective-permute-done.25.refs_2_ = bf16[4,512,128]{2,1,0:T(8,128)(2,1)S(1)} collective-permute-done((bf16[4,512,128]{2,1,0:T(8,128)(2,1)S(1)}, bf16[4,512,128]{2,1,0:T(8,128)(2,1)S(1)}, u32[]{:S(2)}, u32[]{:S(2)}) %collective-permute-start.25) | collective-permute-done | bytes 524320 | tf_op jit(solution)/shard_map/ppermute | solution.py:462
  156.5 1.6 collective-permute-start.33
  161.8 3.7 %place.2 = (f32[2048,512]{1,0:T(8,128)}, f32[512,2048]{1,0:T(8,128)}) custom-call(s32[8]{0:T(128)} %compare_select_fusion.7.info, bf16[4,512,128]{2,1,0:T(8,128)(2,1)} %copy-done.5, bf16[4,512,128]{2,1,0:T(8,128)(2,1)} %copy-done.13, bf16[4,512,128]{2,1,0:T(8,128)(2,1)} %copy-done.12, bf16[4,512,128]{2,1,0:T(8,128)(2,1)} %copy-done.11), custom_call_target="tpu_custom_call" | custom-call | tf_op jit(solution)/shard_map/place/pallas_call | solution.py:406
  165.7 3.7 %place.3 = (f32[2048,512]{1,0:T(8,128)}, f32[512,2048]{1,0:T(8,128)}) custom-call(s32[8]{0:T(128)} %compare_select_fusion.7.info, bf16[4,512,128]{2,1,0:T(8,128)(2,1)} %copy-done.17, bf16[4,512,128]{2,1,0:T(8,128)(2,1)} %copy-done.18, bf16[4,512,128]{2,1,0:T(8,128)(2,1)} %copy-done.19, ...), custom_call_target="tpu_custom_call", output_to_operand_aliasing={{0}: (5, {}), {1}: (6, {})} | custom-call | tf_op jit(solution)/shard_map/place/pallas_call | solution.py:406
  169.4 2.5 %collective-permute-done.32.refs_2_ = bf16[4,64,512]{2,1,0:T(8,128)(2,1)} collective-permute-done((bf16[4,64,512]{2,1,0:T(8,128)(2,1)S(1)}, bf16[4,64,512]{2,1,0:T(8,128)(2,1)}, u32[]{:S(2)}, u32[]{:S(2)}) %collective-permute-start.32) | collective-permute-done | bytes 262176 | tf_op jit(solution)/shard_map/ppermute | solution.py:462
  174.0 2.8 %sort.2 = (f32[512,512]{1,0:T(8,128)}, f32[512,512]{1,0:T(8,128)}, f32[512,512]{1,0:T(8,128)}, f32[512,512]{1,0:T(8,128)}) custom-call(s32[8]{0:T(128)} %compare_select_fusion.7.info, bf16[4,64,512]{2,1,0:T(8,128)(2,1)} %copy-done.9, bf16[4,64,512]{2,1,0:T(8,128)(2,1)} %collective-permute-done.31.refs_1_, ...), custom_call_target="tpu_custom_call" | custom-call | tf_op jit(solution)/shard_map/sort/pallas_call | solution.py:436
  179.2 2.8 %sort.3 = (f32[512,512]{1,0:T(8,128)}, f32[512,512]{1,0:T(8,128)}, f32[512,512]{1,0:T(8,128)}, f32[512,512]{1,0:T(8,128)}) custom-call(s32[8]{0:T(128)} %compare_select_fusion.7.info, bf16[4,64,512]{2,1,0:T(8,128)(2,1)} %copy-done.23, bf16[4,64,512]{2,1,0:T(8,128)(2,1)} %copy-done.24, ...), custom_call_target="tpu_custom_call", output_to_operand_aliasing={{0}: (5, {}), {1}: (6, {}), {2}: (7, {}), {3}: (8, {})} | custom-call | tf_op jit(solution)/shard_map/sort/pallas_call | solution.py:436
  (150 shorter events, 38.9 us)
Async XLA Ops:
  1.8 15.8 %collective-permute-start = (bf16[256,512]{1,0:T(8,128)(2,1)S(1)}, bf16[256,512]{1,0:T(8,128)(2,1)S(1)}, u32[]{:S(2)}, u32[]{:S(2)}) collective-permute-start(bf16[256,512]{1,0:T(8,128)(2,1)S(1)} %get-tuple-element.153), channel_id=1, source_target_pairs={{0,2},{1,3},{2,0},{3,1},{4,6},{5,7},{6,4},{7,5},{8,10},{9,11},{10,... | collective-permute-start | bytes 786440 | tf_op jit(solution)/shard_map/ppermute | solution.py:462
  4.8 8.8 %collective-permute-start.1 = (bf16[256,512]{1,0:T(8,128)(2,1)S(1)}, bf16[256,512]{1,0:T(8,128)(2,1)S(1)}, u32[]{:S(2)}, u32[]{:S(2)}) collective-permute-start(bf16[256,512]{1,0:T(8,128)(2,1)S(1)} %get-tuple-element.154.mine.near), channel_id=1, source_target_pairs={{0,1},{1,0},{2,3},{3,2},{4,5},{5,4},{6,7},{7,6},{8,9},{9,8},{10,11... | collective-permute-start | bytes 786440 | tf_op jit(solution)/shard_map/ppermute | solution.py:462
  51.7 6.8 %collective-permute-start.3 = (bf16[16,512,128]{2,1,0:T(8,128)(2,1)}, bf16[16,512,128]{2,1,0:T(8,128)(2,1)}, u32[]{:S(2)}, u32[]{:S(2)}) collective-permute-start(bf16[16,512,128]{2,1,0:T(8,128)(2,1)} %get-tuple-element.173), channel_id=1, source_target_pairs={{0,1},{1,0},{2,3},{3,2},{4,5},{5,4},{6,7},{7,6},{8,9},{9,8},{10,11... | collective-permute-start | bytes 6291464 | tf_op jit(solution)/shard_map/ppermute | solution.py:462
  61.2 32.9 %collective-permute-start.6 = (bf16[4,512,128]{2,1,0:T(8,128)(2,1)}, bf16[4,512,128]{2,1,0:T(8,128)(2,1)S(1)}, u32[]{:S(2)}, u32[]{:S(2)}) collective-permute-start(bf16[4,512,128]{2,1,0:T(8,128)(2,1)} %get-tuple-element.299), channel_id=1, source_target_pairs={{0,4},{1,5},{2,6},{3,7},{4,0},{5,1},{6,2},{7,3},{8,12},{9,13},{10,... | collective-permute-start | bytes 1572872 | tf_op jit(solution)/shard_map/ppermute | solution.py:462
  62.7 31.4 %collective-permute-start.5 = (bf16[4,512,128]{2,1,0:T(8,128)(2,1)S(1)}, bf16[4,512,128]{2,1,0:T(8,128)(2,1)S(1)}, u32[]{:S(2)}, u32[]{:S(2)}) collective-permute-start(bf16[4,512,128]{2,1,0:T(8,128)(2,1)S(1)} %get-tuple-element.300), channel_id=1, source_target_pairs={{0,2},{1,3},{2,0},{3,1},{4,6},{5,7},{6,4},{7,5},{8,10},{9,11},{10,... | collective-permute-start | bytes 1572872 | tf_op jit(solution)/shard_map/ppermute | solution.py:462
  63.2 30.9 %collective-permute-start.4 = (bf16[4,512,128]{2,1,0:T(8,128)(2,1)S(1)}, bf16[4,512,128]{2,1,0:T(8,128)(2,1)S(1)}, u32[]{:S(2)}, u32[]{:S(2)}) collective-permute-start(bf16[4,512,128]{2,1,0:T(8,128)(2,1)S(1)} %get-tuple-element.301), channel_id=1, source_target_pairs={{0,6},{1,7},{2,4},{3,5},{4,2},{5,3},{6,0},{7,1},{8,14},{9,15},{10,... | collective-permute-start | bytes 1572872 | tf_op jit(solution)/shard_map/ppermute | solution.py:462
  95.1 7.6 %collective-permute-start.7 = (bf16[1056,512]{1,0:T(8,128)(2,1)}, bf16[1056,512]{1,0:T(8,128)(2,1)S(1)}, u32[]{:S(2)}, u32[]{:S(2)}) collective-permute-start(bf16[1056,512]{1,0:T(8,128)(2,1)} %get-tuple-element.203), channel_id=1, source_target_pairs={{0,1},{1,0},{2,3},{3,2},{4,5},{5,4},{6,7},{7,6},{8,9},{9,8},{10,11... | collective-permute-start | bytes 3244040 | tf_op jit(solution)/shard_map/ppermute | solution.py:462
  95.1 7.5 %collective-permute-start.8 = (bf16[544,512]{1,0:T(8,128)(2,1)}, bf16[544,512]{1,0:T(8,128)(2,1)S(1)}, u32[]{:S(2)}, u32[]{:S(2)}) collective-permute-start(bf16[544,512]{1,0:T(8,128)(2,1)} %get-tuple-element.204), channel_id=1, source_target_pairs={{0,1},{1,0},{2,3},{3,2},{4,5},{5,4},{6,7},{7,6},{8,9},{9,8},{10,11... | collective-permute-start | bytes 1671176 | tf_op jit(solution)/shard_map/ppermute | solution.py:462
  98.3 7.6 %collective-permute-start.9 = (bf16[512,128]{1,0:T(8,128)(2,1)}, bf16[512,128]{1,0:T(8,128)(2,1)}, u32[]{:S(2)}, u32[]{:S(2)}) collective-permute-start(bf16[512,128]{1,0:T(8,128)(2,1)} %get-tuple-element.214), channel_id=1, source_target_pairs={{0,8},{1,9},{2,10},{3,11},{4,12},{5,13},{6,14},{7,15},{8,0},{9,1},... | collective-permute-start | bytes 393224 | tf_op jit(solution)/shard_map/ppermute | solution.py:462
  99.9 13.2 %collective-permute-start.10 = (bf16[512,128]{1,0:T(8,128)(2,1)}, bf16[512,128]{1,0:T(8,128)(2,1)}, u32[]{:S(2)}, u32[]{:S(2)}) collective-permute-start(bf16[512,128]{1,0:T(8,128)(2,1)} %get-tuple-element.215), channel_id=1, source_target_pairs={{0,16},{1,17},{2,18},{3,19},{4,20},{5,21},{6,22},{7,23},{8,24},{9,... | collective-permute-start | bytes 393224 | tf_op jit(solution)/shard_map/ppermute | solution.py:462
  102.5 10.6 %collective-permute-start.11 = (bf16[512,128]{1,0:T(8,128)(2,1)}, bf16[512,128]{1,0:T(8,128)(2,1)}, u32[]{:S(2)}, u32[]{:S(2)}) collective-permute-start(bf16[512,128]{1,0:T(8,128)(2,1)} %get-tuple-element.216), channel_id=1, source_target_pairs={{0,24},{1,25},{2,26},{3,27},{4,28},{5,29},{6,30},{7,31},{8,16},{9,... | collective-permute-start | bytes 393224 | tf_op jit(solution)/shard_map/ppermute | solution.py:462
  103.9 14.0 %collective-permute-start.12 = (bf16[288,512]{1,0:T(8,128)(2,1)}, bf16[288,512]{1,0:T(8,128)(2,1)S(1)}, u32[]{:S(2)}, u32[]{:S(2)}) collective-permute-start(bf16[288,512]{1,0:T(8,128)(2,1)} %get-tuple-element.224), channel_id=1, source_target_pairs={{0,2},{1,3},{2,0},{3,1},{4,6},{5,7},{6,4},{7,5},{8,10},{9,11},{10,... | collective-permute-start | bytes 884744 | tf_op jit(solution)/shard_map/ppermute | solution.py:462
  104.2 14.5 %collective-permute-start.13 = (bf16[288,512]{1,0:T(8,128)(2,1)}, bf16[288,512]{1,0:T(8,128)(2,1)S(1)}, u32[]{:S(2)}, u32[]{:S(2)}) collective-permute-start(bf16[288,512]{1,0:T(8,128)(2,1)} %get-tuple-element.225), channel_id=1, source_target_pairs={{0,4},{1,5},{2,6},{3,7},{4,0},{5,1},{6,2},{7,3},{8,12},{9,13},{10,... | collective-permute-start | bytes 884744 | tf_op jit(solution)/shard_map/ppermute | solution.py:462
  105.9 13.9 %collective-permute-start.14 = (bf16[288,512]{1,0:T(8,128)(2,1)S(1)}, bf16[288,512]{1,0:T(8,128)(2,1)S(1)}, u32[]{:S(2)}, u32[]{:S(2)}) collective-permute-start(bf16[288,512]{1,0:T(8,128)(2,1)S(1)} %get-tuple-element.226), channel_id=1, source_target_pairs={{0,6},{1,7},{2,4},{3,5},{4,2},{5,3},{6,0},{7,1},{8,14},{9,15},{10,... | collective-permute-start | bytes 884744 | tf_op jit(solution)/shard_map/ppermute | solution.py:462
  114.3 8.3 %collective-permute-start.17 = (bf16[512,128]{1,0:T(8,128)(2,1)S(1)}, bf16[512,128]{1,0:T(8,128)(2,1)S(1)}, u32[]{:S(2)}, u32[]{:S(2)}) collective-permute-start(bf16[512,128]{1,0:T(8,128)(2,1)S(1)} %add_convert_fusion.3), channel_id=1, source_target_pairs={{0,24},{1,25},{2,26},{3,27},{4,28},{5,29},{6,30},{7,31},{8,16},{9,... | collective-permute-start | bytes 393224 | tf_op jit(solution)/shard_map/ppermute | solution.py:462
  116.7 11.0 %collective-permute-start.16 = (bf16[512,128]{1,0:T(8,128)(2,1)S(1)}, bf16[512,128]{1,0:T(8,128)(2,1)S(1)}, u32[]{:S(2)}, u32[]{:S(2)}) collective-permute-start(bf16[512,128]{1,0:T(8,128)(2,1)S(1)} %add_convert_fusion.3), channel_id=1, source_target_pairs={{0,16},{1,17},{2,18},{3,19},{4,20},{5,21},{6,22},{7,23},{8,24},{9,... | collective-permute-start | bytes 393224 | tf_op jit(solution)/shard_map/ppermute | solution.py:462
  117.9 9.8 %collective-permute-start.15 = (bf16[512,128]{1,0:T(8,128)(2,1)S(1)}, bf16[512,128]{1,0:T(8,128)(2,1)S(1)}, u32[]{:S(2)}, u32[]{:S(2)}) collective-permute-start(bf16[512,128]{1,0:T(8,128)(2,1)S(1)} %add_convert_fusion.3), channel_id=1, source_target_pairs={{0,8},{1,9},{2,10},{3,11},{4,12},{5,13},{6,14},{7,15},{8,0},{9,1},... | collective-permute-start | bytes 393224 | tf_op jit(solution)/shard_map/ppermute | solution.py:462
  127.7 6.5 %collective-permute-start.18 = (bf16[96,512]{1,0:T(8,128)(2,1)S(1)}, bf16[96,512]{1,0:T(8,128)(2,1)S(1)}, u32[]{:S(2)}, u32[]{:S(2)}) collective-permute-start(bf16[96,512]{1,0:T(8,128)(2,1)S(1)} %get-tuple-element.238), channel_id=1, source_target_pairs={{0,8},{1,9},{2,10},{3,11},{4,12},{5,13},{6,14},{7,15},{8,0},{9,1},... | collective-permute-start | bytes 294920 | tf_op jit(solution)/shard_map/ppermute | solution.py:462
  127.7 10.3 %collective-permute-start.19 = (bf16[96,512]{1,0:T(8,128)(2,1)S(1)}, bf16[96,512]{1,0:T(8,128)(2,1)S(1)}, u32[]{:S(2)}, u32[]{:S(2)}) collective-permute-start(bf16[96,512]{1,0:T(8,128)(2,1)S(1)} %get-tuple-element.239), channel_id=1, source_target_pairs={{0,16},{1,17},{2,18},{3,19},{4,20},{5,21},{6,22},{7,23},{8,24},{9,... | collective-permute-start | bytes 294920 | tf_op jit(solution)/shard_map/ppermute | solution.py:462
  130.7 7.3 %collective-permute-start.20 = (bf16[96,512]{1,0:T(8,128)(2,1)S(1)}, bf16[96,512]{1,0:T(8,128)(2,1)S(1)}, u32[]{:S(2)}, u32[]{:S(2)}) collective-permute-start(bf16[96,512]{1,0:T(8,128)(2,1)S(1)} %get-tuple-element.240), channel_id=1, source_target_pairs={{0,24},{1,25},{2,26},{3,27},{4,28},{5,29},{6,30},{7,31},{8,16},{9,... | collective-permute-start | bytes 294920 | tf_op jit(solution)/shard_map/ppermute | solution.py:462
  132.2 17.4 %collective-permute-start.26 = (bf16[4,512,128]{2,1,0:T(8,128)(2,1)S(1)}, bf16[4,512,128]{2,1,0:T(8,128)(2,1)S(1)}, u32[]{:S(2)}, u32[]{:S(2)}) collective-permute-start(bf16[4,512,128]{2,1,0:T(8,128)(2,1)S(1)} %pad_maximum_fusion.refs_0_), channel_id=1, source_target_pairs={{0,6},{1,7},{2,4},{3,5},{4,2},{5,3},{6,0},{7,1},{8,14},{9,15},{10,... | collective-permute-start | bytes 1572872 | tf_op jit(solution)/shard_map/ppermute | solution.py:462
  133.7 22.0 %collective-permute-start.25 = (bf16[4,512,128]{2,1,0:T(8,128)(2,1)S(1)}, bf16[4,512,128]{2,1,0:T(8,128)(2,1)S(1)}, u32[]{:S(2)}, u32[]{:S(2)}) collective-permute-start(bf16[4,512,128]{2,1,0:T(8,128)(2,1)S(1)} %pad_maximum_fusion.refs_0_), channel_id=1, source_target_pairs={{0,4},{1,5},{2,6},{3,7},{4,0},{5,1},{6,2},{7,3},{8,12},{9,13},{10,... | collective-permute-start | bytes 1572872 | tf_op jit(solution)/shard_map/ppermute | solution.py:462
  134.2 21.5 %collective-permute-start.24 = (bf16[4,512,128]{2,1,0:T(8,128)(2,1)S(1)}, bf16[4,512,128]{2,1,0:T(8,128)(2,1)S(1)}, u32[]{:S(2)}, u32[]{:S(2)}) collective-permute-start(bf16[4,512,128]{2,1,0:T(8,128)(2,1)S(1)} %pad_maximum_fusion.refs_0_), channel_id=1, source_target_pairs={{0,2},{1,3},{2,0},{3,1},{4,6},{5,7},{6,4},{7,5},{8,10},{9,11},{10,... | collective-permute-start | bytes 1572872 | tf_op jit(solution)/shard_map/ppermute | solution.py:462
  139.0 6.2 %collective-permute-start.23 = (bf16[64,512]{1,0:T(8,128)(2,1)S(1)}, bf16[64,512]{1,0:T(8,128)(2,1)S(1)}, u32[]{:S(2)}, u32[]{:S(2)}) collective-permute-start(bf16[64,512]{1,0:T(8,128)(2,1)S(1)} %add_convert_fusion.4), channel_id=1, source_target_pairs={{0,24},{1,25},{2,26},{3,27},{4,28},{5,29},{6,30},{7,31},{8,16},{9,... | collective-permute-start | bytes 196616 | tf_op jit(solution)/shard_map/ppermute | solution.py:462
  141.5 5.7 %collective-permute-start.22 = (bf16[64,512]{1,0:T(8,128)(2,1)S(1)}, bf16[64,512]{1,0:T(8,128)(2,1)S(1)}, u32[]{:S(2)}, u32[]{:S(2)}) collective-permute-start(bf16[64,512]{1,0:T(8,128)(2,1)S(1)} %add_convert_fusion.4), channel_id=1, source_target_pairs={{0,16},{1,17},{2,18},{3,19},{4,20},{5,21},{6,22},{7,23},{8,24},{9,... | collective-permute-start | bytes 196616 | tf_op jit(solution)/shard_map/ppermute | solution.py:462
  147.2 22.2 %collective-permute-start.34 = (bf16[288,512]{1,0:T(8,128)(2,1)}, bf16[288,512]{1,0:T(8,128)(2,1)S(1)}, u32[]{:S(2)}, u32[]{:S(2)}) collective-permute-start(bf16[288,512]{1,0:T(8,128)(2,1)} %get-tuple-element.269), channel_id=1, source_target_pairs={{0,2},{1,3},{2,0},{3,1},{4,6},{5,7},{6,4},{7,5},{8,10},{9,11},{10,... | collective-permute-start | bytes 884744 | tf_op jit(solution)/shard_map/ppermute | solution.py:462
  149.5 7.0 %collective-permute-start.27 = (bf16[4,512,128]{2,1,0:T(8,128)(2,1)S(1)}, bf16[4,512,128]{2,1,0:T(8,128)(2,1)S(1)}, u32[]{:S(2)}, u32[]{:S(2)}) collective-permute-start(bf16[4,512,128]{2,1,0:T(8,128)(2,1)S(1)} %pad_maximum_fusion.refs_0_), channel_id=1, source_target_pairs={{0,1},{1,0},{2,3},{3,2},{4,5},{5,4},{6,7},{7,6},{8,9},{9,8},{10,11... | collective-permute-start | bytes 1572872 | tf_op jit(solution)/shard_map/ppermute | solution.py:462
  156.3 9.2 %collective-permute-start.30 = (bf16[4,512,128]{2,1,0:T(8,128)(2,1)S(1)}, bf16[4,512,128]{2,1,0:T(8,128)(2,1)}, u32[]{:S(2)}, u32[]{:S(2)}) collective-permute-start(bf16[4,512,128]{2,1,0:T(8,128)(2,1)S(1)} %collective-permute-done.26.refs_3_), channel_id=1, source_target_pairs={{0,1},{1,0},{2,3},{3,2},{4,5},{5,4},{6,7},{7,6},{8,9},{9,8},{10,11... | collective-permute-start | bytes 1572872 | tf_op jit(solution)/shard_map/ppermute | solution.py:462
  156.5 12.9 %collective-permute-start.33 = (bf16[4,64,512]{2,1,0:T(8,128)(2,1)S(1)}, bf16[4,64,512]{2,1,0:T(8,128)(2,1)}, u32[]{:S(2)}, u32[]{:S(2)}) collective-permute-start(bf16[4,64,512]{2,1,0:T(8,128)(2,1)S(1)} %pad_maximum_fusion.7.refs_0_), channel_id=1, source_target_pairs={{0,6},{1,7},{2,4},{3,5},{4,2},{5,3},{6,0},{7,1},{8,14},{9,15},{10,... | collective-permute-start | bytes 786440 | tf_op jit(solution)/shard_map/ppermute | solution.py:462
  158.1 13.8 %collective-permute-start.32 = (bf16[4,64,512]{2,1,0:T(8,128)(2,1)S(1)}, bf16[4,64,512]{2,1,0:T(8,128)(2,1)}, u32[]{:S(2)}, u32[]{:S(2)}) collective-permute-start(bf16[4,64,512]{2,1,0:T(8,128)(2,1)S(1)} %pad_maximum_fusion.7.refs_0_), channel_id=1, source_target_pairs={{0,4},{1,5},{2,6},{3,7},{4,0},{5,1},{6,2},{7,3},{8,12},{9,13},{10,... | collective-permute-start | bytes 786440 | tf_op jit(solution)/shard_map/ppermute | solution.py:462
  159.5 13.9 %collective-permute-start.31 = (bf16[4,64,512]{2,1,0:T(8,128)(2,1)S(1)}, bf16[4,64,512]{2,1,0:T(8,128)(2,1)}, u32[]{:S(2)}, u32[]{:S(2)}) collective-permute-start(bf16[4,64,512]{2,1,0:T(8,128)(2,1)S(1)} %pad_maximum_fusion.7.refs_0_), channel_id=1, source_target_pairs={{0,2},{1,3},{2,0},{3,1},{4,6},{5,7},{6,4},{7,5},{8,10},{9,11},{10,... | collective-permute-start | bytes 786440 | tf_op jit(solution)/shard_map/ppermute | solution.py:462
  165.6 12.7 %collective-permute-start.35 = (bf16[4,64,512]{2,1,0:T(8,128)(2,1)S(1)}, bf16[4,64,512]{2,1,0:T(8,128)(2,1)S(1)}, u32[]{:S(2)}, u32[]{:S(2)}) collective-permute-start(bf16[4,64,512]{2,1,0:T(8,128)(2,1)S(1)} %pad_maximum_fusion.7.refs_0_), channel_id=1, source_target_pairs={{0,1},{1,0},{2,3},{3,2},{4,5},{5,4},{6,7},{7,6},{8,9},{9,8},{10,11... | collective-permute-start | bytes 786440 | tf_op jit(solution)/shard_map/ppermute | solution.py:462
  (37 other events, 257.4 us)
